TPU v7x, 256 devices: a whole 4x4x8 slice. The times are simulated.
256 devices in a mesh: grp: 64 (over z, y, core), head: 4 (over x).
Axes of the slice: x: 4, y: 4, z: 8, core: 2. Of those that a mesh axis runs over, the one named last changes fastest.
Arguments:
- arriving_hiddens: bfloat16 [512, 4, 2048], P('grp', None, 'head'), may hold values from -6 to 6
- occupied_slot_totals: int32 [512], P('grp'), may hold values from 1 to 4
- former_indices: int32 [512], P('grp'), may hold values from 0 to 511, as said below
- reconstruct_marks: int32 [512], P('grp'), may hold values from 0 to 1, as said below
- retained_hiddens: bfloat16 [512, 32, 2048], P('grp', None, 'head'), may hold values from -6 to 6
- carried_memory_matrices: float32 [512, 16, 64, 64], P('grp', 'head'), may hold values from -12 to 12
- lagged_previous_entries: float32 [512, 2, 2048], P('grp', None, 'head'), may hold values from -6 to 6
- pre_attention_scaling: float32 [2048], replicated, may hold values from 0.5 to 1.5
- pre_feedforward_scaling: float32 [2048], replicated, may hold values from 0.5 to 1.5
- lag_blend_fractions: float32 [5, 2048], replicated, may hold values from 0 to 1
- acceptance_projection: bfloat16 [2048, 1024], P(None, 'head'), may hold values from -0.125 to 0.125
- address_projection: bfloat16 [2048, 1024], P(None, 'head'), may hold values from -0.125 to 0.125
- content_projection: bfloat16 [2048, 1024], P(None, 'head'), may hold values from -0.125 to 0.125
- fading_lowrank_left: bfloat16 [2048, 64], replicated, may hold values from -0.125 to 0.125
- fading_lowrank_right: bfloat16 [64, 1024], P(None, 'head'), may hold values from -0.75 to 0.75
- fading_baseline_entries: float32 [1024], P('head'), may hold values from -6 to 1
- present_item_reward: float32 [1024], P('head'), may hold values from -6 to 6
- grouped_layer_scaling: float32 [1024], P('head'), may hold values from 0.5 to 1.5
- attention_exit_projection: bfloat16 [1024, 2048], P('head'), may hold values from -0.1875 to 0.1875
- feedforward_address_proj: bfloat16 [2048, 3584], P(None, 'head'), may hold values from -0.125 to 0.125
- feedforward_content_proj: bfloat16 [3584, 2048], P('head'), may hold values from -0.09375 to 0.09375
Outputs:
- next_tokens: bfloat16 [512, 4, 2048], P('grp', None, 'head')
- next_state: float32 [512, 16, 64, 64], P('grp', 'head')
- next_shift: float32 [512, 2, 2048], P('grp', None, 'head')
Inputs may be any that keep to these rules, and one draw needn't show every extreme that they name: former_indices[g * 8 + j] = ((g + offset_j) mod 64) * 8 + local_j, where the 8 offsets offset_j are distinct numbers of 0 to 63 and local_j is a permutation of 0 to 7, both the same for every group g. `reconstruct_marks`: among the 8 requests of one group at most 2 are marked, and some group has exactly 2.
All inputs are finite; a program needn't handle non-finite values.
Results may differ from a plain program's by a relative error of at most 0.028.
Values may be sent and summed in bfloat16 or wider, within the bound.
No kernel may reach another device: no remote copies, remote signals or barrier semaphores. Data moves between devices by JAX's collectives and lax.ppermute only.
A program may use at most 128 MiB of HBM per device.

v0:
```python
import jax
import jax.numpy as jnp
from jax import lax
from jax.sharding import PartitionSpec as P

ATTENTION_WIDTH = 64
REB = 2


EPSILON = 1e-05


def shifted_2(value, axis, steps):
    count = lax.axis_size(axis)
    pairs = [(source, (source + steps) % count) for source in range(count)]
    return lax.ppermute(value, axis, pairs)


def layer_norm(inputs, gain):
    centered = inputs - jnp.mean(inputs, axis=-1, keepdims=True)
    spread = jnp.mean(centered * centered, axis=-1, keepdims=True)
    return (centered * lax.rsqrt(spread + EPSILON) * gain).astype(jnp.bfloat16)


def blend_rows(current, previous, rate):
    return (current + (previous - current) * rate).astype(jnp.bfloat16)


def project(inputs, weight):
    flat_rows = inputs.reshape(-1, inputs.shape[-1])
    result = jnp.dot(flat_rows, weight, preferred_element_type=jnp.float32)
    return result.reshape(inputs.shape[:-1] + (weight.shape[1],))


def divide_into_groups(inputs):
    return inputs.reshape(inputs.shape[:-1] + (-1, ATTENTION_WIDTH))


def key_value_decay(
    current,
    previous,
    lag_blend_fractions,
    address_projection,
    content_projection,
    fading_lowrank_left,
    fading_lowrank_right,
    fading_baseline_entries,
):
    key_rows = project(blend_rows(current, previous, lag_blend_fractions[1]), address_projection)
    values = project(blend_rows(current, previous, lag_blend_fractions[2]), content_projection)
    lowrank = jnp.tanh(
        project(blend_rows(current, previous, lag_blend_fractions[3]), fading_lowrank_left)
    ).astype(jnp.bfloat16)
    decay_rates = jnp.exp(
        -jnp.exp(fading_baseline_entries + project(lowrank, fading_lowrank_right))
    )
    return (
        divide_into_groups(key_rows),
        divide_into_groups(values),
        divide_into_groups(decay_rates),
    )


def advance(present_outer_product, inputs):
    key_step, value_step, decay_step = inputs
    return (
        decay_step[..., :, None] * present_outer_product
        + key_step[..., :, None] * value_step[..., None, :],
        None,
    )


def rebuild(
    retained_hiddens,
    pre_attention_scaling,
    lag_blend_fractions,
    address_projection,
    content_projection,
    fading_lowrank_left,
    fading_lowrank_right,
    fading_baseline_entries,
):
    standardized_entry = layer_norm(retained_hiddens.astype(jnp.float32), pre_attention_scaling)
    current = standardized_entry.astype(jnp.float32)
    previous = jnp.concatenate([jnp.zeros_like(current[:, :1]), current[:, :-1]], axis=1)
    key_rows, values, decay_rates = key_value_decay(
        current,
        previous,
        lag_blend_fractions,
        address_projection,
        content_projection,
        fading_lowrank_left,
        fading_lowrank_right,
        fading_baseline_entries,
    )
    start_state = jnp.zeros(
        key_rows.shape[:1] + key_rows.shape[2:] + (ATTENTION_WIDTH,), jnp.float32
    )
    final_state, _ = lax.scan(
        advance,
        start_state,
        (jnp.moveaxis(key_rows, 1, 0), jnp.moveaxis(values, 1, 0), jnp.moveaxis(decay_rates, 1, 0)),
    )
    return (final_state, current[:, -1])


def attention_result(
    standardized_entry,
    lagged_entry,
    present_outer_product,
    occupied_slot_totals,
    lag_blend_fractions,
    acceptance_projection,
    address_projection,
    content_projection,
    fading_lowrank_left,
    fading_lowrank_right,
    fading_baseline_entries,
    present_item_reward,
    grouped_layer_scaling,
):
    current = standardized_entry.astype(jnp.float32)
    previous = jnp.concatenate([lagged_entry[:, None], current[:, :-1]], axis=1)
    acceptance_gate_entries = divide_into_groups(
        project(blend_rows(current, previous, lag_blend_fractions[0]), acceptance_projection)
    )
    key_rows, values, decay_rates = key_value_decay(
        current,
        previous,
        lag_blend_fractions,
        address_projection,
        content_projection,
        fading_lowrank_left,
        fading_lowrank_right,
        fading_baseline_entries,
    )
    reward_grouped = divide_into_groups(present_item_reward)
    decoding_results = []
    for query_slot_index in range(current.shape[1]):
        address_content_product = (
            key_rows[:, query_slot_index, :, :, None] * values[:, query_slot_index, :, None, :]
        )
        decoding_results.append(
            jnp.einsum(
                "ghl,ghlm->ghm",
                acceptance_gate_entries[:, query_slot_index],
                present_outer_product + reward_grouped[:, :, None] * address_content_product,
                precision=lax.Precision.HIGHEST,
            )
        )
        valid_rows = (query_slot_index < occupied_slot_totals)[:, None, None, None]
        present_outer_product = jnp.where(
            valid_rows,
            decay_rates[:, query_slot_index, :, :, None] * present_outer_product
            + address_content_product,
            present_outer_product,
        )
    mixed_heads = jnp.stack(decoding_results, axis=1)
    centered = mixed_heads - jnp.mean(mixed_heads, axis=-1, keepdims=True)
    spread = jnp.mean(centered * centered, axis=-1, keepdims=True)
    grouped_results = (
        centered * lax.rsqrt(spread + EPSILON) * divide_into_groups(grouped_layer_scaling)
    ).astype(jnp.bfloat16)
    return (grouped_results.reshape(grouped_results.shape[:2] + (-1,)), present_outer_product)


def last_live(inputs, occupied_slot_totals):
    pick_table = (
        jnp.arange(inputs.shape[1])[None, :, None] == (occupied_slot_totals - 1)[:, None, None]
    )
    return jnp.sum(jnp.where(pick_table, inputs, jnp.zeros_like(inputs)), axis=1)


def on_device(
    arriving_hiddens,
    occupied_slot_totals,
    former_indices,
    reconstruct_marks,
    retained_hiddens,
    carried_memory_matrices,
    lagged_previous_entries,
    pre_attention_scaling,
    pre_feedforward_scaling,
    lag_blend_fractions,
    acceptance_projection,
    address_projection,
    content_projection,
    fading_lowrank_left,
    fading_lowrank_right,
    fading_baseline_entries,
    present_item_reward,
    grouped_layer_scaling,
    attention_exit_projection,
    feedforward_address_proj,
    feedforward_content_proj,
):
    req_rows = arriving_hiddens.shape[0]
    local_heads = carried_memory_matrices.shape[1]
    model_width = pre_attention_scaling.shape[0]
    grp_index = lax.axis_index("grp")
    groups = lax.axis_size("grp")
    head_index = lax.axis_index("head")
    feature_part = model_width // lax.axis_size("head")
    offset = (former_indices // req_rows - grp_index) % groups
    source_row = former_indices % req_rows
    state_size = local_heads * ATTENTION_WIDTH * ATTENTION_WIDTH
    packed = jnp.concatenate(
        [
            carried_memory_matrices.reshape(req_rows, -1),
            lagged_previous_entries.reshape(req_rows, -1),
        ],
        axis=1,
    )
    ready_rows = jnp.take(packed, source_row, axis=0)
    moved_rows = ready_rows
    for bit_index in range((groups - 1).bit_length()):
        shifted = shifted_2(moved_rows, "grp", -(1 << bit_index))
        moved_rows = jnp.where((offset >> bit_index & 1 == 1)[:, None], shifted, moved_rows)
    present_outer_product = moved_rows[:, :state_size].reshape(
        req_rows, local_heads, ATTENTION_WIDTH, ATTENTION_WIDTH
    )
    shift_part = moved_rows[:, state_size:].reshape(req_rows, 2, feature_part)
    mark_rank = jnp.cumsum(reconstruct_marks) - reconstruct_marks
    slot_table = (
        (reconstruct_marks[None, :] == 1) & (mark_rank[None, :] == jnp.arange(REB)[:, None])
    ).astype(jnp.bfloat16)
    chosen = jnp.einsum(
        "sn,ntd->std", slot_table, retained_hiddens, preferred_element_type=jnp.float32
    ).astype(jnp.bfloat16)
    full_tokens, full_chosen = (
        lax.all_gather(arriving_hiddens, "head", axis=2, tiled=True),
        lax.all_gather(chosen, "head", axis=2, tiled=True),
    )
    full_shift = lax.all_gather(shift_part.astype(jnp.bfloat16), "head", axis=2, tiled=True).astype(
        shift_part.dtype
    )
    rebuilt, last_hist = rebuild(
        full_chosen,
        pre_attention_scaling,
        lag_blend_fractions,
        address_projection,
        content_projection,
        fading_lowrank_left,
        fading_lowrank_right,
        fading_baseline_entries,
    )
    pick_slot = jnp.clip(mark_rank, 0, REB - 1)
    marked = reconstruct_marks == 1
    present_outer_product = jnp.where(
        marked[:, None, None, None], jnp.take(rebuilt, pick_slot, axis=0), present_outer_product
    )
    lagged_entry = jnp.where(
        marked[:, None], jnp.take(last_hist, pick_slot, axis=0), full_shift[:, 0]
    )
    standardized_entry = layer_norm(full_tokens.astype(jnp.float32), pre_attention_scaling)
    grouped_results, present_outer_product = attention_result(
        standardized_entry,
        lagged_entry,
        present_outer_product,
        occupied_slot_totals,
        lag_blend_fractions,
        acceptance_projection,
        address_projection,
        content_projection,
        fading_lowrank_left,
        fading_lowrank_right,
        fading_baseline_entries,
        present_item_reward,
        grouped_layer_scaling,
    )
    flat_heads = grouped_results.reshape(-1, grouped_results.shape[-1])
    mix_total = lax.psum(
        jnp.dot(flat_heads, attention_exit_projection, preferred_element_type=jnp.float32).astype(
            jnp.bfloat16
        ),
        "head",
    ).astype(jnp.float32)
    middle = (full_tokens.astype(jnp.float32) + mix_total.reshape(full_tokens.shape)).astype(
        jnp.bfloat16
    )
    middle_local = lax.dynamic_slice_in_dim(middle, head_index * feature_part, feature_part, 2)
    second = layer_norm(middle.astype(jnp.float32), pre_feedforward_scaling)
    current = second.astype(jnp.float32)
    previous = jnp.concatenate([full_shift[:, 1][:, None], current[:, :-1]], axis=1)
    hidden = jnp.square(
        jax.nn.relu(
            project(blend_rows(current, previous, lag_blend_fractions[4]), feedforward_address_proj)
        )
    ).astype(jnp.bfloat16)
    flat_hidden = hidden.reshape(-1, hidden.shape[-1])
    ffn_rows = lax.psum_scatter(
        lax.dot_general(
            feedforward_content_proj,
            flat_hidden,
            (((0,), (1,)), ((), ())),
            preferred_element_type=jnp.float32,
        ).astype(jnp.bfloat16),
        "head",
        scatter_dimension=0,
        tiled=True,
    ).astype(jnp.float32)
    result = (middle_local.astype(jnp.float32) + ffn_rows.T.reshape(middle_local.shape)).astype(
        jnp.bfloat16
    )
    valid_rows = jnp.arange(arriving_hiddens.shape[1])[None, :] < occupied_slot_totals[:, None]
    result = jnp.where(valid_rows[..., None], result, jnp.zeros_like(result))
    time_last = lax.dynamic_slice_in_dim(
        last_live(standardized_entry.astype(jnp.float32), occupied_slot_totals),
        head_index * feature_part,
        feature_part,
        1,
    )
    channel_last = lax.dynamic_slice_in_dim(
        last_live(current, occupied_slot_totals), head_index * feature_part, feature_part, 1
    )
    return (result, present_outer_product, jnp.stack([time_last, channel_last], axis=1))


def solution(mesh):
    placed = (
        P("grp", None, "head"),
        P("grp"),
        P("grp"),
        P("grp"),
        P("grp", None, "head"),
        P("grp", "head", None, None),
        P("grp", None, "head"),
        P(),
        P(),
        P(),
        P(None, "head"),
        P(None, "head"),
        P(None, "head"),
        P(),
        P(None, "head"),
        P("head"),
        P("head"),
        P("head"),
        P("head", None),
        P(None, "head"),
        P("head", None),
    )
    return jax.shard_map(
        on_device,
        mesh=mesh,
        in_specs=placed,
        out_specs=(P("grp", None, "head"), P("grp", "head", None, None), P("grp", None, "head")),
        check_vma=False,
    )
```

profile of v0, /device:TPU:2, one launch (start us, length us, event | category | flops | bytes accessed | tf_op | source)
XLA Modules:
  0.0 304.2 jit_solution(17810951148594460560)
XLA Ops:
  7.2 1.4 and_compare_fusion.5
  9.4 1.6 reshape.289
  11.8 0.9 broadcast_select_fusion
  12.7 7.7 %collective-permute-start = (f32[8,17408]{1,0:T(8,128)}, f32[8,17408]{1,0:T(8,128)S(1)}, u32[]{:S(2)}, u32[]{:S(2)}) collective-permute-start(f32[8,17408]{1,0:T(8,128)} %broadcast_select_fusion), channel_id=1, source_target_pairs={{0,252},{4,0},{8,4},{12,8},{16,12},{20,16},{24,20},{28,24},{32,28}... | collective-permute-start | bytes 1671176 | tf_op jit(solution)/shard_map/ppermute | solution.py:16
  22.7 12.3 %all_gather.10 = bf16[2,32,2048]{2,1,0:T(8,128)(2,1)S(1)} all-gather(bf16[2,32,512]{2,1,0:T(8,128)(2,1)S(1)} %copy.145), channel_id=1, replica_groups=mesh['grp'=64,'head'=4] {'head'}, dimensions={2}, use_global_device_ids=true | all-gather | bytes 327680 | tf_op jit(solution)/shard_map/all_gather | solution.py:232
  35.6 0.9 copy-done.6
  36.4 1.2 broadcast_select_fusion.1
  37.6 1.1 collective-permute-start.1
  38.7 1.4 fusion.15
  40.4 2.3 copy.80
  42.6 1.5 copy.81
  44.1 2.4 convolution_bitcast_fusion.1
  46.6 2.4 convolution_bitcast_fusion
  48.9 1.4 broadcast_select_fusion.2
  50.3 1.8 collective-permute-start.2
  52.1 34.7 %while.11 = (s32[]{:T(128)}, f32[2,4,64,64]{3,2,1,0:T(8,128)S(1)}, f32[32,2,4,64]{3,2,1,0:T(4,128)S(1)}, f32[32,2,4,64]{3,0,2,1:T(8,128)S(1)}, f32[32,2,4,64]{3,0,2,1:T(8,128)}, /*index=5*/s32[]{:T(128)}, s32[]{:T(128)}) while((s32[]{:T(128)}, f32[2,4,64,64]{3,2,1,0:T(8,128)S(1)}, f32[32,2,4,64]{3,2,1,0:T(4,128)S(1)}, ...), condition=%wide.region_6.7_spmd.clone, body=%wide.region_5.6_spmd.clone.sunk | while | flops 131075 | bytes 280679 | solution.py:99
  53.2 0.8 constant_dynamic-slice_fusion.3
  54.3 0.8 constant_dynamic-slice_fusion.3
  55.4 0.8 constant_dynamic-slice_fusion.3
  56.5 0.8 constant_dynamic-slice_fusion.3
  57.6 0.8 constant_dynamic-slice_fusion.3
  58.7 0.8 constant_dynamic-slice_fusion.3
  59.7 0.8 constant_dynamic-slice_fusion.3
  60.8 0.8 constant_dynamic-slice_fusion.3
  61.9 0.8 constant_dynamic-slice_fusion.3
  63.0 0.8 constant_dynamic-slice_fusion.3
  64.1 0.8 constant_dynamic-slice_fusion.3
  65.2 0.8 constant_dynamic-slice_fusion.3
  66.3 0.8 constant_dynamic-slice_fusion.3
  67.3 0.8 constant_dynamic-slice_fusion.3
  68.4 0.8 constant_dynamic-slice_fusion.3
  69.5 0.8 constant_dynamic-slice_fusion.3
  70.6 0.8 constant_dynamic-slice_fusion.3
  71.7 0.8 constant_dynamic-slice_fusion.3
  72.8 0.8 constant_dynamic-slice_fusion.3
  74.9 0.8 constant_dynamic-slice_fusion.3
  84.7 0.8 constant_dynamic-slice_fusion.3
  86.9 0.9 slice.126
  87.8 1.4 mul.345
  89.2 2.3 copy.77
  91.5 12.2 %all_gather.9 = bf16[8,4,2048]{2,1,0:T(4,128)(2,1)S(1)} all-gather(bf16[8,4,512]{2,1,0:T(4,128)(2,1)S(1)} %copy-done.16), channel_id=1, replica_groups=mesh['grp'=64,'head'=4] {'head'}, dimensions={2}, use_global_device_ids=true | all-gather | bytes 163840 | tf_op jit(solution)/shard_map/all_gather | solution.py:231
  103.6 1.2 broadcast_select_fusion.3
  104.8 1.1 collective-permute-start.3
  106.6 17.3 %collective-permute-done.3 = f32[8,17408]{1,0:T(8,128)S(1)} collective-permute-done((f32[8,17408]{1,0:T(8,128)S(1)}, f32[8,17408]{1,0:T(8,128)S(1)}, u32[]{:S(2)}, u32[]{:S(2)}) %collective-permute-start.3) | collective-permute-done | bytes 557088 | tf_op jit(solution)/shard_map/ppermute | solution.py:16
  125.2 35.1 %collective-permute-done.4 = f32[8,17408]{1,0:T(8,128)S(1)} collective-permute-done((f32[8,17408]{1,0:T(8,128)S(1)}, f32[8,17408]{1,0:T(8,128)S(1)}, u32[]{:S(2)}, u32[]{:S(2)}) %collective-permute-start.4) | collective-permute-done | bytes 557088 | tf_op jit(solution)/shard_map/ppermute | solution.py:16
  161.9 18.2 %collective-permute-done.5 = f32[8,17408]{1,0:T(8,128)} collective-permute-done((f32[8,17408]{1,0:T(8,128)S(1)}, f32[8,17408]{1,0:T(8,128)}, u32[]{:S(2)}, u32[]{:S(2)}) %collective-permute-start.5) | collective-permute-done | bytes 557088 | tf_op jit(solution)/shard_map/ppermute | solution.py:16
  180.1 1.2 broadcast_select_fusion.6
  181.3 0.8 slice.132
  182.1 12.0 %all_gather.11 = bf16[8,2,2048]{2,0,1:T(8,128)(2,1)S(1)} all-gather(bf16[8,2,512]{2,0,1:T(8,128)(2,1)S(1)} %bitcast.193), channel_id=1, replica_groups=mesh['grp'=64,'head'=4] {'head'}, dimensions={2}, use_global_device_ids=true | all-gather | bytes 81920 | tf_op jit(solution)/shard_map/all_gather | solution.py:234
  196.3 1.1 fusion.99
  197.4 1.5 reshape.292
  198.9 1.9 fusion.105
  200.9 1.9 fusion.103
  202.9 1.8 fusion.101
  204.8 4.1 %fusion.36 = (f32[8,4,64,64]{3,2,1,0:T(8,128)}, f32[8,4,64,64]{3,2,1,0:T(8,128)S(1)}) fusion(f32[8,4,64]{2,1,0:T(4,128)S(1)} %copy-done.13, f32[8,4,64]{2,1,0:T(4,128)S(1)} %copy.94, f32[8,4,64]{2,1,0:T(4,128)S(1)} %copy.93, f32[8,4,64]{2,1,0:T(4,128)S(1)} %copy-done.12, f32[8,4,64]{2,1,0:T(4,128)S(1)} %copy.92, f32[8,4,64]{2,1,0:T(4,128)S(1)} %copy.91, ...), kind=kLoop, calls=%fused_computation.49 | loop fusion | flops 2359296 | bytes 2195504 | tf_op jit(solution)/shard_map/jit(_where)/select_n | solution.py:152
  208.9 2.8 fusion.34
  211.7 2.3 fusion.30
  214.0 1.7 fusion.26
  215.8 1.2 fusion.22
  219.0 45.6 %all-reduce.3.cloned.1.call-done = bf16[8,4,2048]{2,1,0:T(4,128)(2,1)} async-done(((bf16[8,4,2048]{2,1,0:T(4,128)(2,1)}), bf16[8,4,2048]{2,1,0:T(4,128)(2,1)}) %all-reduce.3.cloned.1.call-update) | async-done | bytes 131088 | tf_op jit(solution)/shard_map/psum | solution.py:272
  264.6 1.1 convert_reduce_fusion.2
  266.8 2.7 fusion.10
  269.5 3.4 %fusion.3 = bf16[2048,32]{0,1:T(8,128)(2,1)} fusion(bf16[32,896]{1,0:T(8,128)(2,1)S(1)} %reshape.296, bf16[896,2048]{1,0:T(8,128)(2,1)} %param.43), kind=kOutput, calls=%fused_computation.12 | convolution fusion | flops 117506048 | bytes 3858432 | tf_op jit(solution)/shard_map/dot_general | solution.py:292
  273.7 22.2 %reduce-scatter.2.cloned.1.call-done = bf16[512,32]{0,1:T(8,128)(2,1)} async-done(((bf16[2048,32]{0,1:T(8,128)(2,1)}), bf16[512,32]{0,1:T(8,128)(2,1)}) %reduce-scatter.2.cloned.1.call-update) | async-done | bytes 32784 | tf_op jit(solution)/shard_map/reduce_scatter | solution.py:291
  (234 shorter events, 33.1 us)
Async XLA Ops:
  7.2 210.4 %copy-start = (bf16[256,2048]{1,0:T(8,128)(2,1)S(1)}, bf16[256,2048]{1,0:T(8,128)(2,1)}, u32[]{:S(2)}) copy-start(bf16[256,2048]{1,0:T(8,128)(2,1)} %param.41) | copy-start | bytes 3145732
  7.2 257.4 %all-reduce.3.cloned.1.call-start = ((), (), s32[]{:S(2)}) async-start(), calls=%async_computation.1 | async-start | bytes 262144 | tf_op jit(solution)/shard_map/psum | solution.py:272
  10.9 9.5 %copy-start.34 = (s32[8]{0:T(128)S(1)}, s32[8]{0:T(128)}, u32[]{:S(2)}) copy-start(s32[8]{0:T(128)} %param.26) | copy-start | bytes 100
  10.9 10.8 %copy-start.18 = (f32[5,2048]{1,0:T(8,128)S(1)}, f32[5,2048]{1,0:T(8,128)}, u32[]{:S(2)}) copy-start(f32[5,2048]{1,0:T(8,128)} %param.32) | copy-start | bytes 122884
  11.0 11.5 %copy-start.8 = (bf16[8,32,512]{2,1,0:T(8,128)(2,1)S(1)}, bf16[8,32,512]{2,1,0:T(8,128)(2,1)}, u32[]{:S(2)}) copy-start(bf16[8,32,512]{2,1,0:T(8,128)(2,1)} %param.27) | copy-start | bytes 786436
  11.0 24.4 %copy-start.9 = (f32[2048]{0:T(1024)S(1)}, f32[2048]{0:T(1024)}, u32[]{:S(2)}) copy-start(f32[2048]{0:T(1024)} %param.30) | copy-start | bytes 24580
  11.8 27.0 %copy-start.17 = (bf16[64,256]{1,0:T(8,128)(2,1)S(1)}, bf16[64,256]{1,0:T(8,128)(2,1)}, u32[]{:S(2)}) copy-start(bf16[64,256]{1,0:T(8,128)(2,1)} %param.37) | copy-start | bytes 98308
  11.8 26.9 %copy-start.30 = (f32[256]{0:T(256)S(1)}, f32[256]{0:T(256)}, u32[]{:S(2)}) copy-start(f32[256]{0:T(256)} %param.38) | copy-start | bytes 3076
  12.7 22.9 %collective-permute-start = (f32[8,17408]{1,0:T(8,128)}, f32[8,17408]{1,0:T(8,128)S(1)}, u32[]{:S(2)}, u32[]{:S(2)}) collective-permute-start(f32[8,17408]{1,0:T(8,128)} %broadcast_select_fusion), channel_id=1, source_target_pairs={{0,252},{4,0},{8,4},{12,8},{16,12},{20,16},{24,20},{28,24},{32,28}... | collective-permute-start | bytes 1671176 | tf_op jit(solution)/shard_map/ppermute | solution.py:16
  21.2 173.6 %copy-start.19 = (pred[8]{0:T(512)(128)(4,1)}, pred[8]{0:T(512)(128)(4,1)S(1)}, u32[]{:S(2)}) copy-start(pred[8]{0:T(512)(128)(4,1)S(1)} %get-tuple-element.124) | copy-start | bytes 28
  22.4 17.9 %copy-start.21 = (f32[1,2048]{1,0:T(1,128)}, f32[1,2048]{1,0:T(1,128)S(1)}, u32[]{:S(2)}) copy-start(f32[1,2048]{1,0:T(1,128)S(1)} %get-tuple-element.101) | copy-start | bytes 24580
  35.6 4.8 %copy-start.5 = (f32[2,32,2048]{2,1,0:T(8,128)}, f32[2,32,2048]{2,1,0:T(8,128)S(1)}, u32[]{:S(2)}) copy-start(f32[2,32,2048]{2,1,0:T(8,128)S(1)} %fusion.133) | copy-start | bytes 1572868
  35.6 0.9 copy-start.6
  37.6 8.9 %copy-start.2 = (f32[8,17408]{1,0:T(8,128)}, f32[8,17408]{1,0:T(8,128)S(1)}, u32[]{:S(2)}) copy-start(f32[8,17408]{1,0:T(8,128)S(1)} %broadcast_select_fusion.1) | copy-start | bytes 1671172
  37.6 11.3 %collective-permute-start.1 = (f32[8,17408]{1,0:T(8,128)S(1)}, f32[8,17408]{1,0:T(8,128)}, u32[]{:S(2)}, u32[]{:S(2)}) collective-permute-start(f32[8,17408]{1,0:T(8,128)S(1)} %broadcast_select_fusion.1), channel_id=1, source_target_pairs={{0,248},{4,252},{8,0},{12,4},{16,8},{20,12},{24,16},{28,20},{32,24... | collective-permute-start | bytes 1671176 | tf_op jit(solution)/shard_map/ppermute | solution.py:16
  44.1 8.0 %copy-start.1 = (bf16[2048,256]{0,1:T(8,128)(2,1)}, bf16[2048,256]{0,1:T(8,128)(2,1)S(1)}, u32[]{:S(2)}) copy-start(bf16[2048,256]{0,1:T(8,128)(2,1)S(1)} %copy.81) | copy-start | bytes 3145732
  48.9 42.5 %copy-start.16 = (bf16[8,4,512]{2,1,0:T(4,128)(2,1)S(1)}, bf16[8,4,512]{2,1,0:T(4,128)(2,1)}, u32[]{:S(2)}) copy-start(bf16[8,4,512]{2,1,0:T(4,128)(2,1)} %param.23) | copy-start | bytes 98308
  50.3 55.7 %copy-start.35 = (s32[8]{0:T(128)S(1)}, s32[8]{0:T(128)}, u32[]{:S(2)}) copy-start(s32[8]{0:T(128)} %param.24) | copy-start | bytes 100
  50.3 53.3 %collective-permute-start.2 = (f32[8,17408]{1,0:T(8,128)S(1)}, f32[8,17408]{1,0:T(8,128)}, u32[]{:S(2)}, u32[]{:S(2)}) collective-permute-start(f32[8,17408]{1,0:T(8,128)S(1)} %broadcast_select_fusion.2), channel_id=1, source_target_pairs={{0,240},{4,244},{8,248},{12,252},{16,0},{20,4},{24,8},{28,12},{32,... | collective-permute-start | bytes 1671176 | tf_op jit(solution)/shard_map/ppermute | solution.py:16
  86.9 73.4 %copy-start.24 = (pred[8]{0:T(512)(128)(4,1)S(1)}, pred[8]{0:T(512)(128)(4,1)}, u32[]{:S(2)}) copy-start(pred[8]{0:T(512)(128)(4,1)} %get-tuple-element.125) | copy-start | bytes 28
  89.2 71.3 %copy-start.29 = (s32[8]{0:T(128)S(1)}, s32[8]{0:T(128)}, u32[]{:S(2)}) copy-start(s32[8]{0:T(128)} %get-tuple-element.87) | copy-start | bytes 100
  104.8 75.3 %copy-start.28 = (pred[8]{0:T(512)(128)(4,1)S(1)}, pred[8]{0:T(512)(128)(4,1)}, u32[]{:S(2)}) copy-start(pred[8]{0:T(512)(128)(4,1)} %get-tuple-element.89) | copy-start | bytes 28
  104.8 19.1 %collective-permute-start.3 = (f32[8,17408]{1,0:T(8,128)S(1)}, f32[8,17408]{1,0:T(8,128)S(1)}, u32[]{:S(2)}, u32[]{:S(2)}) collective-permute-start(f32[8,17408]{1,0:T(8,128)S(1)} %broadcast_select_fusion.3), channel_id=1, source_target_pairs={{0,224},{4,228},{8,232},{12,236},{16,240},{20,244},{24,248},{28,25... | collective-permute-start | bytes 1671176 | tf_op jit(solution)/shard_map/ppermute | solution.py:16
  124.0 36.3 %collective-permute-start.4 = (f32[8,17408]{1,0:T(8,128)S(1)}, f32[8,17408]{1,0:T(8,128)S(1)}, u32[]{:S(2)}, u32[]{:S(2)}) collective-permute-start(f32[8,17408]{1,0:T(8,128)S(1)} %broadcast_select_fusion.4), channel_id=1, source_target_pairs={{0,192},{4,196},{8,200},{12,204},{16,208},{20,212},{24,216},{28,22... | collective-permute-start | bytes 1671176 | tf_op jit(solution)/shard_map/ppermute | solution.py:16
  160.3 34.5 %copy-start.23 = (pred[8]{0:T(512)(128)(4,1)S(1)}, pred[8]{0:T(512)(128)(4,1)}, u32[]{:S(2)}) copy-start(pred[8]{0:T(512)(128)(4,1)} %get-tuple-element.86) | copy-start | bytes 28
  160.3 34.7 %copy-start.22 = (f32[1,2048]{1,0:T(1,128)S(1)}, f32[1,2048]{1,0:T(1,128)}, u32[]{:S(2)}) copy-start(f32[1,2048]{1,0:T(1,128)} %copy-done.21) | copy-start | bytes 24580
  160.3 34.7 %copy-start.36 = (bf16[2048,64]{0,1:T(8,128)(2,1)S(1)}, bf16[2048,64]{0,1:T(8,128)(2,1)}, u32[]{:S(2)}) copy-start(bf16[2048,64]{0,1:T(8,128)(2,1)} %param.36) | copy-start | bytes 786436
  160.4 19.7 %collective-permute-start.5 = (f32[8,17408]{1,0:T(8,128)S(1)}, f32[8,17408]{1,0:T(8,128)}, u32[]{:S(2)}, u32[]{:S(2)}) collective-permute-start(f32[8,17408]{1,0:T(8,128)S(1)} %broadcast_select_fusion.5), channel_id=1, source_target_pairs={{0,128},{4,132},{8,136},{12,140},{16,144},{20,148},{24,152},{28,15... | collective-permute-start | bytes 1671176 | tf_op jit(solution)/shard_map/ppermute | solution.py:16
  161.1 34.3 %copy-start.31 = (f32[256]{0:T(256)S(1)}, f32[256]{0:T(256)}, u32[]{:S(2)}) copy-start(f32[256]{0:T(256)} %param.38) | copy-start | bytes 3076
  194.1 0.6 copy-start.3
  197.4 5.5 %copy-start.7 = (bf16[8,4,2048,1]{2,1,0,3:T(4,128)(2,1)S(1)}, bf16[8,4,2048,1]{2,1,0,3:T(4,128)(2,1)}, u32[]{:S(2)}) copy-start(bf16[8,4,2048,1]{2,1,0,3:T(4,128)(2,1)} %get-tuple-element.97) | copy-start | bytes 393220
  198.9 5.9 %copy-start.10 = (f32[8,4,64]{2,1,0:T(4,128)S(1)}, f32[8,4,64]{2,1,0:T(4,128)}, u32[]{:S(2)}) copy-start(f32[8,4,64]{2,1,0:T(4,128)} %get-tuple-element.111) | copy-start | bytes 24580
  198.9 5.9 %copy-start.11 = (f32[8,4,64]{2,1,0:T(4,128)S(1)}, f32[8,4,64]{2,1,0:T(4,128)}, u32[]{:S(2)}) copy-start(f32[8,4,64]{2,1,0:T(4,128)} %get-tuple-element.108) | copy-start | bytes 24580
  198.9 5.9 %copy-start.12 = (f32[8,4,64]{2,1,0:T(4,128)S(1)}, f32[8,4,64]{2,1,0:T(4,128)}, u32[]{:S(2)}) copy-start(f32[8,4,64]{2,1,0:T(4,128)} %get-tuple-element.110) | copy-start | bytes 24580
  198.9 5.9 %copy-start.13 = (f32[8,4,64]{2,1,0:T(4,128)S(1)}, f32[8,4,64]{2,1,0:T(4,128)}, u32[]{:S(2)}) copy-start(f32[8,4,64]{2,1,0:T(4,128)} %get-tuple-element.109) | copy-start | bytes 24580
  200.9 8.0 %copy-start.20 = (f32[4,64]{1,0:T(4,128)S(1)}, f32[4,64]{1,0:T(4,128)}, u32[]{:S(2)}) copy-start(f32[4,64]{1,0:T(4,128)} %mul.345) | copy-start | bytes 3076
  200.9 8.0 %copy-start.25 = (pred[8]{0:T(512)(128)(4,1)S(1)}, pred[8]{0:T(512)(128)(4,1)}, u32[]{:S(2)}) copy-start(pred[8]{0:T(512)(128)(4,1)} %get-tuple-element.133) | copy-start | bytes 28
  200.9 8.0 %copy-start.26 = (pred[8]{0:T(512)(128)(4,1)S(1)}, pred[8]{0:T(512)(128)(4,1)}, u32[]{:S(2)}) copy-start(pred[8]{0:T(512)(128)(4,1)} %get-tuple-element.135) | copy-start | bytes 28
  200.9 8.0 %copy-start.27 = (pred[8]{0:T(512)(128)(4,1)S(1)}, pred[8]{0:T(512)(128)(4,1)}, u32[]{:S(2)}) copy-start(pred[8]{0:T(512)(128)(4,1)} %get-tuple-element.134) | copy-start | bytes 28
  211.7 5.8 %copy-start.33 = (f32[256]{0:T(256)S(1)}, f32[256]{0:T(256)}, u32[]{:S(2)}) copy-start(f32[256]{0:T(256)} %param.40) | copy-start | bytes 3076
  214.0 4.9 %copy-start.37 = (s32[8]{0:T(128)S(1)}, s32[8]{0:T(128)}, u32[]{:S(2)}) copy-start(s32[8]{0:T(128)} %broadcast_add_fusion) | copy-start | bytes 100
  214.0 4.9 %copy-start.4 = (bf16[8,2,2048]{2,0,1:T(8,128)(2,1)S(1)}, bf16[8,2,2048]{2,0,1:T(8,128)(2,1)}, u32[]{:S(2)}) copy-start(bf16[8,2,2048]{2,0,1:T(8,128)(2,1)} %copy-done.3) | copy-start | bytes 196612
  214.0 51.9 %copy-start.14 = (f32[2048]{0:T(1024)S(1)}, f32[2048]{0:T(1024)}, u32[]{:S(2)}) copy-start(f32[2048]{0:T(1024)} %param.31) | copy-start | bytes 24580
  214.0 52.1 %copy-start.15 = (f32[1,2048]{1,0:T(1,128)S(1)}, f32[1,2048]{1,0:T(1,128)}, u32[]{:S(2)}) copy-start(f32[1,2048]{1,0:T(1,128)} %get-tuple-element.99) | copy-start | bytes 24580
  218.6 77.3 %reduce-scatter.2.cloned.1.call-start = ((), (), s32[]{:S(2)}) async-start(), calls=%async_computation.2 | async-start | bytes 163840 | tf_op jit(solution)/shard_map/reduce_scatter | solution.py:291
  269.5 27.2 %copy-start.32 = (pred[8,4]{1,0:T(8,128)(4,1)S(1)}, pred[8,4]{1,0:T(8,128)(4,1)}, u32[]{:S(2)}) copy-start(pred[8,4]{1,0:T(8,128)(4,1)} %iota_compare_fusion.1) | copy-start | bytes 100
Sparse Core Ops, SparseCore 0:
  218.7 45.8 all-reduce.2
  273.1 22.6 reduce-scatter.1
where the time goes:
time: 309 us; the launch traced here: 304 us
  waiting for transfers between devices  138 us (45%)
  local copies, waits for them, and re-layouts  44.9 us (15%)
  blocking collectives  36.5 us (12%)
  other arithmetic  29.1 us (9%)
  matrix products  27 us (9%)
  between operations  14.9 us (5%)
  starting transfers between devices  12.4 us (4%)
    ppermute x6, waiting for transfers between devices, shifted_2(): return lax.ppermute(value, axis, pairs)  70.5 us
    psum x1, waiting for transfers between devices, on_device(): lax.psum(jnp.dot(flat_heads, attention_exit_projection, preferred_element...  45.6 us
    dynamic_slice x32, local copies, waits for them, and re-layouts, rebuild(): lax.scan(advance, start_state, (jnp.moveaxis(key_rows, 1, 0), jnp.moveaxi...  24.8 us
    reduce_scatter x1, waiting for transfers between devices, on_device(): lax.psum_scatter(lax.dot_general(feedforward_content_proj, flat_hidden, (...  22.2 us
    dot_general x9, matrix products, project(): result = jnp.dot(flat_rows, weight, preferred_element_type=jnp.float32)  15.1 us
    all_gather x1, blocking collectives, on_device(): lax.all_gather(chosen, 'head', axis=2, tiled=True)  12.3 us
    all_gather x1, blocking collectives, on_device(): lax.all_gather(arriving_hiddens, 'head', axis=2, tiled=True)  12.2 us
    ppermute x6, starting transfers between devices, shifted_2(): return lax.ppermute(value, axis, pairs)  12.1 us
  transfers between devices with their start and end apart: 8, of which 5 were waited for; matrix products, arithmetic and copies ran while one was open for 18% of the time, Pallas kernels for 0%

commit v1 on v0

v1 whole, which is shorter than its diff:
```python
import functools

import jax
import jax.numpy as jnp
from jax import lax
from jax.experimental import pallas as pl
from jax.experimental.pallas import tpu as pltpu
from jax.sharding import PartitionSpec as P

WIDTH = 64
REB = 2
EPSILON = 1e-05
F32 = jnp.float32
BF16 = jnp.bfloat16
HIGH = lax.Precision.HIGHEST
VMEM_LIMIT = 40 * 1024 * 1024
SMEM_SPEC = pl.BlockSpec(memory_space=pltpu.SMEM)
VMEM_SPEC = pl.BlockSpec(memory_space=pltpu.VMEM)
ANY_SPEC = pl.BlockSpec(memory_space=pl.ANY)


def rotate(value, axis, steps):
    count = lax.axis_size(axis)
    pairs = [(source, (source + steps) % count) for source in range(count)]
    return lax.ppermute(value, axis, pairs)


def on_chip(value):
    return pltpu.with_memory_space_constraint(value, pltpu.VMEM)


def call(kernel, name, out_shape, operands, scratch=()):
    specs = {"smem": SMEM_SPEC, "vmem": VMEM_SPEC, "any": ANY_SPEC}
    return pl.pallas_call(
        kernel,
        name=name,
        out_shape=out_shape,
        in_specs=[specs[place] for _, place in operands],
        out_specs=jax.tree.map(lambda _: VMEM_SPEC, out_shape),
        scratch_shapes=list(scratch),
        compiler_params=pltpu.CompilerParams(vmem_limit_bytes=VMEM_LIMIT),
    )(*[on_chip(array) if place == "vmem" else array for array, place in operands])


def out(shape, dtype):
    return jax.ShapeDtypeStruct(shape, dtype)


def normalize(rows, gain):
    centered = rows - jnp.mean(rows, axis=-1, keepdims=True)
    spread = jnp.mean(centered * centered, axis=-1, keepdims=True)
    return (centered * lax.rsqrt(spread + EPSILON) * gain).astype(BF16).astype(F32)


def dot(left, right, contract=(1, 0), precision=None):
    return lax.dot_general(
        left,
        right,
        (((contract[0],), (contract[1],)), ((), ())),
        precision=precision,
        preferred_element_type=F32,
    )


def halves(value):
    high = value.astype(BF16)
    return high, (value - high.astype(F32)).astype(BF16)


def iota(shape, axis):
    return lax.broadcasted_iota(jnp.int32, shape, axis)


def column_of(scalars, rows, lanes):
    row = iota((rows, lanes), 0)
    result = jnp.zeros((rows, lanes), jnp.int32)
    for index in range(rows):
        result = jnp.where(row == index, scalars[index], result)
    return result


def head_blocks(lanes):
    return iota((lanes, lanes), 0) // WIDTH == iota((lanes, lanes), 1) // WIDTH


def head_sums(rows):
    ones = head_blocks(rows.shape[1]).astype(BF16)
    high, low = halves(rows)
    return dot(high, ones) + dot(low, ones)


def pack_kernel(former, marks, held, state, shifts, tokens, gathered, chain_a, chain_b, part, sems):
    count = state.shape[0]
    heads = state.shape[1]
    hist = held.shape[1]
    quarter = heads * WIDTH
    rank = jnp.int32(0)
    chosen = [jnp.int32(0)] * REB
    for index in range(count):
        marked = marks[index] == 1
        chosen = [
            jnp.where(marked & (rank == place), index, value) for place, value in enumerate(chosen)
        ]
        rank = rank + marks[index]
    copies = [
        pltpu.make_async_copy(held.at[value], gathered.at[pl.ds(place * hist, hist)], sems.at[place])
        for place, value in enumerate(chosen)
    ]
    for copy in copies:
        copy.start()
    half = count // 2
    for chain, target in enumerate((chain_a, chain_b)):
        part[...] = jnp.zeros_like(part)
        for index in range(half):
            source = lax.rem(former[chain * half + index], count)
            whole = state[source]
            packed = jnp.concatenate([whole[head] for head in range(heads)], axis=1)
            target[pl.ds(index * WIDTH, WIDTH), :] = packed.astype(BF16)
            line = shifts[source]
            for piece in range(4):
                which, lane = piece // 2, (piece % 2) * quarter
                part[piece * half + index : piece * half + index + 1, :] = line[
                    which : which + 1, lane : lane + quarter
                ]
        target[pl.ds(half * WIDTH, 4 * half), :] = part[...].astype(BF16)
    gathered[pl.ds(REB * hist, tokens.shape[0]), :] = tokens[...]
    for copy in copies:
        copy.wait()


def project_kernel(
    head, occupied, own, by_one, by_two, by_three, gain, rates, w_r, w_k, w_v, w_left, w_right, base,
    a_r, a_k, a_v, a_l, rebuilt, last_hist, time_last,
    entries,
):
    ranks = 4
    feature = own.shape[1]
    hist_rows = REB * 32
    tokens = own.shape[0] - hist_rows
    count = tokens // 4
    me = head[0]
    for steps, piece in enumerate((own, by_one, by_two, by_three)):
        block = lax.rem(me - steps + ranks, ranks)
        entries[:, pl.ds(pl.multiple_of(block * feature, feature), feature)] = piece[...].astype(F32)
    current = normalize(entries[...], gain[...])
    hist = current[:hist_rows]
    live = current[hist_rows:]
    place = iota(hist.shape, 0) % 32
    hist_previous = jnp.where(place == 0, 0.0, pltpu.roll(hist, 1, 0))
    live_previous = jnp.concatenate([jnp.zeros_like(live[:count]), live[:-count]], axis=0)
    previous = jnp.concatenate([hist_previous, live_previous], axis=0)
    change = previous - current

    def mixed(which):
        return (current + change * rates[which : which + 1, :]).astype(BF16)

    a_r[...] = dot(mixed(0)[hist_rows:], w_r[...])
    keys = dot(mixed(1), w_k[...])
    values = dot(mixed(2), w_v[...])
    low = dot(mixed(3), w_left[...], (1, 1))
    a_k[...] = keys[hist_rows:]
    a_v[...] = values[hist_rows:]
    a_l[...] = low[hist_rows:]
    keys, values, low = keys[:hist_rows], values[:hist_rows], low[:hist_rows]
    rank = jnp.tanh(low).astype(BF16)
    decay = jnp.exp(-jnp.exp(base[...] + dot(rank, w_right[...])))
    spot = iota(decay.shape, 0) % 32
    product = decay
    for steps in (1, 2, 4, 8, 16):
        product = product * jnp.where(spot + steps < 32, pltpu.roll(product, hist_rows - steps, 0), 1.0)
    later = jnp.where(spot < 31, pltpu.roll(product, hist_rows - 1, 0), 1.0)
    keys = keys * later
    lane = iota((WIDTH, values.shape[1]), 1) // WIDTH
    for slot in range(REB):
        span = slice(slot * 32, slot * 32 + 32)
        k_high, k_low = halves(keys[span])
        v_high, v_low = halves(values[span])
        outer = dot(
            jnp.concatenate([k_high, k_high, k_low], axis=0),
            jnp.concatenate([v_high, v_low, v_high], axis=0),
            (0, 0),
        )
        packed = outer[:WIDTH]
        for which in range(1, values.shape[1] // WIDTH):
            packed = jnp.where(lane == which, outer[which * WIDTH : (which + 1) * WIDTH], packed)
        rebuilt[slot] = packed
        last_hist[slot : slot + 1, :] = hist[slot * 32 + 31 : slot * 32 + 32]
    occ = column_of(occupied, count, current.shape[1])
    last = jnp.zeros((count, current.shape[1]), F32)
    for slot in range(4):
        last = jnp.where(occ == slot + 1, live[slot * count : (slot + 1) * count], last)
    entries[pl.ds(0, count), :] = last
    time_last[...] = entries[pl.ds(0, count), pl.ds(pl.multiple_of(me * feature, feature), feature)]


def recur_kernel(
    head, occupied, marks, chain_a, chain_b, own, by_one, by_two, by_three, last_hist, rebuilt,
    a_r, a_k, a_v, a_l, rates, w_r, w_k, w_v, w_left, w_right, base, reward, gain, w_out,
    next_state, partial, shift_ffn,
    start_shift,
):
    ranks = 4
    count = marks.shape[0]
    half = count // 2
    quarter = own.shape[1]
    channels = a_r.shape[1]
    me = head[0]
    for steps, piece in enumerate((own, by_one, by_two, by_three)):
        block = lax.rem(me - steps + ranks, ranks)
        lines = piece[...].astype(F32)
        for chain in range(2):
            for part in range(4):
                target = start_shift if part < 2 else shift_ffn
                lane = pl.multiple_of(block * (2 * quarter) + (part % 2) * quarter, quarter)
                row = chain * 4 * half + part * half
                target[pl.ds(chain * half, half), pl.ds(lane, quarter)] = lines[row : row + half]
    rank = jnp.int32(0)
    place = []
    for index in range(count):
        place.append(jnp.where(marks[index] == 1, rank, REB))
        rank = rank + marks[index]
    slots = column_of(place, count, start_shift.shape[1])
    start = start_shift[...]
    for slot in range(REB):
        start = jnp.where(slots == slot, last_hist[slot : slot + 1, :], start)

    def first(which):
        return (start * rates[which : which + 1, :]).astype(BF16)

    def with_first(rows, extra):
        return jnp.concatenate([rows[:count] + extra, rows[count:]], axis=0)

    received = with_first(a_r[...], dot(first(0), w_r[...]))
    keys = with_first(a_k[...], dot(first(1), w_k[...]))
    values = with_first(a_v[...], dot(first(2), w_v[...]))
    low = jnp.tanh(with_first(a_l[...], dot(first(3), w_left[...], (1, 1)))).astype(BF16)
    decay = jnp.exp(-jnp.exp(base[...] + dot(low, w_right[...])))
    occ = column_of(occupied, count, channels)
    slot_of = lambda rows: [rows[slot * count : (slot + 1) * count] for slot in range(4)]
    r, k, v, d = slot_of(received), slot_of(keys), slot_of(values), slot_of(decay)
    d = [jnp.where(occ > slot, d[slot], 1.0) for slot in range(4)]
    k_live = [jnp.where(occ > slot, k[slot], 0.0) for slot in range(4)]
    before = [jnp.ones_like(d[0])]
    for slot in range(4):
        before.append(before[-1] * d[slot])
    query = jnp.concatenate([r[slot] * before[slot] for slot in range(4)], axis=0)
    scores, pairs = [], []
    for slot in range(4):
        scores.append(r[slot] * reward[...] * k[slot])
        pairs.append((slot, slot))
        between = jnp.ones_like(d[0])
        for earlier in range(slot - 1, -1, -1):
            scores.append(r[slot] * between * k_live[earlier])
            pairs.append((slot, earlier))
            between = between * d[earlier]
    sums = head_sums(jnp.concatenate(scores, axis=0))
    inner = [jnp.zeros_like(v[0])] * 4
    for index, (slot, earlier) in enumerate(pairs):
        inner[slot] = inner[slot] + sums[index * count : (index + 1) * count] * v[earlier]
    mixed = jnp.concatenate(inner, axis=0)
    after = jnp.ones_like(d[0])
    k_after = [None] * 4
    for slot in range(3, -1, -1):
        k_after[slot] = k_live[slot] * after
        after = after * d[slot]
    k_high, k_low = halves(jnp.concatenate(k_after, axis=0))
    v_high, v_low = halves(values)
    k_rows = jnp.concatenate([k_high, k_high, k_low], axis=0)
    v_rows = jnp.concatenate([v_high, v_low, v_high], axis=0).astype(F32)
    k_columns = jnp.transpose(k_rows.astype(F32)).astype(BF16)
    after_columns = jnp.transpose(before[4])
    q_high, q_low = halves(query)
    q_rows = jnp.concatenate([q_high, q_low], axis=0).astype(F32)
    q_request = iota(q_rows.shape, 0) % count
    v_request = iota(v_rows.shape, 0) % count
    blocks = head_blocks(channels)
    total = jnp.zeros((q_rows.shape[0], channels), F32)
    for index in range(count):
        chain = chain_a if index < half else chain_b
        packed = chain[pl.ds((index % half) * WIDTH, WIDTH), :].astype(F32)
        for slot in range(REB):
            packed = jnp.where(place[index] == slot, rebuilt[slot], packed)
        tall = jnp.concatenate([packed] * (channels // WIDTH), axis=0)
        tall = jnp.where(blocks, tall, 0.0).astype(BF16)
        total = total + dot(jnp.where(q_request == index, q_rows, 0.0).astype(BF16), tall)
        update = dot(k_columns, jnp.where(v_request == index, v_rows, 0.0).astype(BF16))
        for which in range(channels // WIDTH):
            rows = slice(which * WIDTH, (which + 1) * WIDTH)
            lanes = slice(which // 2 * 128, which // 2 * 128 + 128)
            block = update[rows, lanes] + after_columns[rows, index : index + 1] * packed[:, lanes]
            if which % 2:
                block = pltpu.roll(block, 64, 1)
            next_state[index, which] = block[:, :WIDTH]
    mixed = mixed + total[: 4 * count] + total[4 * count :]
    centered = mixed - head_sums(mixed) * (1.0 / WIDTH)
    spread = head_sums(centered * centered) * (1.0 / WIDTH)
    heads_out = (centered * lax.rsqrt(spread + EPSILON) * gain[...]).astype(BF16)
    partial[...] = dot(heads_out, w_out[...]).astype(BF16)


def ffn_kernel(
    head, occupied, own, by_one, by_two, by_three, p_own, p_one, p_two, p_three, shift_ffn, gain, rates,
    w_up, w_down,
    kept, to_one, to_two, to_three, channel_last,
    entries,
):
    ranks = 4
    feature = own.shape[1]
    tokens = p_own.shape[0]
    count = tokens // 4
    hist_rows = own.shape[0] - tokens
    me = head[0]
    for steps, piece in enumerate((own, by_one, by_two, by_three)):
        block = lax.rem(me - steps + ranks, ranks)
        entries[:, pl.ds(pl.multiple_of(block * feature, feature), feature)] = piece[
            pl.ds(hist_rows, tokens), :
        ].astype(F32)
    mix = sum(piece[...].astype(F32) for piece in (p_own, p_one, p_two, p_three))
    middle = (entries[...] + mix).astype(BF16).astype(F32)
    entries[...] = middle
    own_lanes = pl.ds(pl.multiple_of(me * feature, feature), feature)
    middle_own = entries[:, own_lanes]
    current = normalize(middle, gain[...])
    previous = jnp.concatenate([shift_ffn[...], current[:-count]], axis=0)
    blended = (current + (previous - current) * rates[4:5, :]).astype(BF16)
    hidden = jnp.maximum(dot(blended, w_up[...]), 0.0)
    hidden = (hidden * hidden).astype(BF16)
    for steps, target in enumerate((kept, to_one, to_two, to_three)):
        block = lax.rem(me + steps, ranks)
        lanes = pl.ds(pl.multiple_of(block * feature, feature), feature)
        rows = dot(hidden, w_down[:, lanes])
        if steps == 0:
            target[...] = rows + middle_own
        else:
            target[...] = rows.astype(BF16)
    occ = column_of(occupied, count, current.shape[1])
    last = jnp.zeros((count, current.shape[1]), F32)
    for slot in range(4):
        last = jnp.where(occ == slot + 1, current[slot * count : (slot + 1) * count], last)
    entries[pl.ds(0, count), :] = last
    channel_last[...] = entries[pl.ds(0, count), own_lanes]


def on_device(
    arriving_hiddens,
    occupied_slot_totals,
    former_indices,
    reconstruct_marks,
    retained_hiddens,
    carried_memory_matrices,
    lagged_previous_entries,
    pre_attention_scaling,
    pre_feedforward_scaling,
    lag_blend_fractions,
    acceptance_projection,
    address_projection,
    content_projection,
    fading_lowrank_left,
    fading_lowrank_right,
    fading_baseline_entries,
    present_item_reward,
    grouped_layer_scaling,
    attention_exit_projection,
    feedforward_address_proj,
    feedforward_content_proj,
):
    count, steps, feature = arriving_hiddens.shape
    half = count // 2
    heads = carried_memory_matrices.shape[1]
    channels = heads * WIDTH
    hist = retained_hiddens.shape[1]
    model = pre_attention_scaling.shape[0]
    tokens = count * steps
    groups = lax.axis_size("grp")
    head = lax.axis_index("head").astype(jnp.int32).reshape(1)
    row = lambda value: value.reshape(1, -1)
    token_rows = jnp.swapaxes(arriving_hiddens, 0, 1).reshape(tokens, feature)
    chain_rows = half * WIDTH + 4 * half
    gathered, chain_a, chain_b = call(
        pack_kernel,
        "pack",
        (
            out((REB * hist + tokens, feature), BF16),
            out((chain_rows, channels), BF16),
            out((chain_rows, channels), BF16),
        ),
        [
            (former_indices, "smem"),
            (reconstruct_marks, "smem"),
            (retained_hiddens, "any"),
            (carried_memory_matrices, "vmem"),
            (lagged_previous_entries, "vmem"),
            (token_rows, "vmem"),
        ],
        [pltpu.VMEM((4 * half, channels), F32), pltpu.SemaphoreType.DMA((REB,))],
    )
    grp_index = lax.axis_index("grp")
    offset = (former_indices // count - grp_index) % groups
    request = jnp.where(
        jnp.arange(chain_rows) < half * WIDTH, jnp.arange(chain_rows) // WIDTH, jnp.arange(chain_rows) % half
    )
    member = request[:, None] == jnp.arange(half)[None, :]
    row_offset_a = jnp.sum(jnp.where(member, offset[None, :half], 0), axis=1, keepdims=True)
    row_offset_b = jnp.sum(jnp.where(member, (groups - offset[None, half:]) % groups, 0), axis=1, keepdims=True)
    pieces = [gathered] + [rotate(gathered, "head", k) for k in (1, 3, 2)]
    pieces = [pieces[0], pieces[1], pieces[3], pieces[2]]
    for bit in range((groups - 1).bit_length()):
        moved_a = rotate(chain_a, "grp", -(1 << bit))
        moved_b = rotate(chain_b, "grp", 1 << bit)
        chain_a = jnp.where(row_offset_a >> bit & 1 == 1, moved_a, chain_a)
        chain_b = jnp.where(row_offset_b >> bit & 1 == 1, moved_b, chain_b)
    attention_gain = row(pre_attention_scaling)
    base = row(fading_baseline_entries)
    left = fading_lowrank_left.T
    a_r, a_k, a_v, a_l, rebuilt, last_hist, time_last = call(
        project_kernel,
        "project",
        (
            out((tokens, channels), F32),
            out((tokens, channels), F32),
            out((tokens, channels), F32),
            out((tokens, left.shape[0]), F32),
            out((REB, WIDTH, channels), F32),
            out((REB, model), F32),
            out((count, feature), F32),
        ),
        [(head, "smem"), (occupied_slot_totals, "smem")]
        + [
            (value, "vmem")
            for value in (
                *pieces,
                attention_gain,
                lag_blend_fractions,
                acceptance_projection,
                address_projection,
                content_projection,
                left,
                fading_lowrank_right,
                base,
            )
        ],
        [pltpu.VMEM((REB * hist + tokens, model), F32)],
    )
    shift_rows = jnp.concatenate([chain_a[half * WIDTH :], chain_b[half * WIDTH :]], axis=0)
    shift_pieces = [shift_rows] + [rotate(shift_rows, "head", k) for k in (1, 2, 3)]
    next_state, partial, shift_ffn = call(
        recur_kernel,
        "recur",
        (
            out((count, heads, WIDTH, WIDTH), F32),
            out((tokens, model), BF16),
            out((count, model), F32),
        ),
        [(head, "smem"), (occupied_slot_totals, "smem"), (reconstruct_marks, "smem")]
        + [
            (value, "vmem")
            for value in (
                chain_a,
                chain_b,
                *shift_pieces,
                last_hist,
                rebuilt,
                a_r,
                a_k,
                a_v,
                a_l,
                lag_blend_fractions,
                acceptance_projection,
                address_projection,
                content_projection,
                left,
                fading_lowrank_right,
                base,
                row(present_item_reward),
                row(grouped_layer_scaling),
                attention_exit_projection,
            )
        ],
        [pltpu.VMEM((count, model), F32)],
    )
    partials = [partial] + [rotate(partial, "head", k) for k in (1, 2, 3)]
    kept, to_one, to_two, to_three, channel_last = call(
        ffn_kernel,
        "ffn",
        (
            out((tokens, feature), F32),
            out((tokens, feature), BF16),
            out((tokens, feature), BF16),
            out((tokens, feature), BF16),
            out((count, feature), F32),
        ),
        [(head, "smem"), (occupied_slot_totals, "smem")]
        + [
            (value, "vmem")
            for value in (
                *pieces,
                *partials,
                shift_ffn,
                row(pre_feedforward_scaling),
                lag_blend_fractions,
                feedforward_address_proj,
                feedforward_content_proj,
            )
        ],
        [pltpu.VMEM((tokens, model), F32)],
    )
    arrived = [rotate(value, "head", k + 1) for k, value in enumerate((to_one, to_two, to_three))]
    result = kept + sum(value.astype(F32) for value in arrived)
    result = jnp.swapaxes(result.astype(BF16).reshape(steps, count, feature), 0, 1)
    valid_rows = jnp.arange(steps)[None, :] < occupied_slot_totals[:, None]
    result = jnp.where(valid_rows[..., None], result, jnp.zeros_like(result))
    return (result, next_state, jnp.stack([time_last, channel_last], axis=1))


def solution(mesh):
    placed = (
        P("grp", None, "head"),
        P("grp"),
        P("grp"),
        P("grp"),
        P("grp", None, "head"),
        P("grp", "head", None, None),
        P("grp", None, "head"),
        P(),
        P(),
        P(),
        P(None, "head"),
        P(None, "head"),
        P(None, "head"),
        P(),
        P(None, "head"),
        P("head"),
        P("head"),
        P("head"),
        P("head", None),
        P(None, "head"),
        P("head", None),
    )
    return jax.shard_map(
        on_device,
        mesh=mesh,
        in_specs=placed,
        out_specs=(P("grp", None, "head"), P("grp", "head", None, None), P("grp", None, "head")),
        check_vma=False,
    )
```

time: 309 us -> 113 us (0.37)
  waiting for transfers between devices: 138 us -> 31.5 us
  starting transfers between devices: 12.4 us -> 49.1 us
  blocking collectives: 36.5 us -> 0 us
  local copies, waits for them, and re-layouts: 44.9 us -> 12.4 us
  matrix products: 27 us -> 0 us
  other arithmetic: 29.1 us -> 6.66 us
  between operations: 14.9 us -> 1.04 us
  Pallas kernels: 0 us -> 10.2 us
    psum x1 -> x0, waiting for transfers between devices: 45.6 us -> none  [on_device(): lax.psum(jnp.dot(flat_heads, attention_exit_projection, preferred_element...]
    ppermute x6 -> x24, waiting for transfers between devices: 70.5 us -> 31.5 us  [rotate(): return lax.ppermute(value, axis, pairs)]
    ppermute x6 -> x24, starting transfers between devices: 12.1 us -> 49.1 us  [rotate(): return lax.ppermute(value, axis, pairs)]
    all_gather x3 -> x0, blocking collectives: 36.5 us -> none  [the longest x1 12.3 us: on_device(): lax.all_gather(chosen, 'head', axis=2, tiled=True)]
    dot_general x16 -> x0, matrix products: 27 us -> none  [the longest x9 15.1 us: project(): result = jnp.dot(flat_rows, weight, preferred_element_type=jnp.float32)]
    dynamic_slice x32 -> x0, local copies, waits for them, and re-layouts: 24.8 us -> none  [rebuild(): lax.scan(advance, start_state, (jnp.moveaxis(key_rows, 1, 0), jnp.moveaxi...]
    reduce_scatter x1 -> x0, waiting for transfers between devices: 22.2 us -> none  [on_device(): lax.psum_scatter(lax.dot_general(feedforward_content_proj, flat_hidden, (...]
    pallas_call x0 -> x4, Pallas kernels: none -> 10.2 us  [call(): pl.pallas_call(kernel, name=name, out_shape=out_shape, in_specs=[specs[pl...]
  transfers between devices with their start and end apart: 8 -> 24, of which waited for: 5 -> 14; matrix products, arithmetic and copies ran while one was open for 18% -> 6% of each run, Pallas kernels for 0% -> 2%
where the time goes in v1:
time: 113 us; the launch traced here: 111 us
  starting transfers between devices  49.1 us (43%)
  waiting for transfers between devices  31.5 us (28%)
  local copies, waits for them, and re-layouts  12.4 us (11%)
  Pallas kernels  10.2 us (9%)
  other arithmetic  6.66 us (6%)
    ppermute x24, starting transfers between devices, rotate(): return lax.ppermute(value, axis, pairs)  49.1 us
    ppermute x24, waiting for transfers between devices, rotate(): return lax.ppermute(value, axis, pairs)  31.5 us
    unnamed x51, local copies, waits for them, and re-layouts  11.4 us
    pallas_call x4, Pallas kernels, call(): pl.pallas_call(kernel, name=name, out_shape=out_shape, in_specs=[specs[pl...  10.2 us
  transfers between devices with their start and end apart: 24, of which 14 were waited for; matrix products, arithmetic and copies ran while one was open for 6% of the time, Pallas kernels for 2%

profile of v1, /device:TPU:2, one launch (start us, length us, event | category | flops | bytes accessed | tf_op | source)
XLA Modules:
  0.0 110.9 jit_solution(14560516556256152741)
XLA Ops:
  0.7 0.9 copy.32
  1.6 1.3 %copy-done.6 = f32[8,4,64,64]{3,2,1,0:T(8,128)S(1)} copy-done((f32[8,4,64,64]{3,2,1,0:T(8,128)S(1)}, f32[8,4,64,64]{3,2,1,0:T(8,128)}, u32[]{:S(2)}) %copy-start.6) | copy-done | bytes 524312
  2.9 0.9 copy-done.12
  3.9 0.8 copy-done.15
  4.6 0.7 copy-done.20
  5.3 0.7 copy-done.24
  5.9 1.5 %pack.1 = (bf16[96,512]{1,0:T(8,128)(2,1)}, bf16[272,256]{1,0:T(8,128)(2,1)S(1)}, bf16[272,256]{1,0:T(8,128)(2,1)}) custom-call(s32[8]{0:T(128)S(1)} %copy-done.24, s32[8]{0:T(128)S(1)} %copy-done.20, bf16[8,32,512]{2,1,0:T(8,128)(2,1)S(1)} %copy-done.12, f32[8,4,64,64]{3,2,1,0:T(8,128)S(1)} %copy-done.6, f32[8,2,512]{2,1,0:T(2,128)S(1)} %copy-done.15, ...), custom_call_target="tpu_custom_call" | custom-call | tf_op jit(solution)/shard_map/pack/pallas_call | solution.py:34
  7.4 1.6 %collective-permute-start = (bf16[96,512]{1,0:T(8,128)(2,1)}, bf16[96,512]{1,0:T(8,128)(2,1)}, u32[]{:S(2)}, u32[]{:S(2)}) collective-permute-start(bf16[96,512]{1,0:T(8,128)(2,1)} %get-tuple-element.21.own), channel_id=1, source_target_pairs={{0,1},{1,2},{2,3},{3,0},{4,5},{5,6},{6,7},{7,4},{8,9},{9,10},{10,1... | collective-permute-start | bytes 294920 | tf_op jit(solution)/shard_map/ppermute | solution.py:25
  9.0 2.8 %collective-permute-start.1 = (bf16[96,512]{1,0:T(8,128)(2,1)}, bf16[96,512]{1,0:T(8,128)(2,1)}, u32[]{:S(2)}, u32[]{:S(2)}) collective-permute-start(bf16[96,512]{1,0:T(8,128)(2,1)} %get-tuple-element.21.own), channel_id=1, source_target_pairs={{0,2},{1,3},{2,0},{3,1},{4,6},{5,7},{6,4},{7,5},{8,10},{9,11},{10,... | collective-permute-start | bytes 294920 | tf_op jit(solution)/shard_map/ppermute | solution.py:25
  11.9 0.4 collective-permute-start.2
  12.3 6.9 %collective-permute-start.3 = (bf16[272,256]{1,0:T(8,128)(2,1)S(1)}, bf16[272,256]{1,0:T(8,128)(2,1)}, u32[]{:S(2)}, u32[]{:S(2)}) collective-permute-start(bf16[272,256]{1,0:T(8,128)(2,1)S(1)} %get-tuple-element.22), channel_id=1, source_target_pairs={{0,252},{4,0},{8,4},{12,8},{16,12},{20,16},{24,20},{28,24},{32,28}... | collective-permute-start | bytes 417800 | tf_op jit(solution)/shard_map/ppermute | solution.py:25
  19.2 0.6 fusion.1
  19.8 0.7 and_select_fusion.1
  20.5 0.8 select_reduce_fusion
  21.3 0.9 collective-permute-done.9
  22.2 1.1 broadcast_select_fusion
  23.4 1.0 broadcast_select_fusion.6
  24.4 5.4 %collective-permute-start.4 = (bf16[272,256]{1,0:T(8,128)(2,1)S(1)}, bf16[272,256]{1,0:T(8,128)(2,1)S(1)}, u32[]{:S(2)}, u32[]{:S(2)}) collective-permute-start(bf16[272,256]{1,0:T(8,128)(2,1)S(1)} %broadcast_select_fusion.6), channel_id=1, source_target_pairs={{0,248},{4,252},{8,0},{12,4},{16,8},{20,12},{24,16},{28,20},{32,24... | collective-permute-start | bytes 417800 | tf_op jit(solution)/shard_map/ppermute | solution.py:25
  29.8 2.8 %collective-permute-done.10 = bf16[272,256]{1,0:T(8,128)(2,1)S(1)} collective-permute-done((bf16[272,256]{1,0:T(8,128)(2,1)S(1)}, bf16[272,256]{1,0:T(8,128)(2,1)S(1)}, u32[]{:S(2)}, u32[]{:S(2)}) %collective-permute-start.10) | collective-permute-done | bytes 139296 | tf_op jit(solution)/shard_map/ppermute | solution.py:25
  32.6 0.1 broadcast_select_fusion.1
  32.9 0.1 broadcast_select_fusion.7
  33.0 5.7 %collective-permute-start.5 = (bf16[272,256]{1,0:T(8,128)(2,1)S(1)}, bf16[272,256]{1,0:T(8,128)(2,1)S(1)}, u32[]{:S(2)}, u32[]{:S(2)}) collective-permute-start(bf16[272,256]{1,0:T(8,128)(2,1)S(1)} %broadcast_select_fusion.7), channel_id=1, source_target_pairs={{0,240},{4,244},{8,248},{12,252},{16,0},{20,4},{24,8},{28,12},{32,... | collective-permute-start | bytes 417800 | tf_op jit(solution)/shard_map/ppermute | solution.py:25
  38.7 3.4 %collective-permute-done.11 = bf16[272,256]{1,0:T(8,128)(2,1)S(1)} collective-permute-done((bf16[272,256]{1,0:T(8,128)(2,1)S(1)}, bf16[272,256]{1,0:T(8,128)(2,1)S(1)}, u32[]{:S(2)}, u32[]{:S(2)}) %collective-permute-start.11) | collective-permute-done | bytes 139296 | tf_op jit(solution)/shard_map/ppermute | solution.py:25
  42.1 0.1 broadcast_select_fusion.2
  42.3 0.3 collective-permute-done.5
  42.7 3.1 %collective-permute-start.6 = (bf16[272,256]{1,0:T(8,128)(2,1)S(1)}, bf16[272,256]{1,0:T(8,128)(2,1)S(1)}, u32[]{:S(2)}, u32[]{:S(2)}) collective-permute-start(bf16[272,256]{1,0:T(8,128)(2,1)S(1)} %broadcast_select_fusion.8), channel_id=1, source_target_pairs={{0,224},{4,228},{8,232},{12,236},{16,240},{20,244},{24,248},{28,25... | collective-permute-start | bytes 417800 | tf_op jit(solution)/shard_map/ppermute | solution.py:25
  45.7 4.3 %collective-permute-done.12 = bf16[272,256]{1,0:T(8,128)(2,1)S(1)} collective-permute-done((bf16[272,256]{1,0:T(8,128)(2,1)S(1)}, bf16[272,256]{1,0:T(8,128)(2,1)S(1)}, u32[]{:S(2)}, u32[]{:S(2)}) %collective-permute-start.12) | collective-permute-done | bytes 139296 | tf_op jit(solution)/shard_map/ppermute | solution.py:25
  50.0 0.1 broadcast_select_fusion.3
  50.2 0.4 collective-permute-done.6
  50.7 3.8 %collective-permute-start.7 = (bf16[272,256]{1,0:T(8,128)(2,1)S(1)}, bf16[272,256]{1,0:T(8,128)(2,1)S(1)}, u32[]{:S(2)}, u32[]{:S(2)}) collective-permute-start(bf16[272,256]{1,0:T(8,128)(2,1)S(1)} %broadcast_select_fusion.9), channel_id=1, source_target_pairs={{0,192},{4,196},{8,200},{12,204},{16,208},{20,212},{24,216},{28,22... | collective-permute-start | bytes 417800 | tf_op jit(solution)/shard_map/ppermute | solution.py:25
  54.5 5.3 %collective-permute-done.13 = bf16[272,256]{1,0:T(8,128)(2,1)S(1)} collective-permute-done((bf16[272,256]{1,0:T(8,128)(2,1)S(1)}, bf16[272,256]{1,0:T(8,128)(2,1)S(1)}, u32[]{:S(2)}, u32[]{:S(2)}) %collective-permute-start.13) | collective-permute-done | bytes 139296 | tf_op jit(solution)/shard_map/ppermute | solution.py:25
  59.8 0.1 broadcast_select_fusion.4
  59.9 5.2 %collective-permute-start.14 = (bf16[272,256]{1,0:T(8,128)(2,1)S(1)}, bf16[272,256]{1,0:T(8,128)(2,1)S(1)}, u32[]{:S(2)}, u32[]{:S(2)}) collective-permute-start(bf16[272,256]{1,0:T(8,128)(2,1)S(1)} %broadcast_select_fusion.4), channel_id=1, source_target_pairs={{0,128},{4,132},{8,136},{12,140},{16,144},{20,148},{24,152},{28,15... | collective-permute-start | bytes 417800 | tf_op jit(solution)/shard_map/ppermute | solution.py:25
  65.2 1.5 %collective-permute-start.8 = (bf16[272,256]{1,0:T(8,128)(2,1)S(1)}, bf16[272,256]{1,0:T(8,128)(2,1)S(1)}, u32[]{:S(2)}, u32[]{:S(2)}) collective-permute-start(bf16[272,256]{1,0:T(8,128)(2,1)S(1)} %broadcast_select_fusion.10), channel_id=1, source_target_pairs={{0,128},{4,132},{8,136},{12,140},{16,144},{20,148},{24,152},{28,15... | collective-permute-start | bytes 417800 | tf_op jit(solution)/shard_map/ppermute | solution.py:25
  66.7 2.5 %collective-permute-done.14 = bf16[272,256]{1,0:T(8,128)(2,1)S(1)} collective-permute-done((bf16[272,256]{1,0:T(8,128)(2,1)S(1)}, bf16[272,256]{1,0:T(8,128)(2,1)S(1)}, u32[]{:S(2)}, u32[]{:S(2)}) %collective-permute-start.14) | collective-permute-done | bytes 139296 | tf_op jit(solution)/shard_map/ppermute | solution.py:25
  69.2 0.1 broadcast_select_fusion.5.chain_b
  69.3 5.1 %collective-permute-done.8 = bf16[272,256]{1,0:T(8,128)(2,1)S(1)} collective-permute-done((bf16[272,256]{1,0:T(8,128)(2,1)S(1)}, bf16[272,256]{1,0:T(8,128)(2,1)S(1)}, u32[]{:S(2)}, u32[]{:S(2)}) %collective-permute-start.8) | collective-permute-done | bytes 139296 | tf_op jit(solution)/shard_map/ppermute | solution.py:25
  74.4 0.1 broadcast_select_fusion.11.chain_a
  74.6 0.6 copy-done.8
  75.2 0.6 pad_maximum_fusion.1.own
  75.8 3.5 %collective-permute-start.16 = (bf16[32,256]{1,0:T(8,128)(2,1)}, bf16[32,256]{1,0:T(8,128)(2,1)}, u32[]{:S(2)}, u32[]{:S(2)}) collective-permute-start(bf16[32,256]{1,0:T(8,128)(2,1)} %pad_maximum_fusion.1.own), channel_id=1, source_target_pairs={{0,2},{1,3},{2,0},{3,1},{4,6},{5,7},{6,4},{7,5},{8,10},{9,11},{10,... | collective-permute-start | bytes 49160 | tf_op jit(solution)/shard_map/ppermute | solution.py:25
  79.4 0.9 copy-done.10
  80.4 0.8 copy-done.13
  81.1 0.7 copy-done.18
  81.8 0.7 copy-done.19
  82.5 2.5 %project.1 = (f32[32,256]{1,0:T(8,128)S(1)}, f32[32,256]{1,0:T(8,128)S(1)}, f32[32,256]{1,0:T(8,128)S(1)}, f32[32,64]{1,0:T(8,128)S(1)}, f32[2,64,256]{2,1,0:T(8...) custom-call(s32[1]{0:T(128)} %bitcast.head, s32[8]{0:T(128)S(1)} %copy-done.18, ...), custom_call_target="tpu_custom_call" | custom-call | tf_op jit(solution)/shard_map/project/pallas_call | solution.py:34
  85.1 0.7 copy-done.14
  85.8 0.7 copy-done.21
  86.5 0.7 copy-done.22
  87.2 0.7 copy-done.23
  87.8 3.3 %recur.1 = (f32[8,4,64,64]{3,2,1,0:T(8,128)}, bf16[32,2048]{1,0:T(8,128)(2,1)S(1)}, f32[8,2048]{1,0:T(8,128)S(1)}) custom-call(s32[1]{0:T(128)} %bitcast.head, s32[8]{0:T(128)S(1)} %copy-done.18, s32[8]{0:T(128)S(1)} %copy-done.21, bf16[272,256]{1,0:T(8,128)(2,1)S(1)} %copy-done.9, bf16[272,256]{1,0:T(8,128)(2,1)S(1)} %broadcast_select_fusion.5.chain_b, ...), custom_call_target="tpu_custom_call" | custom-call | tf_op jit(solution)/shard_map/recur/pallas_call | solution.py:34
  91.2 2.0 %collective-permute-start.18 = (bf16[32,2048]{1,0:T(8,128)(2,1)S(1)}, bf16[32,2048]{1,0:T(8,128)(2,1)S(1)}, u32[]{:S(2)}, u32[]{:S(2)}) collective-permute-start(bf16[32,2048]{1,0:T(8,128)(2,1)S(1)} %get-tuple-element.30.p_own), channel_id=1, source_target_pairs={{0,1},{1,2},{2,3},{3,0},{4,5},{5,6},{6,7},{7,4},{8,9},{9,10},{10,1... | collective-permute-start | bytes 393224 | tf_op jit(solution)/shard_map/ppermute | solution.py:25
  93.2 1.2 %collective-permute-start.19 = (bf16[32,2048]{1,0:T(8,128)(2,1)S(1)}, bf16[32,2048]{1,0:T(8,128)(2,1)S(1)}, u32[]{:S(2)}, u32[]{:S(2)}) collective-permute-start(bf16[32,2048]{1,0:T(8,128)(2,1)S(1)} %get-tuple-element.30.p_own), channel_id=1, source_target_pairs={{0,2},{1,3},{2,0},{3,1},{4,6},{5,7},{6,4},{7,5},{8,10},{9,11},{10,... | collective-permute-start | bytes 393224 | tf_op jit(solution)/shard_map/ppermute | solution.py:25
  94.4 0.8 collective-permute-start.20
  95.3 1.2 %collective-permute-done.18.p_one = bf16[32,2048]{1,0:T(8,128)(2,1)S(1)} collective-permute-done((bf16[32,2048]{1,0:T(8,128)(2,1)S(1)}, bf16[32,2048]{1,0:T(8,128)(2,1)S(1)}, u32[]{:S(2)}, u32[]{:S(2)}) %collective-permute-start.18) | collective-permute-done | bytes 131104 | tf_op jit(solution)/shard_map/ppermute | solution.py:25
  96.5 3.3 %collective-permute-done.19.p_two = bf16[32,2048]{1,0:T(8,128)(2,1)S(1)} collective-permute-done((bf16[32,2048]{1,0:T(8,128)(2,1)S(1)}, bf16[32,2048]{1,0:T(8,128)(2,1)S(1)}, u32[]{:S(2)}, u32[]{:S(2)}) %collective-permute-start.19) | collective-permute-done | bytes 131104 | tf_op jit(solution)/shard_map/ppermute | solution.py:25
  99.8 1.0 collective-permute-done.20.p_three
  100.8 2.8 %ffn.1 = (f32[32,512]{1,0:T(8,128)S(1)}, bf16[32,512]{1,0:T(8,128)(2,1)S(1)}, bf16[32,512]{1,0:T(8,128)(2,1)S(1)}, bf16[32,512]{1,0:T(8,128)(2,1)S(1)}, f32[8,512]{1,0:T(8,128)S(1)}) custom-call(s32[1]{0:T(128)} %bitcast.head, s32[8]{0:T(128)S(1)} %copy-done.18, bf16[96,512]{1,0:T(8,128)(2,1)} %get-tuple-element.21.own, ...), custom_call_target="tpu_custom_call" | custom-call | tf_op jit(solution)/shard_map/ffn/pallas_call | solution.py:34
  103.6 0.9 collective-permute-start.21
  104.5 1.3 %collective-permute-start.22 = (bf16[32,512]{1,0:T(8,128)(2,1)S(1)}, bf16[32,512]{1,0:T(8,128)(2,1)S(1)}, u32[]{:S(2)}, u32[]{:S(2)}) collective-permute-start(bf16[32,512]{1,0:T(8,128)(2,1)S(1)} %get-tuple-element.34), channel_id=1, source_target_pairs={{0,2},{1,3},{2,0},{3,1},{4,6},{5,7},{6,4},{7,5},{8,10},{9,11},{10,... | collective-permute-start | bytes 98312 | tf_op jit(solution)/shard_map/ppermute | solution.py:25
  105.9 2.5 %collective-permute-start.23 = (bf16[32,512]{1,0:T(8,128)(2,1)S(1)}, bf16[32,512]{1,0:T(8,128)(2,1)S(1)}, u32[]{:S(2)}, u32[]{:S(2)}) collective-permute-start(bf16[32,512]{1,0:T(8,128)(2,1)S(1)} %get-tuple-element.35), channel_id=1, source_target_pairs={{0,3},{1,0},{2,1},{3,2},{4,7},{5,4},{6,5},{7,6},{8,11},{9,8},{10,9... | collective-permute-start | bytes 98312 | tf_op jit(solution)/shard_map/ppermute | solution.py:25
  108.4 0.6 copy.29
  109.0 1.0 collective-permute-done.22
  110.2 0.7 bitcast_select_fusion
  (65 shorter events, 1.0 us)
Async XLA Ops:
  0.6 78.7 %copy-start.5 = (bf16[2048,64]{0,1:T(8,128)(2,1)S(1)}, bf16[2048,64]{0,1:T(8,128)(2,1)}, u32[]{:S(2)}) copy-start(bf16[2048,64]{0,1:T(8,128)(2,1)} %param.34) | copy-start | bytes 786436
  0.6 78.7 %copy-start = (bf16[2048,256]{1,0:T(8,128)(2,1)S(1)}, bf16[2048,256]{1,0:T(8,128)(2,1)}, u32[]{:S(2)}) copy-start(bf16[2048,256]{1,0:T(8,128)(2,1)} %w_r.3) | copy-start | bytes 3145732
  0.7 78.7 %copy-start.1 = (bf16[2048,256]{1,0:T(8,128)(2,1)S(1)}, bf16[2048,256]{1,0:T(8,128)(2,1)}, u32[]{:S(2)}) copy-start(bf16[2048,256]{1,0:T(8,128)(2,1)} %w_k.3) | copy-start | bytes 3145732
  0.7 78.7 %copy-start.2 = (bf16[2048,256]{1,0:T(8,128)(2,1)S(1)}, bf16[2048,256]{1,0:T(8,128)(2,1)}, u32[]{:S(2)}) copy-start(bf16[2048,256]{1,0:T(8,128)(2,1)} %w_v.3) | copy-start | bytes 3145732
  1.6 1.3 %copy-start.6 = (f32[8,4,64,64]{3,2,1,0:T(8,128)S(1)}, f32[8,4,64,64]{3,2,1,0:T(8,128)}, u32[]{:S(2)}) copy-start(f32[8,4,64,64]{3,2,1,0:T(8,128)} %state.1) | copy-start | bytes 1572868
  2.9 0.9 copy-start.12
  3.8 0.8 copy-start.15
  4.6 0.7 copy-start.20
  5.3 0.7 copy-start.24
  5.9 73.5 %copy-start.16 = (f32[2048]{0:T(1024)S(1)}, f32[2048]{0:T(1024)}, u32[]{:S(2)}) copy-start(f32[2048]{0:T(1024)} %param.28) | copy-start | bytes 24580
  7.4 71.9 %collective-permute-start = (bf16[96,512]{1,0:T(8,128)(2,1)}, bf16[96,512]{1,0:T(8,128)(2,1)}, u32[]{:S(2)}, u32[]{:S(2)}) collective-permute-start(bf16[96,512]{1,0:T(8,128)(2,1)} %get-tuple-element.21.own), channel_id=1, source_target_pairs={{0,1},{1,2},{2,3},{3,0},{4,5},{5,6},{6,7},{7,4},{8,9},{9,10},{10,1... | collective-permute-start | bytes 294920 | tf_op jit(solution)/shard_map/ppermute | solution.py:25
  9.0 70.4 %collective-permute-start.1 = (bf16[96,512]{1,0:T(8,128)(2,1)}, bf16[96,512]{1,0:T(8,128)(2,1)}, u32[]{:S(2)}, u32[]{:S(2)}) collective-permute-start(bf16[96,512]{1,0:T(8,128)(2,1)} %get-tuple-element.21.own), channel_id=1, source_target_pairs={{0,2},{1,3},{2,0},{3,1},{4,6},{5,7},{6,4},{7,5},{8,10},{9,11},{10,... | collective-permute-start | bytes 294920 | tf_op jit(solution)/shard_map/ppermute | solution.py:25
  11.9 67.5 %collective-permute-start.2 = (bf16[96,512]{1,0:T(8,128)(2,1)}, bf16[96,512]{1,0:T(8,128)(2,1)}, u32[]{:S(2)}, u32[]{:S(2)}) collective-permute-start(bf16[96,512]{1,0:T(8,128)(2,1)} %get-tuple-element.21.own), channel_id=1, source_target_pairs={{0,3},{1,0},{2,1},{3,2},{4,7},{5,4},{6,5},{7,6},{8,11},{9,8},{10,9... | collective-permute-start | bytes 294920 | tf_op jit(solution)/shard_map/ppermute | solution.py:25
  12.3 10.0 %collective-permute-start.9 = (bf16[272,256]{1,0:T(8,128)(2,1)}, bf16[272,256]{1,0:T(8,128)(2,1)}, u32[]{:S(2)}, u32[]{:S(2)}) collective-permute-start(bf16[272,256]{1,0:T(8,128)(2,1)} %get-tuple-element.23), channel_id=1, source_target_pairs={{0,4},{4,8},{8,12},{12,16},{16,20},{20,24},{24,28},{28,32},{32,36}... | collective-permute-start | bytes 417800 | tf_op jit(solution)/shard_map/ppermute | solution.py:25
  12.3 11.1 %collective-permute-start.3 = (bf16[272,256]{1,0:T(8,128)(2,1)S(1)}, bf16[272,256]{1,0:T(8,128)(2,1)}, u32[]{:S(2)}, u32[]{:S(2)}) collective-permute-start(bf16[272,256]{1,0:T(8,128)(2,1)S(1)} %get-tuple-element.22), channel_id=1, source_target_pairs={{0,252},{4,0},{8,4},{12,8},{16,12},{20,16},{24,20},{28,24},{32,28}... | collective-permute-start | bytes 417800 | tf_op jit(solution)/shard_map/ppermute | solution.py:25
  23.3 9.3 %collective-permute-start.10 = (bf16[272,256]{1,0:T(8,128)(2,1)S(1)}, bf16[272,256]{1,0:T(8,128)(2,1)S(1)}, u32[]{:S(2)}, u32[]{:S(2)}) collective-permute-start(bf16[272,256]{1,0:T(8,128)(2,1)S(1)} %broadcast_select_fusion), channel_id=1, source_target_pairs={{0,8},{4,12},{8,16},{12,20},{16,24},{20,28},{24,32},{28,36},{32,40... | collective-permute-start | bytes 417800 | tf_op jit(solution)/shard_map/ppermute | solution.py:25
  24.4 8.4 %collective-permute-start.4 = (bf16[272,256]{1,0:T(8,128)(2,1)S(1)}, bf16[272,256]{1,0:T(8,128)(2,1)S(1)}, u32[]{:S(2)}, u32[]{:S(2)}) collective-permute-start(bf16[272,256]{1,0:T(8,128)(2,1)S(1)} %broadcast_select_fusion.6), channel_id=1, source_target_pairs={{0,248},{4,252},{8,0},{12,4},{16,8},{20,12},{24,16},{28,20},{32,24... | collective-permute-start | bytes 417800 | tf_op jit(solution)/shard_map/ppermute | solution.py:25
  32.7 9.4 %collective-permute-start.11 = (bf16[272,256]{1,0:T(8,128)(2,1)S(1)}, bf16[272,256]{1,0:T(8,128)(2,1)S(1)}, u32[]{:S(2)}, u32[]{:S(2)}) collective-permute-start(bf16[272,256]{1,0:T(8,128)(2,1)S(1)} %broadcast_select_fusion.1), channel_id=1, source_target_pairs={{0,16},{4,20},{8,24},{12,28},{16,32},{20,36},{24,40},{28,44},{32,4... | collective-permute-start | bytes 417800 | tf_op jit(solution)/shard_map/ppermute | solution.py:25
  33.0 9.6 %collective-permute-start.5 = (bf16[272,256]{1,0:T(8,128)(2,1)S(1)}, bf16[272,256]{1,0:T(8,128)(2,1)S(1)}, u32[]{:S(2)}, u32[]{:S(2)}) collective-permute-start(bf16[272,256]{1,0:T(8,128)(2,1)S(1)} %broadcast_select_fusion.7), channel_id=1, source_target_pairs={{0,240},{4,244},{8,248},{12,252},{16,0},{20,4},{24,8},{28,12},{32,... | collective-permute-start | bytes 417800 | tf_op jit(solution)/shard_map/ppermute | solution.py:25
  42.2 7.8 %collective-permute-start.12 = (bf16[272,256]{1,0:T(8,128)(2,1)S(1)}, bf16[272,256]{1,0:T(8,128)(2,1)S(1)}, u32[]{:S(2)}, u32[]{:S(2)}) collective-permute-start(bf16[272,256]{1,0:T(8,128)(2,1)S(1)} %broadcast_select_fusion.2), channel_id=1, source_target_pairs={{0,32},{4,36},{8,40},{12,44},{16,48},{20,52},{24,56},{28,60},{32,6... | collective-permute-start | bytes 417800 | tf_op jit(solution)/shard_map/ppermute | solution.py:25
  42.7 7.9 %collective-permute-start.6 = (bf16[272,256]{1,0:T(8,128)(2,1)S(1)}, bf16[272,256]{1,0:T(8,128)(2,1)S(1)}, u32[]{:S(2)}, u32[]{:S(2)}) collective-permute-start(bf16[272,256]{1,0:T(8,128)(2,1)S(1)} %broadcast_select_fusion.8), channel_id=1, source_target_pairs={{0,224},{4,228},{8,232},{12,236},{16,240},{20,244},{24,248},{28,25... | collective-permute-start | bytes 417800 | tf_op jit(solution)/shard_map/ppermute | solution.py:25
  50.1 9.7 %collective-permute-start.13 = (bf16[272,256]{1,0:T(8,128)(2,1)S(1)}, bf16[272,256]{1,0:T(8,128)(2,1)S(1)}, u32[]{:S(2)}, u32[]{:S(2)}) collective-permute-start(bf16[272,256]{1,0:T(8,128)(2,1)S(1)} %broadcast_select_fusion.3), channel_id=1, source_target_pairs={{0,64},{4,68},{8,72},{12,76},{16,80},{20,84},{24,88},{28,92},{32,9... | collective-permute-start | bytes 417800 | tf_op jit(solution)/shard_map/ppermute | solution.py:25
  50.7 14.4 %collective-permute-start.7 = (bf16[272,256]{1,0:T(8,128)(2,1)S(1)}, bf16[272,256]{1,0:T(8,128)(2,1)S(1)}, u32[]{:S(2)}, u32[]{:S(2)}) collective-permute-start(bf16[272,256]{1,0:T(8,128)(2,1)S(1)} %broadcast_select_fusion.9), channel_id=1, source_target_pairs={{0,192},{4,196},{8,200},{12,204},{16,208},{20,212},{24,216},{28,22... | collective-permute-start | bytes 417800 | tf_op jit(solution)/shard_map/ppermute | solution.py:25
  59.9 9.3 %collective-permute-start.14 = (bf16[272,256]{1,0:T(8,128)(2,1)S(1)}, bf16[272,256]{1,0:T(8,128)(2,1)S(1)}, u32[]{:S(2)}, u32[]{:S(2)}) collective-permute-start(bf16[272,256]{1,0:T(8,128)(2,1)S(1)} %broadcast_select_fusion.4), channel_id=1, source_target_pairs={{0,128},{4,132},{8,136},{12,140},{16,144},{20,148},{24,152},{28,15... | collective-permute-start | bytes 417800 | tf_op jit(solution)/shard_map/ppermute | solution.py:25
  65.2 9.2 %collective-permute-start.8 = (bf16[272,256]{1,0:T(8,128)(2,1)S(1)}, bf16[272,256]{1,0:T(8,128)(2,1)S(1)}, u32[]{:S(2)}, u32[]{:S(2)}) collective-permute-start(bf16[272,256]{1,0:T(8,128)(2,1)S(1)} %broadcast_select_fusion.10), channel_id=1, source_target_pairs={{0,128},{4,132},{8,136},{12,140},{16,144},{20,148},{24,152},{28,15... | collective-permute-start | bytes 417800 | tf_op jit(solution)/shard_map/ppermute | solution.py:25
  74.6 0.7 copy-start.8
  75.8 9.2 %collective-permute-start.15 = (bf16[32,256]{1,0:T(8,128)(2,1)}, bf16[32,256]{1,0:T(8,128)(2,1)}, u32[]{:S(2)}, u32[]{:S(2)}) collective-permute-start(bf16[32,256]{1,0:T(8,128)(2,1)} %pad_maximum_fusion.1.own), channel_id=1, source_target_pairs={{0,1},{1,2},{2,3},{3,0},{4,5},{5,6},{6,7},{7,4},{8,9},{9,10},{10,1... | collective-permute-start | bytes 49160 | tf_op jit(solution)/shard_map/ppermute | solution.py:25
  75.8 9.2 %collective-permute-start.16 = (bf16[32,256]{1,0:T(8,128)(2,1)}, bf16[32,256]{1,0:T(8,128)(2,1)}, u32[]{:S(2)}, u32[]{:S(2)}) collective-permute-start(bf16[32,256]{1,0:T(8,128)(2,1)} %pad_maximum_fusion.1.own), channel_id=1, source_target_pairs={{0,2},{1,3},{2,0},{3,1},{4,6},{5,7},{6,4},{7,5},{8,10},{9,11},{10,... | collective-permute-start | bytes 49160 | tf_op jit(solution)/shard_map/ppermute | solution.py:25
  79.3 5.7 %collective-permute-start.17 = (bf16[32,256]{1,0:T(8,128)(2,1)}, bf16[32,256]{1,0:T(8,128)(2,1)}, u32[]{:S(2)}, u32[]{:S(2)}) collective-permute-start(bf16[32,256]{1,0:T(8,128)(2,1)} %pad_maximum_fusion.1.own), channel_id=1, source_target_pairs={{0,3},{1,0},{2,1},{3,2},{4,7},{5,4},{6,5},{7,6},{8,11},{9,8},{10,9... | collective-permute-start | bytes 49160 | tf_op jit(solution)/shard_map/ppermute | solution.py:25
  79.3 5.7 %copy-start.7 = (bf16[256,2048]{1,0:T(8,128)(2,1)S(1)}, bf16[256,2048]{1,0:T(8,128)(2,1)}, u32[]{:S(2)}) copy-start(bf16[256,2048]{1,0:T(8,128)(2,1)} %w_out.1) | copy-start | bytes 3145732
  79.3 5.7 %copy-start.9 = (bf16[272,256]{1,0:T(8,128)(2,1)S(1)}, bf16[272,256]{1,0:T(8,128)(2,1)}, u32[]{:S(2)}) copy-start(bf16[272,256]{1,0:T(8,128)(2,1)} %copy-done.8) | copy-start | bytes 417796
  79.4 0.9 copy-start.10
  80.4 0.8 copy-start.13
  81.1 0.7 copy-start.18
  81.8 0.7 copy-start.19
  82.4 18.3 %copy-start.3 = (bf16[2048,896]{1,0:T(8,128)(2,1)S(1)}, bf16[2048,896]{1,0:T(8,128)(2,1)}, u32[]{:S(2)}) copy-start(bf16[2048,896]{1,0:T(8,128)(2,1)} %w_up.1) | copy-start | bytes 11010052
  82.4 18.3 %copy-start.4 = (bf16[896,2048]{1,0:T(8,128)(2,1)S(1)}, bf16[896,2048]{1,0:T(8,128)(2,1)}, u32[]{:S(2)}) copy-start(bf16[896,2048]{1,0:T(8,128)(2,1)} %w_down.1) | copy-start | bytes 11010052
  82.4 18.3 %copy-start.11 = (f32[5,2048]{1,0:T(8,128)S(1)}, f32[5,2048]{1,0:T(8,128)}, u32[]{:S(2)}) copy-start(f32[5,2048]{1,0:T(8,128)} %rates.5) | copy-start | bytes 122884
  85.1 0.8 copy-start.14
  85.8 0.7 copy-start.21
  86.5 0.7 copy-start.22
  87.2 0.7 copy-start.23
  87.8 13.0 %copy-start.17 = (f32[2048]{0:T(1024)S(1)}, f32[2048]{0:T(1024)}, u32[]{:S(2)}) copy-start(f32[2048]{0:T(1024)} %param.29) | copy-start | bytes 24580
  91.2 5.3 %collective-permute-start.18 = (bf16[32,2048]{1,0:T(8,128)(2,1)S(1)}, bf16[32,2048]{1,0:T(8,128)(2,1)S(1)}, u32[]{:S(2)}, u32[]{:S(2)}) collective-permute-start(bf16[32,2048]{1,0:T(8,128)(2,1)S(1)} %get-tuple-element.30.p_own), channel_id=1, source_target_pairs={{0,1},{1,2},{2,3},{3,0},{4,5},{5,6},{6,7},{7,4},{8,9},{9,10},{10,1... | collective-permute-start | bytes 393224 | tf_op jit(solution)/shard_map/ppermute | solution.py:25
  93.2 6.6 %collective-permute-start.19 = (bf16[32,2048]{1,0:T(8,128)(2,1)S(1)}, bf16[32,2048]{1,0:T(8,128)(2,1)S(1)}, u32[]{:S(2)}, u32[]{:S(2)}) collective-permute-start(bf16[32,2048]{1,0:T(8,128)(2,1)S(1)} %get-tuple-element.30.p_own), channel_id=1, source_target_pairs={{0,2},{1,3},{2,0},{3,1},{4,6},{5,7},{6,4},{7,5},{8,10},{9,11},{10,... | collective-permute-start | bytes 393224 | tf_op jit(solution)/shard_map/ppermute | solution.py:25
  94.4 6.4 %collective-permute-start.20 = (bf16[32,2048]{1,0:T(8,128)(2,1)S(1)}, bf16[32,2048]{1,0:T(8,128)(2,1)S(1)}, u32[]{:S(2)}, u32[]{:S(2)}) collective-permute-start(bf16[32,2048]{1,0:T(8,128)(2,1)S(1)} %get-tuple-element.30.p_own), channel_id=1, source_target_pairs={{0,3},{1,0},{2,1},{3,2},{4,7},{5,4},{6,5},{7,6},{8,11},{9,8},{10,9... | collective-permute-start | bytes 393224 | tf_op jit(solution)/shard_map/ppermute | solution.py:25
  103.6 5.4 %collective-permute-start.21 = (bf16[32,512]{1,0:T(8,128)(2,1)S(1)}, bf16[32,512]{1,0:T(8,128)(2,1)S(1)}, u32[]{:S(2)}, u32[]{:S(2)}) collective-permute-start(bf16[32,512]{1,0:T(8,128)(2,1)S(1)} %get-tuple-element.33), channel_id=1, source_target_pairs={{0,1},{1,2},{2,3},{3,0},{4,5},{5,6},{6,7},{7,4},{8,9},{9,10},{10,1... | collective-permute-start | bytes 98312 | tf_op jit(solution)/shard_map/ppermute | solution.py:25
  104.5 5.5 %collective-permute-start.22 = (bf16[32,512]{1,0:T(8,128)(2,1)S(1)}, bf16[32,512]{1,0:T(8,128)(2,1)S(1)}, u32[]{:S(2)}, u32[]{:S(2)}) collective-permute-start(bf16[32,512]{1,0:T(8,128)(2,1)S(1)} %get-tuple-element.34), channel_id=1, source_target_pairs={{0,2},{1,3},{2,0},{3,1},{4,6},{5,7},{6,4},{7,5},{8,10},{9,11},{10,... | collective-permute-start | bytes 98312 | tf_op jit(solution)/shard_map/ppermute | solution.py:25
  105.9 4.3 %collective-permute-start.23 = (bf16[32,512]{1,0:T(8,128)(2,1)S(1)}, bf16[32,512]{1,0:T(8,128)(2,1)S(1)}, u32[]{:S(2)}, u32[]{:S(2)}) collective-permute-start(bf16[32,512]{1,0:T(8,128)(2,1)S(1)} %get-tuple-element.35), channel_id=1, source_target_pairs={{0,3},{1,0},{2,1},{3,2},{4,7},{5,4},{6,5},{7,6},{8,11},{9,8},{10,9... | collective-permute-start | bytes 98312 | tf_op jit(solution)/shard_map/ppermute | solution.py:25

commit v2 on v1

v2 whole, which is shorter than its diff:
```python
import functools

import jax
import jax.numpy as jnp
from jax import lax
from jax.experimental import pallas as pl
from jax.experimental.pallas import tpu as pltpu
from jax.sharding import PartitionSpec as P

WIDTH = 64
REB = 2
EPSILON = 1e-05
F32 = jnp.float32
BF16 = jnp.bfloat16
HIGH = lax.Precision.HIGHEST
VMEM_LIMIT = 40 * 1024 * 1024
SMEM_SPEC = pl.BlockSpec(memory_space=pltpu.SMEM)
VMEM_SPEC = pl.BlockSpec(memory_space=pltpu.VMEM)
ANY_SPEC = pl.BlockSpec(memory_space=pl.ANY)


def rotate(value, axis, steps):
    count = lax.axis_size(axis)
    pairs = [(source, (source + steps) % count) for source in range(count)]
    return lax.ppermute(value, axis, pairs)


def on_chip(value):
    return pltpu.with_memory_space_constraint(value, pltpu.VMEM)


def off_chip(value):
    return pltpu.with_memory_space_constraint(value, pltpu.HBM)


SPECS = {"smem": SMEM_SPEC, "vmem": VMEM_SPEC, "load": VMEM_SPEC, "any": ANY_SPEC, "scalars": SMEM_SPEC}
PLACES = {"vmem": on_chip, "load": off_chip, "any": off_chip, "scalars": off_chip}


def call(kernel, name, out_shape, operands, scratch=(), out_specs=None):
    return pl.pallas_call(
        kernel,
        name=name,
        out_shape=out_shape,
        in_specs=[SPECS[place] for _, place in operands],
        out_specs=jax.tree.map(lambda _: VMEM_SPEC, out_shape) if out_specs is None else out_specs,
        scratch_shapes=list(scratch),
        compiler_params=pltpu.CompilerParams(vmem_limit_bytes=VMEM_LIMIT),
    )(*[PLACES.get(place, lambda value: value)(array) for array, place in operands])


def out(shape, dtype):
    return jax.ShapeDtypeStruct(shape, dtype)


def normalize(rows, gain):
    centered = rows - jnp.mean(rows, axis=-1, keepdims=True)
    spread = jnp.mean(centered * centered, axis=-1, keepdims=True)
    return (centered * lax.rsqrt(spread + EPSILON) * gain).astype(BF16).astype(F32)


def dot(left, right, contract=(1, 0), precision=None):
    return lax.dot_general(
        left,
        right,
        (((contract[0],), (contract[1],)), ((), ())),
        precision=precision,
        preferred_element_type=F32,
    )


def halves(value):
    high = value.astype(BF16)
    return high, (value - high.astype(F32)).astype(BF16)


def iota(shape, axis):
    return lax.broadcasted_iota(jnp.int32, shape, axis)


def column_of(plan, base, rows, lanes):
    row = iota((rows, lanes), 0)
    result = jnp.zeros((rows, lanes), jnp.int32)
    for index in range(rows):
        result = jnp.where(row == index, plan[base + index], result)
    return result


def head_blocks(lanes):
    return iota((lanes, lanes), 0) // WIDTH == iota((lanes, lanes), 1) // WIDTH


def head_sums(rows):
    ones = head_blocks(rows.shape[1]).astype(BF16)
    high, low = halves(rows)
    return dot(high, ones) + dot(low, ones)


STRIDES = (24, 3, 8, 1)
DIGIT, PLACE, OCCUPIED, PLAN = 0, 32, 40, 48
AUX = 7


def pack_kernel(
    former, marks, occupied, held, state, shifts, tokens,
    gathered, packed, plan,
    slots, rows, sems, row_sems,
):
    count, heads = rows.shape[0], rows.shape[1]
    hist = held.shape[1]
    groups = lax.axis_size("grp")
    here = lax.axis_index("grp")
    sources = [lax.rem(former[index], count) for index in range(count)]
    row_copies = [
        pltpu.make_async_copy(state.at[source], rows.at[index], row_sems.at[index])
        for index, source in enumerate(sources)
    ]
    for copy in row_copies:
        copy.start()
    rank = jnp.int32(0)
    chosen = [jnp.int32(0)] * REB
    for index in range(count):
        marked = marks[index] == 1
        chosen = [
            jnp.where(marked & (rank == place), index, value) for place, value in enumerate(chosen)
        ]
        plan[PLACE + index] = jnp.where(marked, rank, REB)
        rank = rank + marks[index]
        plan[OCCUPIED + index] = occupied[index]
    copies = [
        pltpu.make_async_copy(held.at[value], gathered.at[pl.ds(place * hist, hist)], sems.at[place])
        for place, value in enumerate(chosen)
    ]
    for copy in copies:
        copy.start()
    for index in range(count):
        distance = lax.rem(former[index] // count - here + groups, groups)
        low = lax.rem(distance, 8)
        low = jnp.where(low > 4, low - 8, low)
        high = lax.rem(lax.div(distance - low + groups, 8), 8)
        high = jnp.where(high > 4, high - 8, high)
        for far, near, value in ((0, 2, high), (1, 3, low)):
            triple = jnp.where(value >= 2, 1, jnp.where(value <= -2, -1, 0))
            plan[DIGIT + far * count + index] = triple
            plan[DIGIT + near * count + index] = value - 3 * triple
    base = REB * hist
    for index in range(count):
        lines = tokens[index].astype(F32)
        for slot in range(4):
            slots[slot * count + index : slot * count + index + 1, :] = lines[slot : slot + 1]
        line = shifts[sources[index]]
        for which in range(2):
            row = (4 + which) * count + index
            slots[row : row + 1, :] = line[which : which + 1]
    gathered[pl.ds(base, slots.shape[0]), :] = slots[...].astype(BF16)
    for index in range(count):
        row_copies[index].wait()
        whole = rows[index]
        wide = jnp.concatenate([whole[head] for head in range(heads)], axis=1)
        packed[pl.ds(index * WIDTH, WIDTH), :] = wide.astype(BF16)
    for copy in copies:
        copy.wait()


def digits_of(plan, stage, count):
    return [plan[DIGIT + stage * count + index] for index in range(count)]


def pick_rows(digits, plus, minus, stay, merged, count):
    for index, digit in enumerate(digits):
        rows = pl.ds(index * WIDTH, WIDTH)
        for value, source in ((1, plus), (-1, minus), (0, stay)):

            @pl.when(digit == value)
            def _(rows=rows, source=source):
                merged[rows, :] = source[rows, :]


def pick_aux(digits, plus, minus, stay, count):
    shape = (count, plus.shape[1])
    request = iota(shape, 0)
    take = jnp.zeros(shape, jnp.int32)
    for index, digit in enumerate(digits):
        take = jnp.where(request == index, digit, take)
    take = jnp.concatenate([take] * (plus.shape[0] // count), axis=0)
    plus, minus, stay = (value.astype(F32) for value in (plus, minus, stay))
    return jnp.where(take == 1, plus, jnp.where(take == -1, minus, stay))


def merge_first_kernel(plan, plus, minus, stay, aux_plus, aux_minus, aux_stay, merged):
    count = plus.shape[0] // WIDTH
    digits = digits_of(plan, 0, count)
    pick_rows(digits, plus, minus, stay, merged, count)
    picked = pick_aux(digits, aux_plus[...], aux_minus[...], aux_stay[...], count)
    merged[pl.ds(count * WIDTH, AUX * count), :] = picked.astype(BF16)


def merge_kernel(stage, plan, plus, minus, stay, merged):
    count = plus.shape[0] // (WIDTH + AUX)
    digits = digits_of(plan, stage, count)
    pick_rows(digits, plus, minus, stay, merged, count)
    tail = pl.ds(count * WIDTH, AUX * count)
    picked = pick_aux(digits, plus[tail, :], minus[tail, :], stay[tail, :], count)
    merged[tail, :] = picked.astype(BF16)


def project_kernel(
    plan, own, by_one, by_two, by_three, gain, rates, far_r, far_k, far_v, far_left, far_up, w_right, base,
    a_r, a_k, a_v, a_l, rebuilt, aux, hist_first, hist_low, time_last,
    entries, w_r, w_k, w_v, w_left, w_up, sems,
):
    copies = [
        pltpu.make_async_copy(far, near, sems.at[index])
        for index, (far, near) in enumerate(
            ((far_k, w_k), (far_v, w_v), (far_left, w_left), (far_r, w_r), (far_up, w_up))
        )
    ]
    for copy in copies:
        copy.start()
    ranks = 4
    feature = own.shape[1]
    hist_rows = REB * 32
    tokens = a_r.shape[0]
    count = tokens // 4
    normal = hist_rows + tokens
    me = lax.axis_index("head")
    for steps, piece in enumerate((own, by_one, by_two, by_three)):
        block = lax.rem(me - steps + ranks, ranks)
        entries[:, pl.ds(pl.multiple_of(block * feature, feature), feature)] = piece[...].astype(F32)
    current = normalize(entries[pl.ds(0, normal), :], gain[...])
    hist = current[:hist_rows]
    live = current[hist_rows:]
    place = iota(hist.shape, 0) % 32
    hist_previous = jnp.where(place == 0, 0.0, pltpu.roll(hist, 1, 0))
    live_previous = jnp.concatenate([jnp.zeros_like(live[:count]), live[:-count]], axis=0)
    previous = jnp.concatenate([hist_previous, live_previous], axis=0)
    change = previous - current
    moved_shift = entries[pl.ds(normal, count), :]
    lines = iota(moved_shift.shape, 0)
    last_hist = jnp.zeros_like(moved_shift)
    for slot in range(REB):
        last_hist = jnp.where(lines == slot, hist[slot * 32 + 31 : slot * 32 + 32], last_hist)
    first = jnp.concatenate([moved_shift, last_hist], axis=0)

    def mixed(which):
        rate = rates[which : which + 1, :]
        return jnp.concatenate([current + change * rate, first * rate], axis=0).astype(BF16)

    copies[0].wait()
    keys = dot(mixed(1), w_k[...])
    copies[1].wait()
    values = dot(mixed(2), w_v[...])
    copies[2].wait()
    low = dot(mixed(3), w_left[...], (1, 1))
    copies[3].wait()
    received = dot(mixed(0)[hist_rows:], w_r[...])
    a_r[...] = received[:tokens]
    a_k[...] = keys[hist_rows:normal]
    a_v[...] = values[hist_rows:normal]
    a_l[...] = low[hist_rows:normal]
    hist_first[0] = received[tokens + count :]
    hist_first[1] = keys[normal + count :]
    hist_first[2] = values[normal + count :]
    hist_low[...] = low[normal + count :]
    copies[4].wait()
    up = dot((entries[pl.ds(normal + count, count), :] * rates[4:5, :]).astype(BF16), w_up[...])
    lanes = aux.shape[1]
    whole = up.shape[1] // lanes
    left = jnp.concatenate([low[normal : normal + count], jnp.zeros((count, lanes // 2 - low.shape[1]), F32)], axis=1)
    moving = [received[tokens : tokens + count], keys[normal : normal + count], values[normal : normal + count]]
    moving += [up[:, part * lanes : (part + 1) * lanes] for part in range(whole)]
    moving += [jnp.concatenate([left, up[:, whole * lanes :]], axis=1)]
    aux[...] = jnp.concatenate(moving, axis=0).astype(BF16)
    keys, values, low = keys[:hist_rows], values[:hist_rows], low[:hist_rows]
    rank = jnp.tanh(low).astype(BF16)
    decay = jnp.exp(-jnp.exp(base[...] + dot(rank, w_right[...])))
    spot = iota(decay.shape, 0) % 32
    product = decay
    for steps in (1, 2, 4, 8, 16):
        product = product * jnp.where(spot + steps < 32, pltpu.roll(product, hist_rows - steps, 0), 1.0)
    later = jnp.where(spot < 31, pltpu.roll(product, hist_rows - 1, 0), 1.0)
    keys = keys * later
    lane = iota((WIDTH, values.shape[1]), 1) // WIDTH
    for slot in range(REB):
        span = slice(slot * 32, slot * 32 + 32)
        k_high, k_low = halves(keys[span])
        v_high, v_low = halves(values[span])
        outer = dot(
            jnp.concatenate([k_high, k_high, k_low], axis=0),
            jnp.concatenate([v_high, v_low, v_high], axis=0),
            (0, 0),
        )
        packed = outer[:WIDTH]
        for which in range(1, values.shape[1] // WIDTH):
            packed = jnp.where(lane == which, outer[which * WIDTH : (which + 1) * WIDTH], packed)
        rebuilt[slot] = packed
    occ = column_of(plan, OCCUPIED, count, current.shape[1])
    last = jnp.zeros((count, current.shape[1]), F32)
    for slot in range(4):
        last = jnp.where(occ == slot + 1, live[slot * count : (slot + 1) * count], last)
    entries[pl.ds(0, count), :] = last
    time_last[...] = entries[pl.ds(0, count), pl.ds(pl.multiple_of(me * feature, feature), feature)]


def recur_kernel(
    plan, moved, hist_first, hist_low, rebuilt, a_r, a_k, a_v, a_l, w_right, base, reward, gain, w_out,
    next_state, partial, up_first,
):
    count = next_state.shape[0]
    channels = a_r.shape[1]
    place = [plan[PLACE + index] for index in range(count)]
    slots = column_of(plan, PLACE, count, channels)
    aux = moved[pl.ds(count * WIDTH, AUX * count), :].astype(F32)
    block = lambda part: aux[part * count : (part + 1) * count]
    inner = hist_low.shape[1]

    def with_first(rows, extra, hist):
        for slot in range(REB):
            extra = jnp.where(slots[:, : extra.shape[1]] == slot, hist[slot : slot + 1, :], extra)
        return jnp.concatenate([rows[:count] + extra, rows[count:]], axis=0)

    received = with_first(a_r[...], block(0), hist_first[0])
    keys = with_first(a_k[...], block(1), hist_first[1])
    values = with_first(a_v[...], block(2), hist_first[2])
    low = jnp.tanh(with_first(a_l[...], block(6)[:, :inner], hist_low[...])).astype(BF16)
    up_first[...] = jnp.concatenate([block(3), block(4), block(5), block(6)[:, channels // 2 :]], axis=1)
    decay = jnp.exp(-jnp.exp(base[...] + dot(low, w_right[...])))
    occ = column_of(plan, OCCUPIED, count, channels)
    slot_of = lambda rows: [rows[slot * count : (slot + 1) * count] for slot in range(4)]
    r, k, v, d = slot_of(received), slot_of(keys), slot_of(values), slot_of(decay)
    d = [jnp.where(occ > slot, d[slot], 1.0) for slot in range(4)]
    k_live = [jnp.where(occ > slot, k[slot], 0.0) for slot in range(4)]
    before = [jnp.ones_like(d[0])]
    for slot in range(4):
        before.append(before[-1] * d[slot])
    query = jnp.concatenate([r[slot] * before[slot] for slot in range(4)], axis=0)
    scores, pairs = [], []
    for slot in range(4):
        scores.append(r[slot] * reward[...] * k[slot])
        pairs.append((slot, slot))
        between = jnp.ones_like(d[0])
        for earlier in range(slot - 1, -1, -1):
            scores.append(r[slot] * between * k_live[earlier])
            pairs.append((slot, earlier))
            between = between * d[earlier]
    sums = head_sums(jnp.concatenate(scores, axis=0))
    inner = [jnp.zeros_like(v[0])] * 4
    for index, (slot, earlier) in enumerate(pairs):
        inner[slot] = inner[slot] + sums[index * count : (index + 1) * count] * v[earlier]
    mixed = jnp.concatenate(inner, axis=0)
    after = jnp.ones_like(d[0])
    k_after = [None] * 4
    for slot in range(3, -1, -1):
        k_after[slot] = k_live[slot] * after
        after = after * d[slot]
    k_high, k_low = halves(jnp.concatenate(k_after, axis=0))
    v_high, v_low = halves(values)
    k_rows = jnp.concatenate([k_high, k_high, k_low], axis=0)
    v_rows = jnp.concatenate([v_high, v_low, v_high], axis=0).astype(F32)
    k_columns = jnp.transpose(k_rows.astype(F32)).astype(BF16)
    after_columns = jnp.transpose(before[4])
    q_high, q_low = halves(query)
    q_rows = jnp.concatenate([q_high, q_low], axis=0).astype(F32)
    q_request = iota(q_rows.shape, 0) % count
    v_request = iota(v_rows.shape, 0) % count
    blocks = head_blocks(channels)
    total = jnp.zeros((q_rows.shape[0], channels), F32)
    for index in range(count):
        packed = moved[pl.ds(index * WIDTH, WIDTH), :].astype(F32)
        for slot in range(REB):
            packed = jnp.where(place[index] == slot, rebuilt[slot], packed)
        tall = jnp.concatenate([packed] * (channels // WIDTH), axis=0)
        tall = jnp.where(blocks, tall, 0.0).astype(BF16)
        total = total + dot(jnp.where(q_request == index, q_rows, 0.0).astype(BF16), tall)
        update = dot(k_columns, jnp.where(v_request == index, v_rows, 0.0).astype(BF16))
        for which in range(channels // WIDTH):
            rows = slice(which * WIDTH, (which + 1) * WIDTH)
            lanes = slice(which // 2 * 128, which // 2 * 128 + 128)
            block = update[rows, lanes] + after_columns[rows, index : index + 1] * packed[:, lanes]
            if which % 2:
                block = pltpu.roll(block, 64, 1)
            next_state[index, which] = block[:, :WIDTH]
    mixed = mixed + total[: 4 * count] + total[4 * count :]
    centered = mixed - head_sums(mixed) * (1.0 / WIDTH)
    spread = head_sums(centered * centered) * (1.0 / WIDTH)
    heads_out = (centered * lax.rsqrt(spread + EPSILON) * gain[...]).astype(BF16)
    partial[...] = dot(heads_out, w_out[...]).astype(BF16)


def ffn_kernel(
    plan, own, by_one, by_two, by_three, p_own, p_one, p_two, p_three, up_first, gain, rates,
    w_up, w_down,
    kept, to_one, to_two, to_three, channel_last,
    entries,
):
    ranks = 4
    feature = own.shape[1]
    tokens = p_own.shape[0]
    count = tokens // 4
    hist_rows = REB * 32
    me = lax.axis_index("head")
    for steps, piece in enumerate((own, by_one, by_two, by_three)):
        block = lax.rem(me - steps + ranks, ranks)
        entries[:, pl.ds(pl.multiple_of(block * feature, feature), feature)] = piece[
            pl.ds(hist_rows, tokens), :
        ].astype(F32)
    mix = sum(piece[...].astype(F32) for piece in (p_own, p_one, p_two, p_three))
    middle = (entries[...] + mix).astype(BF16).astype(F32)
    entries[...] = middle
    own_lanes = pl.ds(pl.multiple_of(me * feature, feature), feature)
    middle_own = entries[:, own_lanes]
    current = normalize(middle, gain[...])
    previous = jnp.concatenate([jnp.zeros_like(current[:count]), current[:-count]], axis=0)
    blended = (current + (previous - current) * rates[4:5, :]).astype(BF16)
    hidden = dot(blended, w_up[...])
    hidden = jnp.concatenate([hidden[:count] + up_first[...], hidden[count:]], axis=0)
    hidden = jnp.maximum(hidden, 0.0)
    hidden = (hidden * hidden).astype(BF16)
    for steps, target in enumerate((kept, to_one, to_two, to_three)):
        block = lax.rem(me + steps, ranks)
        lanes = pl.ds(pl.multiple_of(block * feature, feature), feature)
        rows = dot(hidden, w_down[:, lanes])
        if steps == 0:
            target[...] = rows + middle_own
        else:
            target[...] = rows.astype(BF16)
    occ = column_of(plan, OCCUPIED, count, current.shape[1])
    last = jnp.zeros((count, current.shape[1]), F32)
    for slot in range(4):
        last = jnp.where(occ == slot + 1, current[slot * count : (slot + 1) * count], last)
    entries[pl.ds(0, count), :] = last
    channel_last[...] = entries[pl.ds(0, count), own_lanes]


def on_device(
    arriving_hiddens,
    occupied_slot_totals,
    former_indices,
    reconstruct_marks,
    retained_hiddens,
    carried_memory_matrices,
    lagged_previous_entries,
    pre_attention_scaling,
    pre_feedforward_scaling,
    lag_blend_fractions,
    acceptance_projection,
    address_projection,
    content_projection,
    fading_lowrank_left,
    fading_lowrank_right,
    fading_baseline_entries,
    present_item_reward,
    grouped_layer_scaling,
    attention_exit_projection,
    feedforward_address_proj,
    feedforward_content_proj,
):
    count, steps, feature = arriving_hiddens.shape
    heads = carried_memory_matrices.shape[1]
    channels = heads * WIDTH
    hist = retained_hiddens.shape[1]
    model = pre_attention_scaling.shape[0]
    tokens = count * steps
    row = lambda value: value.reshape(1, -1)
    gathered, packed, plan = call(
        pack_kernel,
        "pack",
        (
            out((REB * hist + tokens + 2 * count, feature), BF16),
            out((count * WIDTH, channels), BF16),
            out((PLAN,), jnp.int32),
        ),
        [
            (former_indices, "scalars"),
            (reconstruct_marks, "scalars"),
            (occupied_slot_totals, "scalars"),
            (retained_hiddens, "any"),
            (carried_memory_matrices, "any"),
            (lagged_previous_entries, "load"),
            (arriving_hiddens, "load"),
        ],
        [
            pltpu.VMEM((tokens + 2 * count, feature), F32),
            pltpu.VMEM((count, heads, WIDTH, WIDTH), F32),
            pltpu.SemaphoreType.DMA((REB,)),
            pltpu.SemaphoreType.DMA((count,)),
        ],
        (VMEM_SPEC, VMEM_SPEC, SMEM_SPEC),
    )
    both = lambda value, stride: (rotate(value, "grp", -stride), rotate(value, "grp", stride))
    plus, minus = both(packed, STRIDES[0])
    pieces = [gathered] + [rotate(gathered, "head", k) for k in (1, 2, 3)]
    base = row(fading_baseline_entries)
    weights = (
        acceptance_projection,
        address_projection,
        content_projection,
        fading_lowrank_left.T,
        feedforward_address_proj,
    )
    inner = fading_lowrank_left.shape[1]
    a_r, a_k, a_v, a_l, rebuilt, aux, hist_first, hist_low, time_last = call(
        project_kernel,
        "project",
        (
            out((tokens, channels), F32),
            out((tokens, channels), F32),
            out((tokens, channels), F32),
            out((tokens, inner), F32),
            out((REB, WIDTH, channels), F32),
            out((AUX * count, channels), BF16),
            out((3, count, channels), F32),
            out((count, inner), F32),
            out((count, feature), F32),
        ),
        [(plan, "smem")]
        + [(value, "vmem") for value in pieces]
        + [(row(pre_attention_scaling), "load"), (lag_blend_fractions, "load")]
        + [(value, "any") for value in weights]
        + [(fading_lowrank_right, "load"), (base, "load")],
        [pltpu.VMEM((REB * hist + tokens + 2 * count, model), F32)]
        + [pltpu.VMEM(value.shape, BF16) for value in weights]
        + [pltpu.SemaphoreType.DMA((len(weights),))],
    )
    aux_plus, aux_minus = both(aux, STRIDES[0])
    moved = call(
        merge_first_kernel,
        "merge0",
        out((count * (WIDTH + AUX), channels), BF16),
        [(plan, "smem")] + [(value, "vmem") for value in (plus, minus, packed, aux_plus, aux_minus, aux)],
    )
    for stage in range(1, len(STRIDES)):
        plus, minus = both(moved, STRIDES[stage])
        moved = call(
            functools.partial(merge_kernel, stage),
            "merge",
            out(moved.shape, BF16),
            [(plan, "smem")] + [(value, "vmem") for value in (plus, minus, moved)],
        )
    next_state, partial, up_first = call(
        recur_kernel,
        "recur",
        (
            out((count, heads, WIDTH, WIDTH), F32),
            out((tokens, model), BF16),
            out((count, feedforward_address_proj.shape[1]), F32),
        ),
        [(plan, "smem")]
        + [(value, "vmem") for value in (moved, hist_first, hist_low, rebuilt, a_r, a_k, a_v, a_l)]
        + [(fading_lowrank_right, "load"), (base, "load")]
        + [(row(present_item_reward), "load"), (row(grouped_layer_scaling), "load")]
        + [(attention_exit_projection, "vmem")],
    )
    partials = [partial] + [rotate(partial, "head", k) for k in (1, 2, 3)]
    kept, to_one, to_two, to_three, channel_last = call(
        ffn_kernel,
        "ffn",
        (
            out((tokens, feature), F32),
            out((tokens, feature), BF16),
            out((tokens, feature), BF16),
            out((tokens, feature), BF16),
            out((count, feature), F32),
        ),
        [(plan, "smem")]
        + [(value, "vmem") for value in (*pieces, *partials, up_first)]
        + [(row(pre_feedforward_scaling), "load"), (lag_blend_fractions, "load")]
        + [(feedforward_address_proj, "vmem"), (feedforward_content_proj, "vmem")],
        [pltpu.VMEM((tokens, model), F32)],
    )
    arrived = [rotate(value, "head", k + 1) for k, value in enumerate((to_one, to_two, to_three))]
    result = kept + sum(value.astype(F32) for value in arrived)
    result = jnp.swapaxes(result.astype(BF16).reshape(steps, count, feature), 0, 1)
    valid_rows = jnp.arange(steps)[None, :] < occupied_slot_totals[:, None]
    result = jnp.where(valid_rows[..., None], result, jnp.zeros_like(result))
    return (result, next_state, jnp.stack([time_last, channel_last], axis=1))


def solution(mesh):
    placed = (
        P("grp", None, "head"),
        P("grp"),
        P("grp"),
        P("grp"),
        P("grp", None, "head"),
        P("grp", "head", None, None),
        P("grp", None, "head"),
        P(),
        P(),
        P(),
        P(None, "head"),
        P(None, "head"),
        P(None, "head"),
        P(),
        P(None, "head"),
        P("head"),
        P("head"),
        P("head"),
        P("head", None),
        P(None, "head"),
        P("head", None),
    )
    return jax.shard_map(
        on_device,
        mesh=mesh,
        in_specs=placed,
        out_specs=(P("grp", None, "head"), P("grp", "head", None, None), P("grp", None, "head")),
        check_vma=False,
    )
```

time: 113 us -> 100 us (0.88)
  local copies, waits for them, and re-layouts: 12.4 us -> 0.66 us
  starting transfers between devices: 49.1 us -> 37.6 us
  waiting for transfers between devices: 31.5 us -> 42.4 us
  Pallas kernels: 10.2 us -> 16.4 us
  other arithmetic: 6.66 us -> 0.8 us
    ppermute x24 -> x19, starting transfers between devices: 49.1 us -> 37.6 us  [rotate(): return lax.ppermute(value, axis, pairs)]
    ppermute x24 -> x19, waiting for transfers between devices: 31.5 us -> 42.4 us  [rotate(): return lax.ppermute(value, axis, pairs)]
    unnamed x51 -> x9, local copies, waits for them, and re-layouts: 11.4 us -> 0.66 us
    pallas_call x4 -> x8, Pallas kernels: 10.2 us -> 16.4 us  [call(): pl.pallas_call(kernel, name=name, out_shape=out_shape, in_specs=[SPECS[pl...]
    select_n x14 -> x0, other arithmetic: 4.38 us -> none  [the longest x6 1.6 us: on_device(): chain_b = jnp.where(row_offset_b >> bit & 1 == 1, moved_b, chain_b)]
  transfers between devices with their start and end apart: 24 -> 19, of which waited for: 14 -> 14; matrix products, arithmetic and copies ran while one was open for 6% -> 1% of each run, Pallas kernels for 2% -> 6%
where the time goes in v2:
time: 100 us; the launch traced here: 98.6 us
  waiting for transfers between devices  42.4 us (42%)
  starting transfers between devices  37.6 us (38%)
  Pallas kernels  16.4 us (16%)
    ppermute x19, waiting for transfers between devices, rotate(): return lax.ppermute(value, axis, pairs)  42.4 us
    ppermute x19, starting transfers between devices, rotate(): return lax.ppermute(value, axis, pairs)  37.6 us
    pallas_call x8, Pallas kernels, call(): pl.pallas_call(kernel, name=name, out_shape=out_shape, in_specs=[SPECS[pl...  16.4 us
  transfers between devices with their start and end apart: 19, of which 14 were waited for; matrix products, arithmetic and copies ran while one was open for 1% of the time, Pallas kernels for 6%

profile of v2, /device:TPU:2, one launch (start us, length us, event | category | flops | bytes accessed | tf_op | source)
XLA Modules:
  0.0 98.6 jit_solution(1901282937319575232)
XLA Ops:
  0.6 3.0 %pack.1 = (bf16[112,512]{1,0:T(8,128)(2,1)S(1)}, bf16[512,256]{1,0:T(8,128)(2,1)S(1)}, s32[48]{0:T(128)S(1)}) custom-call(s32[8]{0:T(128)} %former.1, s32[8]{0:T(128)} %marks.1, s32[8]{0:T(128)} %occupied.1, bf16[8,32,512]{2,1,0:T(8,128)(2,1)} %held.1, f32[8,4,64,64]{3,2,1,0:T(8,128)} %state.1, f32[8,2,512]{2,1,0:T(2,128)} %shifts.1, bf16[8,4,512]{2,1,0:T(4,128)(2,1)} %tokens.1), custom_call_target="tpu_custom_call" | custom-call | tf_op jit(solution)/shard_map/pack/pallas_call | solution.py:41
  3.7 6.8 %collective-permute-start.3 = (bf16[512,256]{1,0:T(8,128)(2,1)S(1)}, bf16[512,256]{1,0:T(8,128)(2,1)S(1)}, u32[]{:S(2)}, u32[]{:S(2)}) collective-permute-start(bf16[512,256]{1,0:T(8,128)(2,1)S(1)} %get-tuple-element.25.stay), channel_id=1, source_target_pairs={{0,160},{4,164},{8,168},{12,172},{16,176},{20,180},{24,184},{28,18... | collective-permute-start | bytes 786440 | tf_op jit(solution)/shard_map/ppermute | solution.py:25
  10.5 0.0 collective-permute-start.4
  10.5 1.5 %collective-permute-start = (bf16[112,512]{1,0:T(8,128)(2,1)S(1)}, bf16[112,512]{1,0:T(8,128)(2,1)S(1)}, u32[]{:S(2)}, u32[]{:S(2)}) collective-permute-start(bf16[112,512]{1,0:T(8,128)(2,1)S(1)} %get-tuple-element.24.own), channel_id=1, source_target_pairs={{0,1},{1,2},{2,3},{3,0},{4,5},{5,6},{6,7},{7,4},{8,9},{9,10},{10,1... | collective-permute-start | bytes 344072 | tf_op jit(solution)/shard_map/ppermute | solution.py:25
  12.0 1.1 %collective-permute-start.1 = (bf16[112,512]{1,0:T(8,128)(2,1)S(1)}, bf16[112,512]{1,0:T(8,128)(2,1)S(1)}, u32[]{:S(2)}, u32[]{:S(2)}) collective-permute-start(bf16[112,512]{1,0:T(8,128)(2,1)S(1)} %get-tuple-element.24.own), channel_id=1, source_target_pairs={{0,2},{1,3},{2,0},{3,1},{4,6},{5,7},{6,4},{7,5},{8,10},{9,11},{10,... | collective-permute-start | bytes 344072 | tf_op jit(solution)/shard_map/ppermute | solution.py:25
  13.1 2.2 %collective-permute-start.2 = (bf16[112,512]{1,0:T(8,128)(2,1)S(1)}, bf16[112,512]{1,0:T(8,128)(2,1)S(1)}, u32[]{:S(2)}, u32[]{:S(2)}) collective-permute-start(bf16[112,512]{1,0:T(8,128)(2,1)S(1)} %get-tuple-element.24.own), channel_id=1, source_target_pairs={{0,3},{1,0},{2,1},{3,2},{4,7},{5,4},{6,5},{7,6},{8,11},{9,8},{10,9... | collective-permute-start | bytes 344072 | tf_op jit(solution)/shard_map/ppermute | solution.py:25
  15.3 0.2 collective-permute-done.by_one
  15.5 3.7 %collective-permute-done.1.by_two = bf16[112,512]{1,0:T(8,128)(2,1)S(1)} collective-permute-done((bf16[112,512]{1,0:T(8,128)(2,1)S(1)}, bf16[112,512]{1,0:T(8,128)(2,1)S(1)}, u32[]{:S(2)}, u32[]{:S(2)}) %collective-permute-start.1) | collective-permute-done | bytes 114720 | tf_op jit(solution)/shard_map/ppermute | solution.py:25
  19.1 0.5 collective-permute-done.2.by_three
  19.6 0.0 copy-start.2
  19.6 0.0 copy-start.1
  19.6 5.5 %project.1 = (f32[32,256]{1,0:T(8,128)S(1)}, f32[32,256]{1,0:T(8,128)S(1)}, f32[32,256]{1,0:T(8,128)S(1)}, f32[32,64]{1,0:T(8,128)S(1)}, f32[2,64,256]{2,1,0:T(8...) custom-call(s32[48]{0:T(128)S(1)} %get-tuple-element.23.plan, ...), custom_call_target="tpu_custom_call" | custom-call | tf_op jit(solution)/shard_map/project/pallas_call | solution.py:41
  25.1 0.0 copy-start.3
  25.1 0.0 copy-start
  25.1 4.8 %collective-permute-start.5 = (bf16[56,256]{1,0:T(8,128)(2,1)S(1)}, bf16[56,256]{1,0:T(8,128)(2,1)S(1)}, u32[]{:S(2)}, u32[]{:S(2)}) collective-permute-start(bf16[56,256]{1,0:T(8,128)(2,1)S(1)} %get-tuple-element.26.aux_stay), channel_id=1, source_target_pairs={{0,160},{4,164},{8,168},{12,172},{16,176},{20,180},{24,184},{28,18... | collective-permute-start | bytes 86024 | tf_op jit(solution)/shard_map/ppermute | solution.py:25
  30.0 0.0 collective-permute-start.6
  30.0 1.6 %collective-permute-done.5.aux_plus = bf16[56,256]{1,0:T(8,128)(2,1)S(1)} collective-permute-done((bf16[56,256]{1,0:T(8,128)(2,1)S(1)}, bf16[56,256]{1,0:T(8,128)(2,1)S(1)}, u32[]{:S(2)}, u32[]{:S(2)}) %collective-permute-start.5) | collective-permute-done | bytes 28704 | tf_op jit(solution)/shard_map/ppermute | solution.py:25
  31.5 5.6 %collective-permute-done.6.aux_minus = bf16[56,256]{1,0:T(8,128)(2,1)S(1)} collective-permute-done((bf16[56,256]{1,0:T(8,128)(2,1)S(1)}, bf16[56,256]{1,0:T(8,128)(2,1)S(1)}, u32[]{:S(2)}, u32[]{:S(2)}) %collective-permute-start.6) | collective-permute-done | bytes 28704 | tf_op jit(solution)/shard_map/ppermute | solution.py:25
  37.1 0.0 collective-permute-done.3.plus
  37.2 0.0 collective-permute-done.4.minus
  37.2 0.7 merge0.1.stay
  37.8 0.1 collective-permute-start.7
  37.9 1.7 %collective-permute-start.8 = (bf16[568,256]{1,0:T(8,128)(2,1)S(1)}, bf16[568,256]{1,0:T(8,128)(2,1)S(1)}, u32[]{:S(2)}, u32[]{:S(2)}) collective-permute-start(bf16[568,256]{1,0:T(8,128)(2,1)S(1)} %merge0.1.stay), channel_id=1, source_target_pairs={{0,12},{4,16},{8,20},{12,24},{16,28},{20,32},{24,36},{28,40},{32,4... | collective-permute-start | bytes 872456 | tf_op jit(solution)/shard_map/ppermute | solution.py:25
  39.7 7.5 %collective-permute-done.7.plus = bf16[568,256]{1,0:T(8,128)(2,1)S(1)} collective-permute-done((bf16[568,256]{1,0:T(8,128)(2,1)S(1)}, bf16[568,256]{1,0:T(8,128)(2,1)S(1)}, u32[]{:S(2)}, u32[]{:S(2)}) %collective-permute-start.7) | collective-permute-done | bytes 290848 | tf_op jit(solution)/shard_map/ppermute | solution.py:25
  47.1 1.9 %collective-permute-done.8.minus = bf16[568,256]{1,0:T(8,128)(2,1)S(1)} collective-permute-done((bf16[568,256]{1,0:T(8,128)(2,1)S(1)}, bf16[568,256]{1,0:T(8,128)(2,1)S(1)}, u32[]{:S(2)}, u32[]{:S(2)}) %collective-permute-start.8) | collective-permute-done | bytes 290848 | tf_op jit(solution)/shard_map/ppermute | solution.py:25
  49.0 0.7 merge.3.stay
  49.7 0.5 collective-permute-start.10
  50.2 2.8 %collective-permute-start.9 = (bf16[568,256]{1,0:T(8,128)(2,1)S(1)}, bf16[568,256]{1,0:T(8,128)(2,1)S(1)}, u32[]{:S(2)}, u32[]{:S(2)}) collective-permute-start(bf16[568,256]{1,0:T(8,128)(2,1)S(1)} %merge.3.stay), channel_id=1, source_target_pairs={{0,224},{4,228},{8,232},{12,236},{16,240},{20,244},{24,248},{28,25... | collective-permute-start | bytes 872456 | tf_op jit(solution)/shard_map/ppermute | solution.py:25
  53.0 5.8 %collective-permute-done.10.minus = bf16[568,256]{1,0:T(8,128)(2,1)S(1)} collective-permute-done((bf16[568,256]{1,0:T(8,128)(2,1)S(1)}, bf16[568,256]{1,0:T(8,128)(2,1)S(1)}, u32[]{:S(2)}, u32[]{:S(2)}) %collective-permute-start.10) | collective-permute-done | bytes 290848 | tf_op jit(solution)/shard_map/ppermute | solution.py:25
  58.8 0.0 collective-permute-done.9.plus
  58.8 0.7 merge.4.stay
  59.5 7.1 %collective-permute-start.11 = (bf16[568,256]{1,0:T(8,128)(2,1)S(1)}, bf16[568,256]{1,0:T(8,128)(2,1)S(1)}, u32[]{:S(2)}, u32[]{:S(2)}) collective-permute-start(bf16[568,256]{1,0:T(8,128)(2,1)S(1)} %merge.4.stay), channel_id=1, source_target_pairs={{0,252},{4,0},{8,4},{12,8},{16,12},{20,16},{24,20},{28,24},{32,28}... | collective-permute-start | bytes 872456 | tf_op jit(solution)/shard_map/ppermute | solution.py:25
  66.6 0.0 collective-permute-start.12
  66.6 4.2 %collective-permute-done.11.plus = bf16[568,256]{1,0:T(8,128)(2,1)S(1)} collective-permute-done((bf16[568,256]{1,0:T(8,128)(2,1)S(1)}, bf16[568,256]{1,0:T(8,128)(2,1)S(1)}, u32[]{:S(2)}, u32[]{:S(2)}) %collective-permute-start.11) | collective-permute-done | bytes 290848 | tf_op jit(solution)/shard_map/ppermute | solution.py:25
  70.8 5.2 %collective-permute-done.12.minus = bf16[568,256]{1,0:T(8,128)(2,1)S(1)} collective-permute-done((bf16[568,256]{1,0:T(8,128)(2,1)S(1)}, bf16[568,256]{1,0:T(8,128)(2,1)S(1)}, u32[]{:S(2)}, u32[]{:S(2)}) %collective-permute-start.12) | collective-permute-done | bytes 290848 | tf_op jit(solution)/shard_map/ppermute | solution.py:25
  76.0 0.7 merge.5.moved
  76.7 0.0 copy-done.2
  76.7 2.7 %recur.1 = (f32[8,4,64,64]{3,2,1,0:T(8,128)}, bf16[32,2048]{1,0:T(8,128)(2,1)S(1)}, f32[8,896]{1,0:T(8,128)S(1)}) custom-call(s32[48]{0:T(128)S(1)} %get-tuple-element.23.plan, bf16[568,256]{1,0:T(8,128)(2,1)S(1)} %merge.5.moved, f32[3,8,256]{2,1,0:T(8,128)S(1)} %get-tuple-element.27.hist_first, f32[8,64]{1,0:T(8,128)S(1)} %get-tuple-element.28.hist_low, ...), custom_call_target="tpu_custom_call" | custom-call | tf_op jit(solution)/shard_map/recur/pallas_call | solution.py:41
  79.4 1.3 %collective-permute-start.13 = (bf16[32,2048]{1,0:T(8,128)(2,1)S(1)}, bf16[32,2048]{1,0:T(8,128)(2,1)S(1)}, u32[]{:S(2)}, u32[]{:S(2)}) collective-permute-start(bf16[32,2048]{1,0:T(8,128)(2,1)S(1)} %get-tuple-element.34.p_own), channel_id=1, source_target_pairs={{0,1},{1,2},{2,3},{3,0},{4,5},{5,6},{6,7},{7,4},{8,9},{9,10},{10,1... | collective-permute-start | bytes 393224 | tf_op jit(solution)/shard_map/ppermute | solution.py:25
  80.6 0.9 collective-permute-start.14
  81.6 2.0 %collective-permute-start.15 = (bf16[32,2048]{1,0:T(8,128)(2,1)S(1)}, bf16[32,2048]{1,0:T(8,128)(2,1)S(1)}, u32[]{:S(2)}, u32[]{:S(2)}) collective-permute-start(bf16[32,2048]{1,0:T(8,128)(2,1)S(1)} %get-tuple-element.34.p_own), channel_id=1, source_target_pairs={{0,3},{1,0},{2,1},{3,2},{4,7},{5,4},{6,5},{7,6},{8,11},{9,8},{10,9... | collective-permute-start | bytes 393224 | tf_op jit(solution)/shard_map/ppermute | solution.py:25
  83.6 0.0 copy-done.3
  83.6 0.1 iota_compare_fusion
  83.7 0.6 collective-permute-done.13.p_one
  84.3 3.5 %collective-permute-done.14.p_two = bf16[32,2048]{1,0:T(8,128)(2,1)S(1)} collective-permute-done((bf16[32,2048]{1,0:T(8,128)(2,1)S(1)}, bf16[32,2048]{1,0:T(8,128)(2,1)S(1)}, u32[]{:S(2)}, u32[]{:S(2)}) %collective-permute-start.14) | collective-permute-done | bytes 131104 | tf_op jit(solution)/shard_map/ppermute | solution.py:25
  87.8 0.8 collective-permute-done.15.p_three
  88.6 0.0 copy-done.1
  88.6 0.0 copy-done
  88.6 2.6 %ffn.1 = (f32[32,512]{1,0:T(8,128)S(1)}, bf16[32,512]{1,0:T(8,128)(2,1)S(1)}, bf16[32,512]{1,0:T(8,128)(2,1)S(1)}, bf16[32,512]{1,0:T(8,128)(2,1)S(1)}, f32[8,512]{1,0:T(8,128)S(1)}) custom-call(s32[48]{0:T(128)S(1)} %get-tuple-element.23.plan, bf16[112,512]{1,0:T(8,128)(2,1)S(1)} %get-tuple-element.24.own, ...), custom_call_target="tpu_custom_call" | custom-call | tf_op jit(solution)/shard_map/ffn/pallas_call | solution.py:41
  91.2 1.2 %collective-permute-start.16 = (bf16[32,512]{1,0:T(8,128)(2,1)S(1)}, bf16[32,512]{1,0:T(8,128)(2,1)S(1)}, u32[]{:S(2)}, u32[]{:S(2)}) collective-permute-start(bf16[32,512]{1,0:T(8,128)(2,1)S(1)} %get-tuple-element.37), channel_id=1, source_target_pairs={{0,1},{1,2},{2,3},{3,0},{4,5},{5,6},{6,7},{7,4},{8,9},{9,10},{10,1... | collective-permute-start | bytes 98312 | tf_op jit(solution)/shard_map/ppermute | solution.py:25
  92.4 1.1 %collective-permute-start.17 = (bf16[32,512]{1,0:T(8,128)(2,1)S(1)}, bf16[32,512]{1,0:T(8,128)(2,1)S(1)}, u32[]{:S(2)}, u32[]{:S(2)}) collective-permute-start(bf16[32,512]{1,0:T(8,128)(2,1)S(1)} %get-tuple-element.38), channel_id=1, source_target_pairs={{0,2},{1,3},{2,0},{3,1},{4,6},{5,7},{6,4},{7,5},{8,10},{9,11},{10,... | collective-permute-start | bytes 98312 | tf_op jit(solution)/shard_map/ppermute | solution.py:25
  93.5 2.4 %collective-permute-start.18 = (bf16[32,512]{1,0:T(8,128)(2,1)S(1)}, bf16[32,512]{1,0:T(8,128)(2,1)S(1)}, u32[]{:S(2)}, u32[]{:S(2)}) collective-permute-start(bf16[32,512]{1,0:T(8,128)(2,1)S(1)} %get-tuple-element.39), channel_id=1, source_target_pairs={{0,3},{1,0},{2,1},{3,2},{4,7},{5,4},{6,5},{7,6},{8,11},{9,8},{10,9... | collective-permute-start | bytes 98312 | tf_op jit(solution)/shard_map/ppermute | solution.py:25
  96.0 0.6 copy.25
  96.6 0.0 collective-permute-done.16
  96.6 1.3 %collective-permute-done.17 = bf16[32,512]{1,0:T(8,128)(2,1)S(1)} collective-permute-done((bf16[32,512]{1,0:T(8,128)(2,1)S(1)}, bf16[32,512]{1,0:T(8,128)(2,1)S(1)}, u32[]{:S(2)}, u32[]{:S(2)}) %collective-permute-start.17) | collective-permute-done | bytes 32800 | tf_op jit(solution)/shard_map/ppermute | solution.py:25
  97.9 0.0 collective-permute-done.18
  97.9 0.7 bitcast_select_fusion
  (2 shorter events, 0.0 us)
Async XLA Ops:
  3.7 33.5 %collective-permute-start.3 = (bf16[512,256]{1,0:T(8,128)(2,1)S(1)}, bf16[512,256]{1,0:T(8,128)(2,1)S(1)}, u32[]{:S(2)}, u32[]{:S(2)}) collective-permute-start(bf16[512,256]{1,0:T(8,128)(2,1)S(1)} %get-tuple-element.25.stay), channel_id=1, source_target_pairs={{0,160},{4,164},{8,168},{12,172},{16,176},{20,180},{24,184},{28,18... | collective-permute-start | bytes 786440 | tf_op jit(solution)/shard_map/ppermute | solution.py:25
  10.5 26.7 %collective-permute-start.4 = (bf16[512,256]{1,0:T(8,128)(2,1)S(1)}, bf16[512,256]{1,0:T(8,128)(2,1)S(1)}, u32[]{:S(2)}, u32[]{:S(2)}) collective-permute-start(bf16[512,256]{1,0:T(8,128)(2,1)S(1)} %get-tuple-element.25.stay), channel_id=1, source_target_pairs={{0,96},{4,100},{8,104},{12,108},{16,112},{20,116},{24,120},{28,124... | collective-permute-start | bytes 786440 | tf_op jit(solution)/shard_map/ppermute | solution.py:25
  10.5 5.0 %collective-permute-start = (bf16[112,512]{1,0:T(8,128)(2,1)S(1)}, bf16[112,512]{1,0:T(8,128)(2,1)S(1)}, u32[]{:S(2)}, u32[]{:S(2)}) collective-permute-start(bf16[112,512]{1,0:T(8,128)(2,1)S(1)} %get-tuple-element.24.own), channel_id=1, source_target_pairs={{0,1},{1,2},{2,3},{3,0},{4,5},{5,6},{6,7},{7,4},{8,9},{9,10},{10,1... | collective-permute-start | bytes 344072 | tf_op jit(solution)/shard_map/ppermute | solution.py:25
  12.0 7.2 %collective-permute-start.1 = (bf16[112,512]{1,0:T(8,128)(2,1)S(1)}, bf16[112,512]{1,0:T(8,128)(2,1)S(1)}, u32[]{:S(2)}, u32[]{:S(2)}) collective-permute-start(bf16[112,512]{1,0:T(8,128)(2,1)S(1)} %get-tuple-element.24.own), channel_id=1, source_target_pairs={{0,2},{1,3},{2,0},{3,1},{4,6},{5,7},{6,4},{7,5},{8,10},{9,11},{10,... | collective-permute-start | bytes 344072 | tf_op jit(solution)/shard_map/ppermute | solution.py:25
  13.1 6.5 %collective-permute-start.2 = (bf16[112,512]{1,0:T(8,128)(2,1)S(1)}, bf16[112,512]{1,0:T(8,128)(2,1)S(1)}, u32[]{:S(2)}, u32[]{:S(2)}) collective-permute-start(bf16[112,512]{1,0:T(8,128)(2,1)S(1)} %get-tuple-element.24.own), channel_id=1, source_target_pairs={{0,3},{1,0},{2,1},{3,2},{4,7},{5,4},{6,5},{7,6},{8,11},{9,8},{10,9... | collective-permute-start | bytes 344072 | tf_op jit(solution)/shard_map/ppermute | solution.py:25
  19.6 57.1 %copy-start.2 = (bf16[256,2048]{1,0:T(8,128)(2,1)S(1)}, bf16[256,2048]{1,0:T(8,128)(2,1)}, u32[]{:S(2)}) copy-start(bf16[256,2048]{1,0:T(8,128)(2,1)} %w_out.1) | copy-start | bytes 3145732
  19.6 69.0 %copy-start.1 = (bf16[896,2048]{1,0:T(8,128)(2,1)S(1)}, bf16[896,2048]{1,0:T(8,128)(2,1)}, u32[]{:S(2)}) copy-start(bf16[896,2048]{1,0:T(8,128)(2,1)} %w_down.1) | copy-start | bytes 11010052
  25.1 58.5 %copy-start.3 = (s32[8]{0:T(128)S(1)}, s32[8]{0:T(128)}, u32[]{:S(2)}) copy-start(s32[8]{0:T(128)} %occupied.1) | copy-start | bytes 100
  25.1 63.5 %copy-start = (bf16[2048,896]{1,0:T(8,128)(2,1)S(1)}, bf16[2048,896]{1,0:T(8,128)(2,1)}, u32[]{:S(2)}) copy-start(bf16[2048,896]{1,0:T(8,128)(2,1)} %w_up.1) | copy-start | bytes 11010052
  25.1 6.4 %collective-permute-start.5 = (bf16[56,256]{1,0:T(8,128)(2,1)S(1)}, bf16[56,256]{1,0:T(8,128)(2,1)S(1)}, u32[]{:S(2)}, u32[]{:S(2)}) collective-permute-start(bf16[56,256]{1,0:T(8,128)(2,1)S(1)} %get-tuple-element.26.aux_stay), channel_id=1, source_target_pairs={{0,160},{4,164},{8,168},{12,172},{16,176},{20,180},{24,184},{28,18... | collective-permute-start | bytes 86024 | tf_op jit(solution)/shard_map/ppermute | solution.py:25
  30.0 7.2 %collective-permute-start.6 = (bf16[56,256]{1,0:T(8,128)(2,1)S(1)}, bf16[56,256]{1,0:T(8,128)(2,1)S(1)}, u32[]{:S(2)}, u32[]{:S(2)}) collective-permute-start(bf16[56,256]{1,0:T(8,128)(2,1)S(1)} %get-tuple-element.26.aux_stay), channel_id=1, source_target_pairs={{0,96},{4,100},{8,104},{12,108},{16,112},{20,116},{24,120},{28,124... | collective-permute-start | bytes 86024 | tf_op jit(solution)/shard_map/ppermute | solution.py:25
  37.8 9.3 %collective-permute-start.7 = (bf16[568,256]{1,0:T(8,128)(2,1)S(1)}, bf16[568,256]{1,0:T(8,128)(2,1)S(1)}, u32[]{:S(2)}, u32[]{:S(2)}) collective-permute-start(bf16[568,256]{1,0:T(8,128)(2,1)S(1)} %merge0.1.stay), channel_id=1, source_target_pairs={{0,244},{4,248},{8,252},{12,0},{16,4},{20,8},{24,12},{28,16},{32,2... | collective-permute-start | bytes 872456 | tf_op jit(solution)/shard_map/ppermute | solution.py:25
  37.9 11.1 %collective-permute-start.8 = (bf16[568,256]{1,0:T(8,128)(2,1)S(1)}, bf16[568,256]{1,0:T(8,128)(2,1)S(1)}, u32[]{:S(2)}, u32[]{:S(2)}) collective-permute-start(bf16[568,256]{1,0:T(8,128)(2,1)S(1)} %merge0.1.stay), channel_id=1, source_target_pairs={{0,12},{4,16},{8,20},{12,24},{16,28},{20,32},{24,36},{28,40},{32,4... | collective-permute-start | bytes 872456 | tf_op jit(solution)/shard_map/ppermute | solution.py:25
  49.7 9.2 %collective-permute-start.10 = (bf16[568,256]{1,0:T(8,128)(2,1)S(1)}, bf16[568,256]{1,0:T(8,128)(2,1)S(1)}, u32[]{:S(2)}, u32[]{:S(2)}) collective-permute-start(bf16[568,256]{1,0:T(8,128)(2,1)S(1)} %merge.3.stay), channel_id=1, source_target_pairs={{0,32},{4,36},{8,40},{12,44},{16,48},{20,52},{24,56},{28,60},{32,6... | collective-permute-start | bytes 872456 | tf_op jit(solution)/shard_map/ppermute | solution.py:25
  50.2 8.7 %collective-permute-start.9 = (bf16[568,256]{1,0:T(8,128)(2,1)S(1)}, bf16[568,256]{1,0:T(8,128)(2,1)S(1)}, u32[]{:S(2)}, u32[]{:S(2)}) collective-permute-start(bf16[568,256]{1,0:T(8,128)(2,1)S(1)} %merge.3.stay), channel_id=1, source_target_pairs={{0,224},{4,228},{8,232},{12,236},{16,240},{20,244},{24,248},{28,25... | collective-permute-start | bytes 872456 | tf_op jit(solution)/shard_map/ppermute | solution.py:25
  59.5 11.3 %collective-permute-start.11 = (bf16[568,256]{1,0:T(8,128)(2,1)S(1)}, bf16[568,256]{1,0:T(8,128)(2,1)S(1)}, u32[]{:S(2)}, u32[]{:S(2)}) collective-permute-start(bf16[568,256]{1,0:T(8,128)(2,1)S(1)} %merge.4.stay), channel_id=1, source_target_pairs={{0,252},{4,0},{8,4},{12,8},{16,12},{20,16},{24,20},{28,24},{32,28}... | collective-permute-start | bytes 872456 | tf_op jit(solution)/shard_map/ppermute | solution.py:25
  66.6 9.4 %collective-permute-start.12 = (bf16[568,256]{1,0:T(8,128)(2,1)S(1)}, bf16[568,256]{1,0:T(8,128)(2,1)S(1)}, u32[]{:S(2)}, u32[]{:S(2)}) collective-permute-start(bf16[568,256]{1,0:T(8,128)(2,1)S(1)} %merge.4.stay), channel_id=1, source_target_pairs={{0,4},{4,8},{8,12},{12,16},{16,20},{20,24},{24,28},{28,32},{32,36}... | collective-permute-start | bytes 872456 | tf_op jit(solution)/shard_map/ppermute | solution.py:25
  79.4 5.0 %collective-permute-start.13 = (bf16[32,2048]{1,0:T(8,128)(2,1)S(1)}, bf16[32,2048]{1,0:T(8,128)(2,1)S(1)}, u32[]{:S(2)}, u32[]{:S(2)}) collective-permute-start(bf16[32,2048]{1,0:T(8,128)(2,1)S(1)} %get-tuple-element.34.p_own), channel_id=1, source_target_pairs={{0,1},{1,2},{2,3},{3,0},{4,5},{5,6},{6,7},{7,4},{8,9},{9,10},{10,1... | collective-permute-start | bytes 393224 | tf_op jit(solution)/shard_map/ppermute | solution.py:25
  80.6 7.2 %collective-permute-start.14 = (bf16[32,2048]{1,0:T(8,128)(2,1)S(1)}, bf16[32,2048]{1,0:T(8,128)(2,1)S(1)}, u32[]{:S(2)}, u32[]{:S(2)}) collective-permute-start(bf16[32,2048]{1,0:T(8,128)(2,1)S(1)} %get-tuple-element.34.p_own), channel_id=1, source_target_pairs={{0,2},{1,3},{2,0},{3,1},{4,6},{5,7},{6,4},{7,5},{8,10},{9,11},{10,... | collective-permute-start | bytes 393224 | tf_op jit(solution)/shard_map/ppermute | solution.py:25
  81.6 7.1 %collective-permute-start.15 = (bf16[32,2048]{1,0:T(8,128)(2,1)S(1)}, bf16[32,2048]{1,0:T(8,128)(2,1)S(1)}, u32[]{:S(2)}, u32[]{:S(2)}) collective-permute-start(bf16[32,2048]{1,0:T(8,128)(2,1)S(1)} %get-tuple-element.34.p_own), channel_id=1, source_target_pairs={{0,3},{1,0},{2,1},{3,2},{4,7},{5,4},{6,5},{7,6},{8,11},{9,8},{10,9... | collective-permute-start | bytes 393224 | tf_op jit(solution)/shard_map/ppermute | solution.py:25
  91.2 5.4 %collective-permute-start.16 = (bf16[32,512]{1,0:T(8,128)(2,1)S(1)}, bf16[32,512]{1,0:T(8,128)(2,1)S(1)}, u32[]{:S(2)}, u32[]{:S(2)}) collective-permute-start(bf16[32,512]{1,0:T(8,128)(2,1)S(1)} %get-tuple-element.37), channel_id=1, source_target_pairs={{0,1},{1,2},{2,3},{3,0},{4,5},{5,6},{6,7},{7,4},{8,9},{9,10},{10,1... | collective-permute-start | bytes 98312 | tf_op jit(solution)/shard_map/ppermute | solution.py:25
  92.4 5.4 %collective-permute-start.17 = (bf16[32,512]{1,0:T(8,128)(2,1)S(1)}, bf16[32,512]{1,0:T(8,128)(2,1)S(1)}, u32[]{:S(2)}, u32[]{:S(2)}) collective-permute-start(bf16[32,512]{1,0:T(8,128)(2,1)S(1)} %get-tuple-element.38), channel_id=1, source_target_pairs={{0,2},{1,3},{2,0},{3,1},{4,6},{5,7},{6,4},{7,5},{8,10},{9,11},{10,... | collective-permute-start | bytes 98312 | tf_op jit(solution)/shard_map/ppermute | solution.py:25
  93.5 4.3 %collective-permute-start.18 = (bf16[32,512]{1,0:T(8,128)(2,1)S(1)}, bf16[32,512]{1,0:T(8,128)(2,1)S(1)}, u32[]{:S(2)}, u32[]{:S(2)}) collective-permute-start(bf16[32,512]{1,0:T(8,128)(2,1)S(1)} %get-tuple-element.39), channel_id=1, source_target_pairs={{0,3},{1,0},{2,1},{3,2},{4,7},{5,4},{6,5},{7,6},{8,11},{9,8},{10,9... | collective-permute-start | bytes 98312 | tf_op jit(solution)/shard_map/ppermute | solution.py:25

commit v3 on v2

--- a/solution.py
+++ b/solution.py
@@ -97,19 +97,88 @@
 
 
 STRIDES = (24, 3, 8, 1)
-DIGIT, PLACE, OCCUPIED, PLAN = 0, 32, 40, 48
+SEATS = 5
+STAGES = len(STRIDES)
+DIGIT, SEAT, PLACE, OCCUPIED, OVER, PLAN = 0, 32, 64, 72, 80, 88
 AUX = 7
+
+
+def signed_residue(value):
+    residue = lax.rem(value, 8)
+    return jnp.where(residue > 4, residue - 8, residue)
+
+
+def plan_moves(former, plan, count):
+    groups = lax.axis_size("grp")
+    here = lax.axis_index("grp")
+    distances = [
+        lax.rem(lax.div(former[index], count) - here + groups, groups) for index in range(count)
+    ]
+    one = lambda test: test.astype(jnp.int32)
+    over = jnp.int32(0)
+    for far, near in ((1, 3), (0, 2)):
+        values = [signed_residue(distance) for distance in distances]
+        far_up = sum(one((value == 2) | (value == 3)) for value in values)
+        far_down = sum(one((value == -2) | (value == -3)) for value in values)
+        near_up = sum(one((value == 1) | (value == -2)) for value in values)
+        near_down = sum(one((value == -1) | (value == 2)) for value in values)
+        up, down = jnp.maximum(far_up, near_up), jnp.maximum(far_down, near_down)
+        seats = {(far, 1): 0, (far, -1): 0, (near, 1): 0, (near, -1): 0}
+        for index, value in enumerate(values):
+            free = value == 4
+            rise = free & (up <= down)
+            fall = free & (up > down)
+            up, down = up + one(rise), down + one(fall)
+            value = jnp.where(fall, -4, value)
+            distances[index] = lax.div(distances[index] - value + groups, 8)
+            triple = one(value >= 2) - one(value <= -2)
+            for stage, digit in ((far, triple), (near, value - 3 * triple)):
+                plan[DIGIT + stage * count + index] = digit
+                seat = jnp.where(digit == 1, seats[stage, 1], seats[stage, -1])
+                plan[SEAT + stage * count + index] = jnp.minimum(seat, SEATS - 1)
+                for sign in (1, -1):
+                    seats[stage, sign] = seats[stage, sign] + one(digit == sign)
+        for used in seats.values():
+            over = jnp.maximum(over, one(used > SEATS))
+    plan[OVER] = over
+
+
+def seat_rows(plan, stage, index, count):
+    seat = plan[SEAT + stage * count + index]
+    return pl.ds(pl.multiple_of(seat * WIDTH, WIDTH), WIDTH)
+
+
+def home_rows(index):
+    return pl.ds(index * WIDTH, WIDTH)
+
+
+def store_row(plan, stage, index, count, value, plus, minus, stay):
+    digit = plan[DIGIT + stage * count + index]
+    seat = seat_rows(plan, stage, index, count)
+    for sign, target, rows in ((1, plus, seat), (-1, minus, seat), (0, stay, home_rows(index))):
+
+        @pl.when(digit == sign)
+        def _(target=target, rows=rows):
+            target[rows, :] = value()
+
+
+def load_row(plan, stage, index, count, target, plus, minus, stay):
+    digit = plan[DIGIT + stage * count + index]
+    seat = seat_rows(plan, stage, index, count)
+    for sign, source, rows in ((1, plus, seat), (-1, minus, seat), (0, stay, home_rows(index))):
+
+        @pl.when(digit == sign)
+        def _(source=source, rows=rows):
+            target[home_rows(index), :] = source[rows, :]
 
 
 def pack_kernel(
     former, marks, occupied, held, state, shifts, tokens,
-    gathered, packed, plan,
+    gathered, plus, minus, stay, plan,
     slots, rows, sems, row_sems,
 ):
     count, heads = rows.shape[0], rows.shape[1]
     hist = held.shape[1]
-    groups = lax.axis_size("grp")
-    here = lax.axis_index("grp")
     sources = [lax.rem(former[index], count) for index in range(count)]
     row_copies = [
         pltpu.make_async_copy(state.at[source], rows.at[index], row_sems.at[index])
@@ -133,16 +202,7 @@
     ]
     for copy in copies:
         copy.start()
-    for index in range(count):
-        distance = lax.rem(former[index] // count - here + groups, groups)
-        low = lax.rem(distance, 8)
-        low = jnp.where(low > 4, low - 8, low)
-        high = lax.rem(lax.div(distance - low + groups, 8), 8)
-        high = jnp.where(high > 4, high - 8, high)
-        for far, near, value in ((0, 2, high), (1, 3, low)):
-            triple = jnp.where(value >= 2, 1, jnp.where(value <= -2, -1, 0))
-            plan[DIGIT + far * count + index] = triple
-            plan[DIGIT + near * count + index] = value - 3 * triple
+    plan_moves(former, plan, count)
     base = REB * hist
     for index in range(count):
         lines = tokens[index].astype(F32)
@@ -156,67 +216,98 @@
     for index in range(count):
         row_copies[index].wait()
         whole = rows[index]
-        wide = jnp.concatenate([whole[head] for head in range(heads)], axis=1)
-        packed[pl.ds(index * WIDTH, WIDTH), :] = wide.astype(BF16)
+        wide = jnp.concatenate([whole[head] for head in range(heads)], axis=1).astype(BF16)
+        store_row(plan, 0, index, count, lambda: wide, plus, minus, stay)
     for copy in copies:
         copy.wait()
 
 
-def digits_of(plan, stage, count):
-    return [plan[DIGIT + stage * count + index] for index in range(count)]
-
-
-def pick_rows(digits, plus, minus, stay, merged, count):
-    for index, digit in enumerate(digits):
-        rows = pl.ds(index * WIDTH, WIDTH)
-        for value, source in ((1, plus), (-1, minus), (0, stay)):
-
-            @pl.when(digit == value)
-            def _(rows=rows, source=source):
-                merged[rows, :] = source[rows, :]
-
-
-def pick_aux(digits, plus, minus, stay, count):
+def pack_all_kernel(former, state, packed, rows, row_sems):
+    count, heads = rows.shape[0], rows.shape[1]
+    row_copies = [
+        pltpu.make_async_copy(state.at[lax.rem(former[index], count)], rows.at[index], row_sems.at[index])
+        for index in range(count)
+    ]
+    for copy in row_copies:
+        copy.start()
+    for index in range(count):
+        row_copies[index].wait()
+        whole = rows[index]
+        wide = jnp.concatenate([whole[head] for head in range(heads)], axis=1)
+        packed[home_rows(index), :] = wide.astype(BF16)
+
+
+def pick_aux(plan, stage, plus, minus, stay, count):
     shape = (count, plus.shape[1])
     request = iota(shape, 0)
     take = jnp.zeros(shape, jnp.int32)
-    for index, digit in enumerate(digits):
-        take = jnp.where(request == index, digit, take)
+    for index in range(count):
+        take = jnp.where(request == index, plan[DIGIT + stage * count + index], take)
     take = jnp.concatenate([take] * (plus.shape[0] // count), axis=0)
     plus, minus, stay = (value.astype(F32) for value in (plus, minus, stay))
-    return jnp.where(take == 1, plus, jnp.where(take == -1, minus, stay))
-
-
-def merge_first_kernel(plan, plus, minus, stay, aux_plus, aux_minus, aux_stay, merged):
-    count = plus.shape[0] // WIDTH
-    digits = digits_of(plan, 0, count)
-    pick_rows(digits, plus, minus, stay, merged, count)
-    picked = pick_aux(digits, aux_plus[...], aux_minus[...], aux_stay[...], count)
-    merged[pl.ds(count * WIDTH, AUX * count), :] = picked.astype(BF16)
-
-
-def merge_kernel(stage, plan, plus, minus, stay, merged):
-    count = plus.shape[0] // (WIDTH + AUX)
-    digits = digits_of(plan, stage, count)
-    pick_rows(digits, plus, minus, stay, merged, count)
-    tail = pl.ds(count * WIDTH, AUX * count)
-    picked = pick_aux(digits, plus[tail, :], minus[tail, :], stay[tail, :], count)
-    merged[tail, :] = picked.astype(BF16)
-
-
-def project_kernel(
-    plan, own, by_one, by_two, by_three, gain, rates, far_r, far_k, far_v, far_left, far_up, w_right, base,
-    a_r, a_k, a_v, a_l, rebuilt, aux, hist_first, hist_low, time_last,
-    entries, w_r, w_k, w_v, w_left, w_up, sems,
-):
+    return jnp.where(take == 1, plus, jnp.where(take == -1, minus, stay)).astype(BF16)
+
+
+def merge_kernel(stage, count, separate, plan, *refs):
+    plus, minus, stay = refs[:3]
+    seated, home = SEATS * WIDTH, count * WIDTH
+    aux = AUX * count
+    if separate:
+        aux_values = [ref[...] for ref in refs[3:6]]
+        refs = refs[6:]
+    else:
+        aux_values = [plus[pl.ds(seated, aux), :], minus[pl.ds(seated, aux), :], stay[pl.ds(home, aux), :]]
+        refs = refs[3:]
+    picked = pick_aux(plan, stage, *aux_values, count)
+    if stage + 1 == STAGES:
+        (moved,) = refs
+        for index in range(count):
+            load_row(plan, stage, index, count, moved, plus, minus, stay)
+        moved[pl.ds(home, aux), :] = picked
+        return
+    next_plus, next_minus, next_stay, hold = refs
+    for index in range(count):
+        load_row(plan, stage, index, count, hold, plus, minus, stay)
+    for index in range(count):
+        rows = home_rows(index)
+        store_row(plan, stage + 1, index, count, lambda: hold[rows, :], next_plus, next_minus, next_stay)
+    next_plus[pl.ds(seated, aux), :] = picked
+    next_minus[pl.ds(seated, aux), :] = picked
+    next_stay[pl.ds(home, aux), :] = picked
+
+
+def merge_all_kernel(stage, count, plan, plus, minus, stay, moved):
+    home, aux = count * WIDTH, AUX * count
+    for index in range(count):
+        digit = plan[DIGIT + stage * count + index]
+        rows = home_rows(index)
+        for sign, source in ((1, plus), (-1, minus), (0, stay)):
+
+            @pl.when(digit == sign)
+            def _(source=source, rows=rows):
+                moved[rows, :] = source[rows, :]
+
+    tail = pl.ds(home, aux)
+    moved[tail, :] = pick_aux(plan, stage, plus[tail, :], minus[tail, :], stay[tail, :], count)
+
+
+def fetch_kernel(*refs):
+    count = (len(refs) - 1) // 2
     copies = [
-        pltpu.make_async_copy(far, near, sems.at[index])
-        for index, (far, near) in enumerate(
-            ((far_k, w_k), (far_v, w_v), (far_left, w_left), (far_r, w_r), (far_up, w_up))
-        )
+        pltpu.make_async_copy(far, near, refs[-1].at[index])
+        for index, (far, near) in enumerate(zip(refs[:count], refs[count:-1]))
     ]
     for copy in copies:
         copy.start()
+    for copy in copies:
+        copy.wait()
+
+
+def project_kernel(
+    plan, own, by_one, by_two, by_three, gain, rates, w_r, w_k, w_v, w_left, w_up, w_right, base,
+    a_r, a_k, a_v, a_l, rebuilt, aux, hist_first, hist_low, time_last,
+    entries,
+):
     ranks = 4
     feature = own.shape[1]
     hist_rows = REB * 32
@@ -246,13 +337,9 @@
         rate = rates[which : which + 1, :]
         return jnp.concatenate([current + change * rate, first * rate], axis=0).astype(BF16)
 
-    copies[0].wait()
     keys = dot(mixed(1), w_k[...])
-    copies[1].wait()
     values = dot(mixed(2), w_v[...])
-    copies[2].wait()
     low = dot(mixed(3), w_left[...], (1, 1))
-    copies[3].wait()
     received = dot(mixed(0)[hist_rows:], w_r[...])
     a_r[...] = received[:tokens]
     a_k[...] = keys[hist_rows:normal]
@@ -262,7 +349,6 @@
     hist_first[1] = keys[normal + count :]
     hist_first[2] = values[normal + count :]
     hist_low[...] = low[normal + count :]
-    copies[4].wait()
     up = dot((entries[pl.ds(normal + count, count), :] * rates[4:5, :]).astype(BF16), w_up[...])
     lanes = aux.shape[1]
     whole = up.shape[1] // lanes
@@ -462,12 +548,15 @@
     model = pre_attention_scaling.shape[0]
     tokens = count * steps
     row = lambda value: value.reshape(1, -1)
-    gathered, packed, plan = call(
+    home, seated, aux_rows = count * WIDTH, SEATS * WIDTH, AUX * count
+    gathered, plus, minus, stay, plan = call(
         pack_kernel,
         "pack",
         (
             out((REB * hist + tokens + 2 * count, feature), BF16),
-            out((count * WIDTH, channels), BF16),
+            out((seated, channels), BF16),
+            out((seated, channels), BF16),
+            out((home, channels), BF16),
             out((PLAN,), jnp.int32),
         ),
         [
@@ -485,19 +574,34 @@
             pltpu.SemaphoreType.DMA((REB,)),
             pltpu.SemaphoreType.DMA((count,)),
         ],
-        (VMEM_SPEC, VMEM_SPEC, SMEM_SPEC),
-    )
-    both = lambda value, stride: (rotate(value, "grp", -stride), rotate(value, "grp", stride))
-    plus, minus = both(packed, STRIDES[0])
+        (VMEM_SPEC, VMEM_SPEC, VMEM_SPEC, VMEM_SPEC, SMEM_SPEC),
+    )
+
+    def send(stage, up, down):
+        return rotate(up, "grp", -STRIDES[stage]), rotate(down, "grp", STRIDES[stage])
+
+    plus, minus = send(0, plus, minus)
     pieces = [gathered] + [rotate(gathered, "head", k) for k in (1, 2, 3)]
     base = row(fading_baseline_entries)
-    weights = (
+    far_weights = (
         acceptance_projection,
         address_projection,
         content_projection,
         fading_lowrank_left.T,
         feedforward_address_proj,
     )
+
+    def fetch(values, after):
+        values, _ = lax.optimization_barrier((values, after))
+        return call(
+            fetch_kernel,
+            "fetch",
+            tuple(out(value.shape, BF16) for value in values),
+            [(value, "any") for value in values],
+            [pltpu.SemaphoreType.DMA((len(values),))],
+        )
+
+    weights = fetch(far_weights, gathered)
     inner = fading_lowrank_left.shape[1]
     a_r, a_k, a_v, a_l, rebuilt, aux, hist_first, hist_low, time_last = call(
         project_kernel,
@@ -516,27 +620,52 @@
         [(plan, "smem")]
         + [(value, "vmem") for value in pieces]
         + [(row(pre_attention_scaling), "load"), (lag_blend_fractions, "load")]
-        + [(value, "any") for value in weights]
+        + [(value, "vmem") for value in weights]
         + [(fading_lowrank_right, "load"), (base, "load")],
-        [pltpu.VMEM((REB * hist + tokens + 2 * count, model), F32)]
-        + [pltpu.VMEM(value.shape, BF16) for value in weights]
-        + [pltpu.SemaphoreType.DMA((len(weights),))],
-    )
-    aux_plus, aux_minus = both(aux, STRIDES[0])
-    moved = call(
-        merge_first_kernel,
-        "merge0",
-        out((count * (WIDTH + AUX), channels), BF16),
-        [(plan, "smem")] + [(value, "vmem") for value in (plus, minus, packed, aux_plus, aux_minus, aux)],
-    )
-    for stage in range(1, len(STRIDES)):
-        plus, minus = both(moved, STRIDES[stage])
-        moved = call(
-            functools.partial(merge_kernel, stage),
+        [pltpu.VMEM((REB * hist + tokens + 2 * count, model), F32)],
+    )
+    arrived = (plus, minus, stay, *send(0, aux, aux), aux)
+    shape = lambda rows: out((rows + aux_rows, channels), BF16)
+    for stage in range(STAGES):
+        last = stage + 1 == STAGES
+        merged = call(
+            functools.partial(merge_kernel, stage, count, stage == 0),
             "merge",
-            out(moved.shape, BF16),
-            [(plan, "smem")] + [(value, "vmem") for value in (plus, minus, moved)],
+            shape(home) if last else (shape(seated), shape(seated), shape(home)),
+            [(plan, "smem")] + [(value, "vmem") for value in arrived],
+            [] if last else [pltpu.VMEM((home, channels), BF16)],
         )
+        if not last:
+            arrived = (*send(stage + 1, *merged[:2]), merged[2])
+
+    def move_all(moved, aux, plan, former, state):
+        packed = call(
+            pack_all_kernel,
+            "pack_all",
+            out((home, channels), BF16),
+            [(former, "scalars"), (state, "any")],
+            [pltpu.VMEM((count, heads, WIDTH, WIDTH), F32), pltpu.SemaphoreType.DMA((count,))],
+        )
+        moved = jnp.concatenate([packed, aux], axis=0)
+        for stage in range(STAGES):
+            moved = call(
+                functools.partial(merge_all_kernel, stage, count),
+                "merge_all",
+                shape(home),
+                [(plan, "smem")] + [(value, "load") for value in (*send(stage, moved, moved), moved)],
+            )
+        return moved
+
+    moved = lax.cond(
+        plan[OVER] > 0,
+        move_all,
+        lambda moved, *_: moved,
+        merged,
+        aux,
+        plan,
+        former_indices,
+        carried_memory_matrices,
+    )
     next_state, partial, up_first = call(
         recur_kernel,
         "recur",
@@ -552,6 +681,7 @@
         + [(attention_exit_projection, "vmem")],
     )
     partials = [partial] + [rotate(partial, "head", k) for k in (1, 2, 3)]
+    ffn_weights = fetch((feedforward_address_proj, feedforward_content_proj), partial)
     kept, to_one, to_two, to_three, channel_last = call(
         ffn_kernel,
         "ffn",
@@ -565,7 +695,7 @@
         [(plan, "smem")]
         + [(value, "vmem") for value in (*pieces, *partials, up_first)]
         + [(row(pre_feedforward_scaling), "load"), (lag_blend_fractions, "load")]
-        + [(feedforward_address_proj, "vmem"), (feedforward_content_proj, "vmem")],
+        + [(value, "vmem") for value in ffn_weights],
         [pltpu.VMEM((tokens, model), F32)],
     )
     arrived = [rotate(value, "head", k + 1) for k, value in enumerate((to_one, to_two, to_three))]

time: 100 us -> 87.4 us (0.87); the launches traced: 98.6 us -> 87.1 us
  waiting for transfers between devices: 42.4 us -> 29.1 us
  Pallas kernels: 16.4 us -> 20.5 us
  starting transfers between devices: 37.6 us -> 33.6 us
  local copies, waits for them, and re-layouts: 0.66 us -> 1.73 us
    ppermute x19, waiting for transfers between devices: 42.4 us -> 29.1 us  [rotate(): return lax.ppermute(value, axis, pairs)]
    pallas_call x8 -> x10, Pallas kernels: 16.4 us -> 20.5 us  [call(): pl.pallas_call(kernel, name=name, out_shape=out_shape, in_specs=[SPECS[pl...]
    ppermute x19, starting transfers between devices: 37.6 us -> 33.6 us  [rotate(): return lax.ppermute(value, axis, pairs)]
  transfers between devices with their start and end apart: 19 -> 19, of which waited for: 14 -> 10; matrix products, arithmetic and copies ran while one was open for 1% -> 1% of each run, Pallas kernels for 6% -> 10%
where the time goes in v3:
time: 87.4 us; the launch traced here: 87.1 us
  starting transfers between devices  33.6 us (38%)
  waiting for transfers between devices  29.1 us (33%)
  Pallas kernels  20.5 us (23%)
  local copies, waits for them, and re-layouts  1.73 us (2%)
  between operations  1.45 us (2%)
    ppermute x19, starting transfers between devices, rotate(): return lax.ppermute(value, axis, pairs)  33.6 us
    ppermute x19, waiting for transfers between devices, rotate(): return lax.ppermute(value, axis, pairs)  29.1 us
    pallas_call x10, Pallas kernels, call(): pl.pallas_call(kernel, name=name, out_shape=out_shape, in_specs=[SPECS[pl...  20.5 us
  transfers between devices with their start and end apart: 19, of which 10 were waited for; matrix products, arithmetic and copies ran while one was open for 1% of the time, Pallas kernels for 10%

profile of v3, /device:TPU:2, one launch (start us, length us, event | category | flops | bytes accessed | tf_op | source)
XLA Modules:
  0.0 87.1 jit_solution(11242323476228778324)
XLA Ops:
  0.6 3.1 %pack.1 = (bf16[112,512]{1,0:T(8,128)(2,1)S(1)}, bf16[320,256]{1,0:T(8,128)(2,1)S(1)}, bf16[320,256]{1,0:T(8,128)(2,1)S(1)}, bf16[512,256]{1,0:T(8,128)(2,1)S(1)}, s32[88]{0:T(128)S(1)}) custom-call(s32[8]{0:T(128)} %former.1, s32[8]{0:T(128)} %marks.1, s32[8]{0:T(128)} %occupied.1, bf16[8,32,512]{2,1,0:T(8,128)(2,1)} %held.1, f32[8,4,64,64]{3,2,1,0:T(8,128)} %state.1, ...), custom_call_target="tpu_custom_call" | custom-call | tf_op jit(solution)/shard_map/pack/pallas_call | solution.py:41
  3.7 6.8 %collective-permute-start.11 = (bf16[320,256]{1,0:T(8,128)(2,1)S(1)}, bf16[320,256]{1,0:T(8,128)(2,1)S(1)}, u32[]{:S(2)}, u32[]{:S(2)}) collective-permute-start(bf16[320,256]{1,0:T(8,128)(2,1)S(1)} %get-tuple-element.66), channel_id=1, source_target_pairs={{0,160},{4,164},{8,168},{12,172},{16,176},{20,180},{24,184},{28,18... | collective-permute-start | bytes 491528 | tf_op jit(solution)/shard_map/ppermute | solution.py:25
  10.5 0.0 collective-permute-start.12
  10.5 0.5 collective-permute-start.10
  11.1 1.5 %collective-permute-start.8 = (bf16[112,512]{1,0:T(8,128)(2,1)S(1)}, bf16[112,512]{1,0:T(8,128)(2,1)S(1)}, u32[]{:S(2)}, u32[]{:S(2)}) collective-permute-start(bf16[112,512]{1,0:T(8,128)(2,1)S(1)} %get-tuple-element.65.own), channel_id=1, source_target_pairs={{0,1},{1,2},{2,3},{3,0},{4,5},{5,6},{6,7},{7,4},{8,9},{9,10},{10,1... | collective-permute-start | bytes 344072 | tf_op jit(solution)/shard_map/ppermute | solution.py:25
  12.6 3.3 %collective-permute-start.9 = (bf16[112,512]{1,0:T(8,128)(2,1)S(1)}, bf16[112,512]{1,0:T(8,128)(2,1)S(1)}, u32[]{:S(2)}, u32[]{:S(2)}) collective-permute-start(bf16[112,512]{1,0:T(8,128)(2,1)S(1)} %get-tuple-element.65.own), channel_id=1, source_target_pairs={{0,2},{1,3},{2,0},{3,1},{4,6},{5,7},{6,4},{7,5},{8,10},{9,11},{10,... | collective-permute-start | bytes 344072 | tf_op jit(solution)/shard_map/ppermute | solution.py:25
  15.9 3.1 %fetch.2 = (bf16[2048,256]{1,0:T(8,128)(2,1)S(1)}, bf16[2048,256]{1,0:T(8,128)(2,1)S(1)}, bf16[2048,256]{1,0:T(8,128)(2,1)S(1)}, bf16[64,2048]{1,0:T(8,128)(2,1)S(1)}, bf16[2048,896]{1,0:T(8,128)(2,1)S(1)}) custom-call(bf16[2048,256]{1,0:T(8,128)(2,1)} %refs_0_, bf16[2048,256]{1,0:T(8,128)(2,1)} %refs_1_, bf16[2048,256]{1,0:T(8,128)(2,1)} %refs_2_, ...), custom_call_target="tpu_custom_call" | custom-call | tf_op jit(solution)/shard_map/fetch/pallas_call | solution.py:41
  19.0 0.0 collective-permute-done.10.by_three
  19.0 0.0 collective-permute-done.8.by_one
  19.1 0.0 collective-permute-done.9.by_two
  19.1 2.7 %project.1 = (f32[32,256]{1,0:T(8,128)S(1)}, f32[32,256]{1,0:T(8,128)S(1)}, f32[32,256]{1,0:T(8,128)S(1)}, f32[32,64]{1,0:T(8,128)S(1)}, f32[2,64,256]{2,1,0:T(8...) custom-call(s32[88]{0:T(128)S(1)} %get-tuple-element.64.plan, ...), custom_call_target="tpu_custom_call" | custom-call | tf_op jit(solution)/shard_map/project/pallas_call | solution.py:41
  21.8 5.1 %collective-permute-start.13 = (bf16[56,256]{1,0:T(8,128)(2,1)S(1)}, bf16[56,256]{1,0:T(8,128)(2,1)S(1)}, u32[]{:S(2)}, u32[]{:S(2)}) collective-permute-start(bf16[56,256]{1,0:T(8,128)(2,1)S(1)} %get-tuple-element.79.refs_5_), channel_id=1, source_target_pairs={{0,160},{4,164},{8,168},{12,172},{16,176},{20,180},{24,184},{28,18... | collective-permute-start | bytes 86024 | tf_op jit(solution)/shard_map/ppermute | solution.py:25
  26.9 0.0 collective-permute-start.14
  26.9 1.6 %collective-permute-done.13.refs_3_ = bf16[56,256]{1,0:T(8,128)(2,1)S(1)} collective-permute-done((bf16[56,256]{1,0:T(8,128)(2,1)S(1)}, bf16[56,256]{1,0:T(8,128)(2,1)S(1)}, u32[]{:S(2)}, u32[]{:S(2)}) %collective-permute-start.13) | collective-permute-done | bytes 28704 | tf_op jit(solution)/shard_map/ppermute | solution.py:25
  28.4 5.4 %collective-permute-done.14.refs_4_ = bf16[56,256]{1,0:T(8,128)(2,1)S(1)} collective-permute-done((bf16[56,256]{1,0:T(8,128)(2,1)S(1)}, bf16[56,256]{1,0:T(8,128)(2,1)S(1)}, u32[]{:S(2)}, u32[]{:S(2)}) %collective-permute-start.14) | collective-permute-done | bytes 28704 | tf_op jit(solution)/shard_map/ppermute | solution.py:25
  33.8 0.0 collective-permute-done.11.refs_0_
  33.8 0.0 collective-permute-done.12.refs_1_
  33.8 0.8 merge.4
  34.6 0.1 collective-permute-start.15
  34.7 1.7 %collective-permute-start.16 = (bf16[376,256]{1,0:T(8,128)(2,1)S(1)}, bf16[376,256]{1,0:T(8,128)(2,1)S(1)}, u32[]{:S(2)}, u32[]{:S(2)}) collective-permute-start(bf16[376,256]{1,0:T(8,128)(2,1)S(1)} %get-tuple-element.81), channel_id=1, source_target_pairs={{0,12},{4,16},{8,20},{12,24},{16,28},{20,32},{24,36},{28,40},{32,4... | collective-permute-start | bytes 577544 | tf_op jit(solution)/shard_map/ppermute | solution.py:25
  36.5 5.4 %collective-permute-done.15.refs_0_ = bf16[376,256]{1,0:T(8,128)(2,1)S(1)} collective-permute-done((bf16[376,256]{1,0:T(8,128)(2,1)S(1)}, bf16[376,256]{1,0:T(8,128)(2,1)S(1)}, u32[]{:S(2)}, u32[]{:S(2)}) %collective-permute-start.15) | collective-permute-done | bytes 192544 | tf_op jit(solution)/shard_map/ppermute | solution.py:25
  41.8 2.1 %collective-permute-done.16.refs_1_ = bf16[376,256]{1,0:T(8,128)(2,1)S(1)} collective-permute-done((bf16[376,256]{1,0:T(8,128)(2,1)S(1)}, bf16[376,256]{1,0:T(8,128)(2,1)S(1)}, u32[]{:S(2)}, u32[]{:S(2)}) %collective-permute-start.16) | collective-permute-done | bytes 192544 | tf_op jit(solution)/shard_map/ppermute | solution.py:25
  43.9 0.8 merge.5
  44.8 0.1 collective-permute-start.17
  44.8 2.0 %collective-permute-start.18 = (bf16[376,256]{1,0:T(8,128)(2,1)S(1)}, bf16[376,256]{1,0:T(8,128)(2,1)S(1)}, u32[]{:S(2)}, u32[]{:S(2)}) collective-permute-start(bf16[376,256]{1,0:T(8,128)(2,1)S(1)} %get-tuple-element.84), channel_id=1, source_target_pairs={{0,32},{4,36},{8,40},{12,44},{16,48},{20,52},{24,56},{28,60},{32,6... | collective-permute-start | bytes 577544 | tf_op jit(solution)/shard_map/ppermute | solution.py:25
  46.9 4.5 %collective-permute-done.17.refs_0_ = bf16[376,256]{1,0:T(8,128)(2,1)S(1)} collective-permute-done((bf16[376,256]{1,0:T(8,128)(2,1)S(1)}, bf16[376,256]{1,0:T(8,128)(2,1)S(1)}, u32[]{:S(2)}, u32[]{:S(2)}) %collective-permute-start.17) | collective-permute-done | bytes 192544 | tf_op jit(solution)/shard_map/ppermute | solution.py:25
  51.3 1.3 %collective-permute-done.18.refs_1_ = bf16[376,256]{1,0:T(8,128)(2,1)S(1)} collective-permute-done((bf16[376,256]{1,0:T(8,128)(2,1)S(1)}, bf16[376,256]{1,0:T(8,128)(2,1)S(1)}, u32[]{:S(2)}, u32[]{:S(2)}) %collective-permute-start.18) | collective-permute-done | bytes 192544 | tf_op jit(solution)/shard_map/ppermute | solution.py:25
  52.6 0.8 merge.6
  53.5 0.1 collective-permute-start.19
  53.6 1.3 %collective-permute-start.20 = (bf16[376,256]{1,0:T(8,128)(2,1)S(1)}, bf16[376,256]{1,0:T(8,128)(2,1)S(1)}, u32[]{:S(2)}, u32[]{:S(2)}) collective-permute-start(bf16[376,256]{1,0:T(8,128)(2,1)S(1)} %get-tuple-element.87), channel_id=1, source_target_pairs={{0,4},{4,8},{8,12},{12,16},{16,20},{20,24},{24,28},{28,32},{32,36}... | collective-permute-start | bytes 577544 | tf_op jit(solution)/shard_map/ppermute | solution.py:25
  54.8 0.6 slice.3
  56.1 0.6 collective-permute-done.19.refs_0_
  56.7 5.5 %collective-permute-done.20.refs_1_ = bf16[376,256]{1,0:T(8,128)(2,1)S(1)} collective-permute-done((bf16[376,256]{1,0:T(8,128)(2,1)S(1)}, bf16[376,256]{1,0:T(8,128)(2,1)S(1)}, u32[]{:S(2)}, u32[]{:S(2)}) %collective-permute-start.20) | collective-permute-done | bytes 192544 | tf_op jit(solution)/shard_map/ppermute | solution.py:25
  62.2 0.0 copy-start.3
  62.2 0.7 merge.7
  62.9 0.0 copy-start.13
  62.9 0.5 copy-done.3
  63.4 2.6 %recur.1 = (f32[8,4,64,64]{3,2,1,0:T(8,128)}, bf16[32,2048]{1,0:T(8,128)(2,1)S(1)}, f32[8,896]{1,0:T(8,128)S(1)}) custom-call(s32[88]{0:T(128)S(1)} %get-tuple-element.64.plan, bf16[568,256]{1,0:T(8,128)(2,1)S(1)} %get-tuple-element.112.moved, f32[3,8,256]{2,1,0:T(8,128)S(1)} %get-tuple-element.89.hist_first, f32[8,64]{1,0:T(8,128)S(1)} %get-tuple-element.90.hist_low, ...), custom_call_target="tpu_custom_call" | custom-call | tf_op jit(solution)/shard_map/recur/pallas_call | solution.py:41
  66.1 1.4 %collective-permute-start.21 = (bf16[32,2048]{1,0:T(8,128)(2,1)S(1)}, bf16[32,2048]{1,0:T(8,128)(2,1)S(1)}, u32[]{:S(2)}, u32[]{:S(2)}) collective-permute-start(bf16[32,2048]{1,0:T(8,128)(2,1)S(1)} %get-tuple-element.96.p_own), channel_id=1, source_target_pairs={{0,1},{1,2},{2,3},{3,0},{4,5},{5,6},{6,7},{7,4},{8,9},{9,10},{10,1... | collective-permute-start | bytes 393224 | tf_op jit(solution)/shard_map/ppermute | solution.py:25
  67.5 3.9 %collective-permute-start.22 = (bf16[32,2048]{1,0:T(8,128)(2,1)S(1)}, bf16[32,2048]{1,0:T(8,128)(2,1)S(1)}, u32[]{:S(2)}, u32[]{:S(2)}) collective-permute-start(bf16[32,2048]{1,0:T(8,128)(2,1)S(1)} %get-tuple-element.96.p_own), channel_id=1, source_target_pairs={{0,2},{1,3},{2,0},{3,1},{4,6},{5,7},{6,4},{7,5},{8,10},{9,11},{10,... | collective-permute-start | bytes 393224 | tf_op jit(solution)/shard_map/ppermute | solution.py:25
  71.3 0.4 collective-permute-start.23
  71.8 0.0 copy-done.13
  71.8 0.1 iota_compare_fusion
  71.9 3.2 %fetch.3 = (bf16[2048,896]{1,0:T(8,128)(2,1)S(1)}, bf16[896,2048]{1,0:T(8,128)(2,1)S(1)}) custom-call(bf16[2048,896]{1,0:T(8,128)(2,1)} %refs_0_.1, bf16[896,2048]{1,0:T(8,128)(2,1)} %refs_1_.1), custom_call_target="tpu_custom_call" | custom-call | tf_op jit(solution)/shard_map/fetch/pallas_call | solution.py:41
  75.1 0.0 collective-permute-done.21.p_one
  75.1 0.0 collective-permute-done.22.p_two
  75.1 1.2 %collective-permute-done.23.p_three = bf16[32,2048]{1,0:T(8,128)(2,1)S(1)} collective-permute-done((bf16[32,2048]{1,0:T(8,128)(2,1)S(1)}, bf16[32,2048]{1,0:T(8,128)(2,1)S(1)}, u32[]{:S(2)}, u32[]{:S(2)}) %collective-permute-start.23) | collective-permute-done | bytes 131104 | tf_op jit(solution)/shard_map/ppermute | solution.py:25
  76.3 2.6 %ffn.1 = (f32[32,512]{1,0:T(8,128)S(1)}, bf16[32,512]{1,0:T(8,128)(2,1)S(1)}, bf16[32,512]{1,0:T(8,128)(2,1)S(1)}, bf16[32,512]{1,0:T(8,128)(2,1)S(1)}, f32[8,512]{1,0:T(8,128)S(1)}) custom-call(s32[88]{0:T(128)S(1)} %get-tuple-element.64.plan, bf16[112,512]{1,0:T(8,128)(2,1)S(1)} %get-tuple-element.65.own, ...), custom_call_target="tpu_custom_call" | custom-call | tf_op jit(solution)/shard_map/ffn/pallas_call | solution.py:41
  78.9 0.4 collective-permute-start.24
  79.3 3.2 %collective-permute-start.25 = (bf16[32,512]{1,0:T(8,128)(2,1)S(1)}, bf16[32,512]{1,0:T(8,128)(2,1)S(1)}, u32[]{:S(2)}, u32[]{:S(2)}) collective-permute-start(bf16[32,512]{1,0:T(8,128)(2,1)S(1)} %get-tuple-element.104), channel_id=1, source_target_pairs={{0,2},{1,3},{2,0},{3,1},{4,6},{5,7},{6,4},{7,5},{8,10},{9,11},{10,... | collective-permute-start | bytes 98312 | tf_op jit(solution)/shard_map/ppermute | solution.py:25
  82.5 1.7 %collective-permute-start.26 = (bf16[32,512]{1,0:T(8,128)(2,1)S(1)}, bf16[32,512]{1,0:T(8,128)(2,1)S(1)}, u32[]{:S(2)}, u32[]{:S(2)}) collective-permute-start(bf16[32,512]{1,0:T(8,128)(2,1)S(1)} %get-tuple-element.105), channel_id=1, source_target_pairs={{0,3},{1,0},{2,1},{3,2},{4,7},{5,4},{6,5},{7,6},{8,11},{9,8},{10,9... | collective-permute-start | bytes 98312 | tf_op jit(solution)/shard_map/ppermute | solution.py:25
  84.2 0.6 copy.25
  84.8 0.0 collective-permute-done.24
  84.8 0.0 collective-permute-done.25
  84.8 1.5 %collective-permute-done.26 = bf16[32,512]{1,0:T(8,128)(2,1)S(1)} collective-permute-done((bf16[32,512]{1,0:T(8,128)(2,1)S(1)}, bf16[32,512]{1,0:T(8,128)(2,1)S(1)}, u32[]{:S(2)}, u32[]{:S(2)}) %collective-permute-start.26) | collective-permute-done | bytes 32800 | tf_op jit(solution)/shard_map/ppermute | solution.py:25
  86.4 0.7 bitcast_select_fusion
  (3 shorter events, 0.0 us)
Async XLA Ops:
  3.7 30.1 %collective-permute-start.11 = (bf16[320,256]{1,0:T(8,128)(2,1)S(1)}, bf16[320,256]{1,0:T(8,128)(2,1)S(1)}, u32[]{:S(2)}, u32[]{:S(2)}) collective-permute-start(bf16[320,256]{1,0:T(8,128)(2,1)S(1)} %get-tuple-element.66), channel_id=1, source_target_pairs={{0,160},{4,164},{8,168},{12,172},{16,176},{20,180},{24,184},{28,18... | collective-permute-start | bytes 491528 | tf_op jit(solution)/shard_map/ppermute | solution.py:25
  10.5 23.3 %collective-permute-start.12 = (bf16[320,256]{1,0:T(8,128)(2,1)S(1)}, bf16[320,256]{1,0:T(8,128)(2,1)S(1)}, u32[]{:S(2)}, u32[]{:S(2)}) collective-permute-start(bf16[320,256]{1,0:T(8,128)(2,1)S(1)} %get-tuple-element.67), channel_id=1, source_target_pairs={{0,96},{4,100},{8,104},{12,108},{16,112},{20,116},{24,120},{28,124... | collective-permute-start | bytes 491528 | tf_op jit(solution)/shard_map/ppermute | solution.py:25
  10.5 8.5 %collective-permute-start.10 = (bf16[112,512]{1,0:T(8,128)(2,1)S(1)}, bf16[112,512]{1,0:T(8,128)(2,1)S(1)}, u32[]{:S(2)}, u32[]{:S(2)}) collective-permute-start(bf16[112,512]{1,0:T(8,128)(2,1)S(1)} %get-tuple-element.65.own), channel_id=1, source_target_pairs={{0,3},{1,0},{2,1},{3,2},{4,7},{5,4},{6,5},{7,6},{8,11},{9,8},{10,9... | collective-permute-start | bytes 344072 | tf_op jit(solution)/shard_map/ppermute | solution.py:25
  11.1 8.0 %collective-permute-start.8 = (bf16[112,512]{1,0:T(8,128)(2,1)S(1)}, bf16[112,512]{1,0:T(8,128)(2,1)S(1)}, u32[]{:S(2)}, u32[]{:S(2)}) collective-permute-start(bf16[112,512]{1,0:T(8,128)(2,1)S(1)} %get-tuple-element.65.own), channel_id=1, source_target_pairs={{0,1},{1,2},{2,3},{3,0},{4,5},{5,6},{6,7},{7,4},{8,9},{9,10},{10,1... | collective-permute-start | bytes 344072 | tf_op jit(solution)/shard_map/ppermute | solution.py:25
  12.6 6.5 %collective-permute-start.9 = (bf16[112,512]{1,0:T(8,128)(2,1)S(1)}, bf16[112,512]{1,0:T(8,128)(2,1)S(1)}, u32[]{:S(2)}, u32[]{:S(2)}) collective-permute-start(bf16[112,512]{1,0:T(8,128)(2,1)S(1)} %get-tuple-element.65.own), channel_id=1, source_target_pairs={{0,2},{1,3},{2,0},{3,1},{4,6},{5,7},{6,4},{7,5},{8,10},{9,11},{10,... | collective-permute-start | bytes 344072 | tf_op jit(solution)/shard_map/ppermute | solution.py:25
  21.8 6.7 %collective-permute-start.13 = (bf16[56,256]{1,0:T(8,128)(2,1)S(1)}, bf16[56,256]{1,0:T(8,128)(2,1)S(1)}, u32[]{:S(2)}, u32[]{:S(2)}) collective-permute-start(bf16[56,256]{1,0:T(8,128)(2,1)S(1)} %get-tuple-element.79.refs_5_), channel_id=1, source_target_pairs={{0,160},{4,164},{8,168},{12,172},{16,176},{20,180},{24,184},{28,18... | collective-permute-start | bytes 86024 | tf_op jit(solution)/shard_map/ppermute | solution.py:25
  26.9 6.9 %collective-permute-start.14 = (bf16[56,256]{1,0:T(8,128)(2,1)S(1)}, bf16[56,256]{1,0:T(8,128)(2,1)S(1)}, u32[]{:S(2)}, u32[]{:S(2)}) collective-permute-start(bf16[56,256]{1,0:T(8,128)(2,1)S(1)} %get-tuple-element.79.refs_5_), channel_id=1, source_target_pairs={{0,96},{4,100},{8,104},{12,108},{16,112},{20,116},{24,120},{28,124... | collective-permute-start | bytes 86024 | tf_op jit(solution)/shard_map/ppermute | solution.py:25
  34.6 7.2 %collective-permute-start.15 = (bf16[376,256]{1,0:T(8,128)(2,1)S(1)}, bf16[376,256]{1,0:T(8,128)(2,1)S(1)}, u32[]{:S(2)}, u32[]{:S(2)}) collective-permute-start(bf16[376,256]{1,0:T(8,128)(2,1)S(1)} %get-tuple-element.80), channel_id=1, source_target_pairs={{0,244},{4,248},{8,252},{12,0},{16,4},{20,8},{24,12},{28,16},{32,2... | collective-permute-start | bytes 577544 | tf_op jit(solution)/shard_map/ppermute | solution.py:25
  34.7 9.2 %collective-permute-start.16 = (bf16[376,256]{1,0:T(8,128)(2,1)S(1)}, bf16[376,256]{1,0:T(8,128)(2,1)S(1)}, u32[]{:S(2)}, u32[]{:S(2)}) collective-permute-start(bf16[376,256]{1,0:T(8,128)(2,1)S(1)} %get-tuple-element.81), channel_id=1, source_target_pairs={{0,12},{4,16},{8,20},{12,24},{16,28},{20,32},{24,36},{28,40},{32,4... | collective-permute-start | bytes 577544 | tf_op jit(solution)/shard_map/ppermute | solution.py:25
  44.8 6.6 %collective-permute-start.17 = (bf16[376,256]{1,0:T(8,128)(2,1)S(1)}, bf16[376,256]{1,0:T(8,128)(2,1)S(1)}, u32[]{:S(2)}, u32[]{:S(2)}) collective-permute-start(bf16[376,256]{1,0:T(8,128)(2,1)S(1)} %get-tuple-element.83), channel_id=1, source_target_pairs={{0,224},{4,228},{8,232},{12,236},{16,240},{20,244},{24,248},{28,25... | collective-permute-start | bytes 577544 | tf_op jit(solution)/shard_map/ppermute | solution.py:25
  44.8 7.8 %collective-permute-start.18 = (bf16[376,256]{1,0:T(8,128)(2,1)S(1)}, bf16[376,256]{1,0:T(8,128)(2,1)S(1)}, u32[]{:S(2)}, u32[]{:S(2)}) collective-permute-start(bf16[376,256]{1,0:T(8,128)(2,1)S(1)} %get-tuple-element.84), channel_id=1, source_target_pairs={{0,32},{4,36},{8,40},{12,44},{16,48},{20,52},{24,56},{28,60},{32,6... | collective-permute-start | bytes 577544 | tf_op jit(solution)/shard_map/ppermute | solution.py:25
  53.5 3.2 %collective-permute-start.19 = (bf16[376,256]{1,0:T(8,128)(2,1)S(1)}, bf16[376,256]{1,0:T(8,128)(2,1)S(1)}, u32[]{:S(2)}, u32[]{:S(2)}) collective-permute-start(bf16[376,256]{1,0:T(8,128)(2,1)S(1)} %get-tuple-element.86), channel_id=1, source_target_pairs={{0,252},{4,0},{8,4},{12,8},{16,12},{20,16},{24,20},{28,24},{32,28}... | collective-permute-start | bytes 577544 | tf_op jit(solution)/shard_map/ppermute | solution.py:25
  53.6 8.6 %collective-permute-start.20 = (bf16[376,256]{1,0:T(8,128)(2,1)S(1)}, bf16[376,256]{1,0:T(8,128)(2,1)S(1)}, u32[]{:S(2)}, u32[]{:S(2)}) collective-permute-start(bf16[376,256]{1,0:T(8,128)(2,1)S(1)} %get-tuple-element.87), channel_id=1, source_target_pairs={{0,4},{4,8},{8,12},{12,16},{16,20},{20,24},{24,28},{28,32},{32,36}... | collective-permute-start | bytes 577544 | tf_op jit(solution)/shard_map/ppermute | solution.py:25
  62.2 1.2 %copy-start.3 = (bf16[256,2048]{1,0:T(8,128)(2,1)S(1)}, bf16[256,2048]{1,0:T(8,128)(2,1)}, u32[]{:S(2)}) copy-start(bf16[256,2048]{1,0:T(8,128)(2,1)} %w_out.1) | copy-start | bytes 3145732
  62.9 8.9 %copy-start.13 = (s32[8]{0:T(128)S(1)}, s32[8]{0:T(128)}, u32[]{:S(2)}) copy-start(s32[8]{0:T(128)} %occupied.1) | copy-start | bytes 100
  66.1 9.0 %collective-permute-start.21 = (bf16[32,2048]{1,0:T(8,128)(2,1)S(1)}, bf16[32,2048]{1,0:T(8,128)(2,1)S(1)}, u32[]{:S(2)}, u32[]{:S(2)}) collective-permute-start(bf16[32,2048]{1,0:T(8,128)(2,1)S(1)} %get-tuple-element.96.p_own), channel_id=1, source_target_pairs={{0,1},{1,2},{2,3},{3,0},{4,5},{5,6},{6,7},{7,4},{8,9},{9,10},{10,1... | collective-permute-start | bytes 393224 | tf_op jit(solution)/shard_map/ppermute | solution.py:25
  67.5 7.6 %collective-permute-start.22 = (bf16[32,2048]{1,0:T(8,128)(2,1)S(1)}, bf16[32,2048]{1,0:T(8,128)(2,1)S(1)}, u32[]{:S(2)}, u32[]{:S(2)}) collective-permute-start(bf16[32,2048]{1,0:T(8,128)(2,1)S(1)} %get-tuple-element.96.p_own), channel_id=1, source_target_pairs={{0,2},{1,3},{2,0},{3,1},{4,6},{5,7},{6,4},{7,5},{8,10},{9,11},{10,... | collective-permute-start | bytes 393224 | tf_op jit(solution)/shard_map/ppermute | solution.py:25
  71.3 5.0 %collective-permute-start.23 = (bf16[32,2048]{1,0:T(8,128)(2,1)S(1)}, bf16[32,2048]{1,0:T(8,128)(2,1)S(1)}, u32[]{:S(2)}, u32[]{:S(2)}) collective-permute-start(bf16[32,2048]{1,0:T(8,128)(2,1)S(1)} %get-tuple-element.96.p_own), channel_id=1, source_target_pairs={{0,3},{1,0},{2,1},{3,2},{4,7},{5,4},{6,5},{7,6},{8,11},{9,8},{10,9... | collective-permute-start | bytes 393224 | tf_op jit(solution)/shard_map/ppermute | solution.py:25
  78.9 5.9 %collective-permute-start.24 = (bf16[32,512]{1,0:T(8,128)(2,1)S(1)}, bf16[32,512]{1,0:T(8,128)(2,1)S(1)}, u32[]{:S(2)}, u32[]{:S(2)}) collective-permute-start(bf16[32,512]{1,0:T(8,128)(2,1)S(1)} %get-tuple-element.103), channel_id=1, source_target_pairs={{0,1},{1,2},{2,3},{3,0},{4,5},{5,6},{6,7},{7,4},{8,9},{9,10},{10,1... | collective-permute-start | bytes 98312 | tf_op jit(solution)/shard_map/ppermute | solution.py:25
  79.3 5.5 %collective-permute-start.25 = (bf16[32,512]{1,0:T(8,128)(2,1)S(1)}, bf16[32,512]{1,0:T(8,128)(2,1)S(1)}, u32[]{:S(2)}, u32[]{:S(2)}) collective-permute-start(bf16[32,512]{1,0:T(8,128)(2,1)S(1)} %get-tuple-element.104), channel_id=1, source_target_pairs={{0,2},{1,3},{2,0},{3,1},{4,6},{5,7},{6,4},{7,5},{8,10},{9,11},{10,... | collective-permute-start | bytes 98312 | tf_op jit(solution)/shard_map/ppermute | solution.py:25
  82.5 3.9 %collective-permute-start.26 = (bf16[32,512]{1,0:T(8,128)(2,1)S(1)}, bf16[32,512]{1,0:T(8,128)(2,1)S(1)}, u32[]{:S(2)}, u32[]{:S(2)}) collective-permute-start(bf16[32,512]{1,0:T(8,128)(2,1)S(1)} %get-tuple-element.105), channel_id=1, source_target_pairs={{0,3},{1,0},{2,1},{3,2},{4,7},{5,4},{6,5},{7,6},{8,11},{9,8},{10,9... | collective-permute-start | bytes 98312 | tf_op jit(solution)/shard_map/ppermute | solution.py:25

commit v4 on v3

--- a/solution.py
+++ b/solution.py
@@ -37,7 +37,7 @@
 PLACES = {"vmem": on_chip, "load": off_chip, "any": off_chip, "scalars": off_chip}
 
 
-def call(kernel, name, out_shape, operands, scratch=(), out_specs=None):
+def call(kernel, name, out_shape, operands, scratch=(), out_specs=None, cost=None):
     return pl.pallas_call(
         kernel,
         name=name,
@@ -45,6 +45,7 @@
         in_specs=[SPECS[place] for _, place in operands],
         out_specs=jax.tree.map(lambda _: VMEM_SPEC, out_shape) if out_specs is None else out_specs,
         scratch_shapes=list(scratch),
+        cost_estimate=cost,
         compiler_params=pltpu.CompilerParams(vmem_limit_bytes=VMEM_LIMIT),
     )(*[PLACES.get(place, lambda value: value)(array) for array, place in operands])
 
@@ -173,9 +174,9 @@
 
 
 def pack_kernel(
-    former, marks, occupied, held, state, shifts, tokens,
-    gathered, plus, minus, stay, plan,
-    slots, rows, sems, row_sems,
+    former, marks, occupied, held, state, shifts, tokens, far_r, far_k, far_v, far_left,
+    gathered, plus, minus, stay, w_r, w_k, w_v, w_left, plan,
+    slots, rows, sems, row_sems, weight_sems,
 ):
     count, heads = rows.shape[0], rows.shape[1]
     hist = held.shape[1]
@@ -185,6 +186,13 @@
         for index, source in enumerate(sources)
     ]
     for copy in row_copies:
+        copy.start()
+    far = (far_r, far_k, far_v, far_left)
+    weight_copies = [
+        pltpu.make_async_copy(source, target, weight_sems.at[index])
+        for index, (source, target) in enumerate(zip(far, (w_r, w_k, w_v, w_left)))
+    ]
+    for copy in weight_copies:
         copy.start()
     rank = jnp.int32(0)
     chosen = [jnp.int32(0)] * REB
@@ -218,7 +226,7 @@
         whole = rows[index]
         wide = jnp.concatenate([whole[head] for head in range(heads)], axis=1).astype(BF16)
         store_row(plan, 0, index, count, lambda: wide, plus, minus, stay)
-    for copy in copies:
+    for copy in copies + weight_copies:
         copy.wait()
 
 
@@ -304,10 +312,12 @@
 
 
 def project_kernel(
-    plan, own, by_one, by_two, by_three, gain, rates, w_r, w_k, w_v, w_left, w_up, w_right, base,
+    plan, own, by_one, by_two, by_three, gain, rates, w_r, w_k, w_v, w_left, far_up, w_right, base,
     a_r, a_k, a_v, a_l, rebuilt, aux, hist_first, hist_low, time_last,
-    entries,
+    entries, w_up, up_sem,
 ):
+    fetch_up = pltpu.make_async_copy(far_up, w_up, up_sem.at[0])
+    fetch_up.start()
     ranks = 4
     feature = own.shape[1]
     hist_rows = REB * 32
@@ -349,14 +359,8 @@
     hist_first[1] = keys[normal + count :]
     hist_first[2] = values[normal + count :]
     hist_low[...] = low[normal + count :]
-    up = dot((entries[pl.ds(normal + count, count), :] * rates[4:5, :]).astype(BF16), w_up[...])
-    lanes = aux.shape[1]
-    whole = up.shape[1] // lanes
-    left = jnp.concatenate([low[normal : normal + count], jnp.zeros((count, lanes // 2 - low.shape[1]), F32)], axis=1)
     moving = [received[tokens : tokens + count], keys[normal : normal + count], values[normal : normal + count]]
-    moving += [up[:, part * lanes : (part + 1) * lanes] for part in range(whole)]
-    moving += [jnp.concatenate([left, up[:, whole * lanes :]], axis=1)]
-    aux[...] = jnp.concatenate(moving, axis=0).astype(BF16)
+    low_moving = low[normal : normal + count]
     keys, values, low = keys[:hist_rows], values[:hist_rows], low[:hist_rows]
     rank = jnp.tanh(low).astype(BF16)
     decay = jnp.exp(-jnp.exp(base[...] + dot(rank, w_right[...])))
@@ -380,6 +384,14 @@
         for which in range(1, values.shape[1] // WIDTH):
             packed = jnp.where(lane == which, outer[which * WIDTH : (which + 1) * WIDTH], packed)
         rebuilt[slot] = packed
+    fetch_up.wait()
+    up = dot((entries[pl.ds(normal + count, count), :] * rates[4:5, :]).astype(BF16), w_up[...])
+    lanes = aux.shape[1]
+    whole = up.shape[1] // lanes
+    left = jnp.concatenate([low_moving, jnp.zeros((count, lanes // 2 - low_moving.shape[1]), F32)], axis=1)
+    moving += [up[:, part * lanes : (part + 1) * lanes] for part in range(whole)]
+    moving += [jnp.concatenate([left, up[:, whole * lanes :]], axis=1)]
+    aux[...] = jnp.concatenate(moving, axis=0).astype(BF16)
     occ = column_of(plan, OCCUPIED, count, current.shape[1])
     last = jnp.zeros((count, current.shape[1]), F32)
     for slot in range(4):
@@ -549,7 +561,13 @@
     tokens = count * steps
     row = lambda value: value.reshape(1, -1)
     home, seated, aux_rows = count * WIDTH, SEATS * WIDTH, AUX * count
-    gathered, plus, minus, stay, plan = call(
+    far_weights = (
+        acceptance_projection,
+        address_projection,
+        content_projection,
+        fading_lowrank_left.T,
+    )
+    gathered, plus, minus, stay, *weights, plan = call(
         pack_kernel,
         "pack",
         (
@@ -557,6 +575,7 @@
             out((seated, channels), BF16),
             out((seated, channels), BF16),
             out((home, channels), BF16),
+            *(out(value.shape, BF16) for value in far_weights),
             out((PLAN,), jnp.int32),
         ),
         [
@@ -567,14 +586,16 @@
             (carried_memory_matrices, "any"),
             (lagged_previous_entries, "load"),
             (arriving_hiddens, "load"),
+            *((value, "any") for value in far_weights),
         ],
         [
             pltpu.VMEM((tokens + 2 * count, feature), F32),
             pltpu.VMEM((count, heads, WIDTH, WIDTH), F32),
             pltpu.SemaphoreType.DMA((REB,)),
             pltpu.SemaphoreType.DMA((count,)),
+            pltpu.SemaphoreType.DMA((len(far_weights),)),
         ],
-        (VMEM_SPEC, VMEM_SPEC, VMEM_SPEC, VMEM_SPEC, SMEM_SPEC),
+        (VMEM_SPEC,) * (4 + len(far_weights)) + (SMEM_SPEC,),
     )
 
     def send(stage, up, down):
@@ -583,25 +604,6 @@
     plus, minus = send(0, plus, minus)
     pieces = [gathered] + [rotate(gathered, "head", k) for k in (1, 2, 3)]
     base = row(fading_baseline_entries)
-    far_weights = (
-        acceptance_projection,
-        address_projection,
-        content_projection,
-        fading_lowrank_left.T,
-        feedforward_address_proj,
-    )
-
-    def fetch(values, after):
-        values, _ = lax.optimization_barrier((values, after))
-        return call(
-            fetch_kernel,
-            "fetch",
-            tuple(out(value.shape, BF16) for value in values),
-            [(value, "any") for value in values],
-            [pltpu.SemaphoreType.DMA((len(values),))],
-        )
-
-    weights = fetch(far_weights, gathered)
     inner = fading_lowrank_left.shape[1]
     a_r, a_k, a_v, a_l, rebuilt, aux, hist_first, hist_low, time_last = call(
         project_kernel,
@@ -621,8 +623,13 @@
         + [(value, "vmem") for value in pieces]
         + [(row(pre_attention_scaling), "load"), (lag_blend_fractions, "load")]
         + [(value, "vmem") for value in weights]
-        + [(fading_lowrank_right, "load"), (base, "load")],
-        [pltpu.VMEM((REB * hist + tokens + 2 * count, model), F32)],
+        + [(feedforward_address_proj, "any"), (fading_lowrank_right, "load"), (base, "load")],
+        [
+            pltpu.VMEM((REB * hist + tokens + 2 * count, model), F32),
+            pltpu.VMEM(feedforward_address_proj.shape, BF16),
+            pltpu.SemaphoreType.DMA((1,)),
+        ],
+        cost=pl.CostEstimate(flops=20_000_000_000, transcendentals=0, bytes_accessed=8_000_000),
     )
     arrived = (plus, minus, stay, *send(0, aux, aux), aux)
     shape = lambda rows: out((rows + aux_rows, channels), BF16)
@@ -681,7 +688,16 @@
         + [(attention_exit_projection, "vmem")],
     )
     partials = [partial] + [rotate(partial, "head", k) for k in (1, 2, 3)]
-    ffn_weights = fetch((feedforward_address_proj, feedforward_content_proj), partial)
+    ffn_weights, _ = lax.optimization_barrier(
+        ((feedforward_address_proj, feedforward_content_proj), partial)
+    )
+    ffn_weights = call(
+        fetch_kernel,
+        "fetch",
+        tuple(out(value.shape, BF16) for value in ffn_weights),
+        [(value, "any") for value in ffn_weights],
+        [pltpu.SemaphoreType.DMA((len(ffn_weights),))],
+    )
     kept, to_one, to_two, to_three, channel_last = call(
         ffn_kernel,
         "ffn",

time: 87.4 us -> 86.6 us (level)
  Pallas kernels: 20.5 us -> 19.2 us
  starting transfers between devices: 33.6 us -> 34.7 us
    pallas_call x10 -> x9, Pallas kernels: 20.5 us -> 19.2 us  [call(): pl.pallas_call(kernel, name=name, out_shape=out_shape, in_specs=[SPECS[pl...]
    ppermute x19, starting transfers between devices: 33.6 us -> 34.7 us  [rotate(): return lax.ppermute(value, axis, pairs)]
  transfers between devices with their start and end apart: 19 -> 19, of which waited for: 10 -> 10; matrix products, arithmetic and copies ran while one was open for 1% -> 2% of each run, Pallas kernels for 10% -> 8%
where the time goes in v4:
time: 86.6 us; the launch traced here: 86.2 us
  starting transfers between devices  34.7 us (40%)
  waiting for transfers between devices  28.3 us (33%)
  Pallas kernels  19.2 us (22%)
  local copies, waits for them, and re-layouts  1.73 us (2%)
  between operations  1.42 us (2%)
    ppermute x19, starting transfers between devices, rotate(): return lax.ppermute(value, axis, pairs)  34.7 us
    ppermute x19, waiting for transfers between devices, rotate(): return lax.ppermute(value, axis, pairs)  28.3 us
    pallas_call x9, Pallas kernels, call(): pl.pallas_call(kernel, name=name, out_shape=out_shape, in_specs=[SPECS[pl...  19.2 us
  transfers between devices with their start and end apart: 19, of which 10 were waited for; matrix products, arithmetic and copies ran while one was open for 2% of the time, Pallas kernels for 8%

profile of v4, /device:TPU:2, one launch (start us, length us, event | category | flops | bytes accessed | tf_op | source)
XLA Modules:
  0.0 86.2 jit_solution(16687613624446940911)
XLA Ops:
  0.6 3.9 %pack.1 = (bf16[112,512]{1,0:T(8,128)(2,1)S(1)}, bf16[320,256]{1,0:T(8,128)(2,1)S(1)}, bf16[320,256]{1,0:T(8,128)(2,1)S(1)}, bf16[512,256]{1,0:T(8,128)(2,1)S(1)...) custom-call(s32[8]{0:T(128)} %former.1, s32[8]{0:T(128)} %marks.1, ...), custom_call_target="tpu_custom_call" | custom-call | tf_op jit(solution)/shard_map/pack/pallas_call | solution.py:41
  4.6 2.3 %collective-permute-start.10 = (bf16[112,512]{1,0:T(8,128)(2,1)S(1)}, bf16[112,512]{1,0:T(8,128)(2,1)S(1)}, u32[]{:S(2)}, u32[]{:S(2)}) collective-permute-start(bf16[112,512]{1,0:T(8,128)(2,1)S(1)} %get-tuple-element.59.own), channel_id=1, source_target_pairs={{0,3},{1,0},{2,1},{3,2},{4,7},{5,4},{6,5},{7,6},{8,11},{9,8},{10,9... | collective-permute-start | bytes 344072 | tf_op jit(solution)/shard_map/ppermute | solution.py:25
  6.9 0.0 collective-permute-start.8
  6.9 3.1 %collective-permute-start.9 = (bf16[112,512]{1,0:T(8,128)(2,1)S(1)}, bf16[112,512]{1,0:T(8,128)(2,1)S(1)}, u32[]{:S(2)}, u32[]{:S(2)}) collective-permute-start(bf16[112,512]{1,0:T(8,128)(2,1)S(1)} %get-tuple-element.59.own), channel_id=1, source_target_pairs={{0,2},{1,3},{2,0},{3,1},{4,6},{5,7},{6,4},{7,5},{8,10},{9,11},{10,... | collective-permute-start | bytes 344072 | tf_op jit(solution)/shard_map/ppermute | solution.py:25
  10.0 6.7 %collective-permute-start.11 = (bf16[320,256]{1,0:T(8,128)(2,1)S(1)}, bf16[320,256]{1,0:T(8,128)(2,1)S(1)}, u32[]{:S(2)}, u32[]{:S(2)}) collective-permute-start(bf16[320,256]{1,0:T(8,128)(2,1)S(1)} %get-tuple-element.60), channel_id=1, source_target_pairs={{0,160},{4,164},{8,168},{12,172},{16,176},{20,180},{24,184},{28,18... | collective-permute-start | bytes 491528 | tf_op jit(solution)/shard_map/ppermute | solution.py:25
  16.7 0.0 collective-permute-start.12
  16.7 0.0 collective-permute-done.10.by_three
  16.7 0.0 collective-permute-done.8.by_one
  16.8 0.0 collective-permute-done.9.by_two
  16.8 3.6 %project.1 = (f32[32,256]{1,0:T(8,128)S(1)}, f32[32,256]{1,0:T(8,128)S(1)}, f32[32,256]{1,0:T(8,128)S(1)}, f32[32,64]{1,0:T(8,128)S(1)}, f32[2,64,256]{2,1,0:T(8...) custom-call(s32[88]{0:T(128)S(1)} %get-tuple-element.58.plan, ...), custom_call_target="tpu_custom_call" | custom-call | flops 20000000000 | bytes 8000000 | tf_op jit(solution)/shard_map/project/pallas_call | solution.py:41
  20.4 5.1 %collective-permute-start.13 = (bf16[56,256]{1,0:T(8,128)(2,1)S(1)}, bf16[56,256]{1,0:T(8,128)(2,1)S(1)}, u32[]{:S(2)}, u32[]{:S(2)}) collective-permute-start(bf16[56,256]{1,0:T(8,128)(2,1)S(1)} %get-tuple-element.67.refs_5_), channel_id=1, source_target_pairs={{0,160},{4,164},{8,168},{12,172},{16,176},{20,180},{24,184},{28,18... | collective-permute-start | bytes 86024 | tf_op jit(solution)/shard_map/ppermute | solution.py:25
  25.5 0.0 collective-permute-start.14
  25.5 2.7 %collective-permute-done.13.refs_3_ = bf16[56,256]{1,0:T(8,128)(2,1)S(1)} collective-permute-done((bf16[56,256]{1,0:T(8,128)(2,1)S(1)}, bf16[56,256]{1,0:T(8,128)(2,1)S(1)}, u32[]{:S(2)}, u32[]{:S(2)}) %collective-permute-start.13) | collective-permute-done | bytes 28704 | tf_op jit(solution)/shard_map/ppermute | solution.py:25
  28.3 4.1 %collective-permute-done.14.refs_4_ = bf16[56,256]{1,0:T(8,128)(2,1)S(1)} collective-permute-done((bf16[56,256]{1,0:T(8,128)(2,1)S(1)}, bf16[56,256]{1,0:T(8,128)(2,1)S(1)}, u32[]{:S(2)}, u32[]{:S(2)}) %collective-permute-start.14) | collective-permute-done | bytes 28704 | tf_op jit(solution)/shard_map/ppermute | solution.py:25
  32.4 0.0 collective-permute-done.11.refs_0_
  32.4 0.0 collective-permute-done.12.refs_1_
  32.4 0.8 merge.4
  33.2 0.1 collective-permute-start.15
  33.3 1.7 %collective-permute-start.16 = (bf16[376,256]{1,0:T(8,128)(2,1)S(1)}, bf16[376,256]{1,0:T(8,128)(2,1)S(1)}, u32[]{:S(2)}, u32[]{:S(2)}) collective-permute-start(bf16[376,256]{1,0:T(8,128)(2,1)S(1)} %get-tuple-element.69), channel_id=1, source_target_pairs={{0,12},{4,16},{8,20},{12,24},{16,28},{20,32},{24,36},{28,40},{32,4... | collective-permute-start | bytes 577544 | tf_op jit(solution)/shard_map/ppermute | solution.py:25
  35.1 3.3 %collective-permute-done.15.refs_0_ = bf16[376,256]{1,0:T(8,128)(2,1)S(1)} collective-permute-done((bf16[376,256]{1,0:T(8,128)(2,1)S(1)}, bf16[376,256]{1,0:T(8,128)(2,1)S(1)}, u32[]{:S(2)}, u32[]{:S(2)}) %collective-permute-start.15) | collective-permute-done | bytes 192544 | tf_op jit(solution)/shard_map/ppermute | solution.py:25
  38.4 3.8 %collective-permute-done.16.refs_1_ = bf16[376,256]{1,0:T(8,128)(2,1)S(1)} collective-permute-done((bf16[376,256]{1,0:T(8,128)(2,1)S(1)}, bf16[376,256]{1,0:T(8,128)(2,1)S(1)}, u32[]{:S(2)}, u32[]{:S(2)}) %collective-permute-start.16) | collective-permute-done | bytes 192544 | tf_op jit(solution)/shard_map/ppermute | solution.py:25
  42.2 0.8 merge.5
  43.0 1.1 %collective-permute-start.17 = (bf16[376,256]{1,0:T(8,128)(2,1)S(1)}, bf16[376,256]{1,0:T(8,128)(2,1)S(1)}, u32[]{:S(2)}, u32[]{:S(2)}) collective-permute-start(bf16[376,256]{1,0:T(8,128)(2,1)S(1)} %get-tuple-element.71), channel_id=1, source_target_pairs={{0,224},{4,228},{8,232},{12,236},{16,240},{20,244},{24,248},{28,25... | collective-permute-start | bytes 577544 | tf_op jit(solution)/shard_map/ppermute | solution.py:25
  44.1 2.3 %collective-permute-start.18 = (bf16[376,256]{1,0:T(8,128)(2,1)S(1)}, bf16[376,256]{1,0:T(8,128)(2,1)S(1)}, u32[]{:S(2)}, u32[]{:S(2)}) collective-permute-start(bf16[376,256]{1,0:T(8,128)(2,1)S(1)} %get-tuple-element.72), channel_id=1, source_target_pairs={{0,32},{4,36},{8,40},{12,44},{16,48},{20,52},{24,56},{28,60},{32,6... | collective-permute-start | bytes 577544 | tf_op jit(solution)/shard_map/ppermute | solution.py:25
  46.4 4.3 %collective-permute-done.17.refs_0_ = bf16[376,256]{1,0:T(8,128)(2,1)S(1)} collective-permute-done((bf16[376,256]{1,0:T(8,128)(2,1)S(1)}, bf16[376,256]{1,0:T(8,128)(2,1)S(1)}, u32[]{:S(2)}, u32[]{:S(2)}) %collective-permute-start.17) | collective-permute-done | bytes 192544 | tf_op jit(solution)/shard_map/ppermute | solution.py:25
  50.7 0.7 collective-permute-done.18.refs_1_
  51.4 0.8 merge.6
  52.2 0.8 collective-permute-start.19
  53.0 1.0 %collective-permute-start.20 = (bf16[376,256]{1,0:T(8,128)(2,1)S(1)}, bf16[376,256]{1,0:T(8,128)(2,1)S(1)}, u32[]{:S(2)}, u32[]{:S(2)}) collective-permute-start(bf16[376,256]{1,0:T(8,128)(2,1)S(1)} %get-tuple-element.75), channel_id=1, source_target_pairs={{0,4},{4,8},{8,12},{12,16},{16,20},{20,24},{24,28},{28,32},{32,36}... | collective-permute-start | bytes 577544 | tf_op jit(solution)/shard_map/ppermute | solution.py:25
  54.0 0.6 slice.3
  55.2 0.9 %collective-permute-done.19.refs_0_ = bf16[376,256]{1,0:T(8,128)(2,1)S(1)} collective-permute-done((bf16[376,256]{1,0:T(8,128)(2,1)S(1)}, bf16[376,256]{1,0:T(8,128)(2,1)S(1)}, u32[]{:S(2)}, u32[]{:S(2)}) %collective-permute-start.19) | collective-permute-done | bytes 192544 | tf_op jit(solution)/shard_map/ppermute | solution.py:25
  56.1 5.2 %collective-permute-done.20.refs_1_ = bf16[376,256]{1,0:T(8,128)(2,1)S(1)} collective-permute-done((bf16[376,256]{1,0:T(8,128)(2,1)S(1)}, bf16[376,256]{1,0:T(8,128)(2,1)S(1)}, u32[]{:S(2)}, u32[]{:S(2)}) %collective-permute-start.20) | collective-permute-done | bytes 192544 | tf_op jit(solution)/shard_map/ppermute | solution.py:25
  61.4 0.0 copy-start.3
  61.4 0.7 merge.7
  62.1 0.0 copy-start.13
  62.1 0.5 copy-done.3
  62.6 2.6 %recur.1 = (f32[8,4,64,64]{3,2,1,0:T(8,128)}, bf16[32,2048]{1,0:T(8,128)(2,1)S(1)}, f32[8,896]{1,0:T(8,128)S(1)}) custom-call(s32[88]{0:T(128)S(1)} %get-tuple-element.58.plan, bf16[568,256]{1,0:T(8,128)(2,1)S(1)} %get-tuple-element.100.moved, f32[3,8,256]{2,1,0:T(8,128)S(1)} %get-tuple-element.77.hist_first, f32[8,64]{1,0:T(8,128)S(1)} %get-tuple-element.78.hist_low, ...), custom_call_target="tpu_custom_call" | custom-call | tf_op jit(solution)/shard_map/recur/pallas_call | solution.py:41
  65.2 0.0 collective-permute-start.21
  65.2 5.2 %collective-permute-start.22 = (bf16[32,2048]{1,0:T(8,128)(2,1)S(1)}, bf16[32,2048]{1,0:T(8,128)(2,1)S(1)}, u32[]{:S(2)}, u32[]{:S(2)}) collective-permute-start(bf16[32,2048]{1,0:T(8,128)(2,1)S(1)} %get-tuple-element.84.p_own), channel_id=1, source_target_pairs={{0,2},{1,3},{2,0},{3,1},{4,6},{5,7},{6,4},{7,5},{8,10},{9,11},{10,... | collective-permute-start | bytes 393224 | tf_op jit(solution)/shard_map/ppermute | solution.py:25
  70.4 0.0 collective-permute-start.23
  70.4 0.0 copy-done.13
  70.4 0.1 iota_compare_fusion
  70.5 3.2 %fetch.1 = (bf16[2048,896]{1,0:T(8,128)(2,1)S(1)}, bf16[896,2048]{1,0:T(8,128)(2,1)S(1)}) custom-call(bf16[2048,896]{1,0:T(8,128)(2,1)} %refs_0_, bf16[896,2048]{1,0:T(8,128)(2,1)} %refs_1_), custom_call_target="tpu_custom_call" | custom-call | tf_op jit(solution)/shard_map/fetch/pallas_call | solution.py:41
  73.7 0.0 collective-permute-done.21.p_one
  73.7 0.0 collective-permute-done.22.p_two
  73.7 1.7 %collective-permute-done.23.p_three = bf16[32,2048]{1,0:T(8,128)(2,1)S(1)} collective-permute-done((bf16[32,2048]{1,0:T(8,128)(2,1)S(1)}, bf16[32,2048]{1,0:T(8,128)(2,1)S(1)}, u32[]{:S(2)}, u32[]{:S(2)}) %collective-permute-start.23) | collective-permute-done | bytes 131104 | tf_op jit(solution)/shard_map/ppermute | solution.py:25
  75.4 2.6 %ffn.1 = (f32[32,512]{1,0:T(8,128)S(1)}, bf16[32,512]{1,0:T(8,128)(2,1)S(1)}, bf16[32,512]{1,0:T(8,128)(2,1)S(1)}, bf16[32,512]{1,0:T(8,128)(2,1)S(1)}, f32[8,512]{1,0:T(8,128)S(1)}) custom-call(s32[88]{0:T(128)S(1)} %get-tuple-element.58.plan, bf16[112,512]{1,0:T(8,128)(2,1)S(1)} %get-tuple-element.59.own, ...), custom_call_target="tpu_custom_call" | custom-call | tf_op jit(solution)/shard_map/ffn/pallas_call | solution.py:41
  78.0 0.4 collective-permute-start.24
  78.4 3.2 %collective-permute-start.25 = (bf16[32,512]{1,0:T(8,128)(2,1)S(1)}, bf16[32,512]{1,0:T(8,128)(2,1)S(1)}, u32[]{:S(2)}, u32[]{:S(2)}) collective-permute-start(bf16[32,512]{1,0:T(8,128)(2,1)S(1)} %get-tuple-element.92), channel_id=1, source_target_pairs={{0,2},{1,3},{2,0},{3,1},{4,6},{5,7},{6,4},{7,5},{8,10},{9,11},{10,... | collective-permute-start | bytes 98312 | tf_op jit(solution)/shard_map/ppermute | solution.py:25
  81.5 1.7 %collective-permute-start.26 = (bf16[32,512]{1,0:T(8,128)(2,1)S(1)}, bf16[32,512]{1,0:T(8,128)(2,1)S(1)}, u32[]{:S(2)}, u32[]{:S(2)}) collective-permute-start(bf16[32,512]{1,0:T(8,128)(2,1)S(1)} %get-tuple-element.93), channel_id=1, source_target_pairs={{0,3},{1,0},{2,1},{3,2},{4,7},{5,4},{6,5},{7,6},{8,11},{9,8},{10,9... | collective-permute-start | bytes 98312 | tf_op jit(solution)/shard_map/ppermute | solution.py:25
  83.3 0.6 copy.25
  83.9 0.0 collective-permute-done.24
  83.9 0.0 collective-permute-done.25
  83.9 1.5 %collective-permute-done.26 = bf16[32,512]{1,0:T(8,128)(2,1)S(1)} collective-permute-done((bf16[32,512]{1,0:T(8,128)(2,1)S(1)}, bf16[32,512]{1,0:T(8,128)(2,1)S(1)}, u32[]{:S(2)}, u32[]{:S(2)}) %collective-permute-start.26) | collective-permute-done | bytes 32800 | tf_op jit(solution)/shard_map/ppermute | solution.py:25
  85.5 0.7 bitcast_select_fusion
  (3 shorter events, 0.0 us)
Async XLA Ops:
  4.6 12.2 %collective-permute-start.10 = (bf16[112,512]{1,0:T(8,128)(2,1)S(1)}, bf16[112,512]{1,0:T(8,128)(2,1)S(1)}, u32[]{:S(2)}, u32[]{:S(2)}) collective-permute-start(bf16[112,512]{1,0:T(8,128)(2,1)S(1)} %get-tuple-element.59.own), channel_id=1, source_target_pairs={{0,3},{1,0},{2,1},{3,2},{4,7},{5,4},{6,5},{7,6},{8,11},{9,8},{10,9... | collective-permute-start | bytes 344072 | tf_op jit(solution)/shard_map/ppermute | solution.py:25
  6.9 9.8 %collective-permute-start.8 = (bf16[112,512]{1,0:T(8,128)(2,1)S(1)}, bf16[112,512]{1,0:T(8,128)(2,1)S(1)}, u32[]{:S(2)}, u32[]{:S(2)}) collective-permute-start(bf16[112,512]{1,0:T(8,128)(2,1)S(1)} %get-tuple-element.59.own), channel_id=1, source_target_pairs={{0,1},{1,2},{2,3},{3,0},{4,5},{5,6},{6,7},{7,4},{8,9},{9,10},{10,1... | collective-permute-start | bytes 344072 | tf_op jit(solution)/shard_map/ppermute | solution.py:25
  6.9 9.8 %collective-permute-start.9 = (bf16[112,512]{1,0:T(8,128)(2,1)S(1)}, bf16[112,512]{1,0:T(8,128)(2,1)S(1)}, u32[]{:S(2)}, u32[]{:S(2)}) collective-permute-start(bf16[112,512]{1,0:T(8,128)(2,1)S(1)} %get-tuple-element.59.own), channel_id=1, source_target_pairs={{0,2},{1,3},{2,0},{3,1},{4,6},{5,7},{6,4},{7,5},{8,10},{9,11},{10,... | collective-permute-start | bytes 344072 | tf_op jit(solution)/shard_map/ppermute | solution.py:25
  10.0 22.4 %collective-permute-start.11 = (bf16[320,256]{1,0:T(8,128)(2,1)S(1)}, bf16[320,256]{1,0:T(8,128)(2,1)S(1)}, u32[]{:S(2)}, u32[]{:S(2)}) collective-permute-start(bf16[320,256]{1,0:T(8,128)(2,1)S(1)} %get-tuple-element.60), channel_id=1, source_target_pairs={{0,160},{4,164},{8,168},{12,172},{16,176},{20,180},{24,184},{28,18... | collective-permute-start | bytes 491528 | tf_op jit(solution)/shard_map/ppermute | solution.py:25
  16.7 15.7 %collective-permute-start.12 = (bf16[320,256]{1,0:T(8,128)(2,1)S(1)}, bf16[320,256]{1,0:T(8,128)(2,1)S(1)}, u32[]{:S(2)}, u32[]{:S(2)}) collective-permute-start(bf16[320,256]{1,0:T(8,128)(2,1)S(1)} %get-tuple-element.61), channel_id=1, source_target_pairs={{0,96},{4,100},{8,104},{12,108},{16,112},{20,116},{24,120},{28,124... | collective-permute-start | bytes 491528 | tf_op jit(solution)/shard_map/ppermute | solution.py:25
  20.4 7.8 %collective-permute-start.13 = (bf16[56,256]{1,0:T(8,128)(2,1)S(1)}, bf16[56,256]{1,0:T(8,128)(2,1)S(1)}, u32[]{:S(2)}, u32[]{:S(2)}) collective-permute-start(bf16[56,256]{1,0:T(8,128)(2,1)S(1)} %get-tuple-element.67.refs_5_), channel_id=1, source_target_pairs={{0,160},{4,164},{8,168},{12,172},{16,176},{20,180},{24,184},{28,18... | collective-permute-start | bytes 86024 | tf_op jit(solution)/shard_map/ppermute | solution.py:25
  25.5 6.9 %collective-permute-start.14 = (bf16[56,256]{1,0:T(8,128)(2,1)S(1)}, bf16[56,256]{1,0:T(8,128)(2,1)S(1)}, u32[]{:S(2)}, u32[]{:S(2)}) collective-permute-start(bf16[56,256]{1,0:T(8,128)(2,1)S(1)} %get-tuple-element.67.refs_5_), channel_id=1, source_target_pairs={{0,96},{4,100},{8,104},{12,108},{16,112},{20,116},{24,120},{28,124... | collective-permute-start | bytes 86024 | tf_op jit(solution)/shard_map/ppermute | solution.py:25
  33.2 5.1 %collective-permute-start.15 = (bf16[376,256]{1,0:T(8,128)(2,1)S(1)}, bf16[376,256]{1,0:T(8,128)(2,1)S(1)}, u32[]{:S(2)}, u32[]{:S(2)}) collective-permute-start(bf16[376,256]{1,0:T(8,128)(2,1)S(1)} %get-tuple-element.68), channel_id=1, source_target_pairs={{0,244},{4,248},{8,252},{12,0},{16,4},{20,8},{24,12},{28,16},{32,2... | collective-permute-start | bytes 577544 | tf_op jit(solution)/shard_map/ppermute | solution.py:25
  33.3 8.8 %collective-permute-start.16 = (bf16[376,256]{1,0:T(8,128)(2,1)S(1)}, bf16[376,256]{1,0:T(8,128)(2,1)S(1)}, u32[]{:S(2)}, u32[]{:S(2)}) collective-permute-start(bf16[376,256]{1,0:T(8,128)(2,1)S(1)} %get-tuple-element.69), channel_id=1, source_target_pairs={{0,12},{4,16},{8,20},{12,24},{16,28},{20,32},{24,36},{28,40},{32,4... | collective-permute-start | bytes 577544 | tf_op jit(solution)/shard_map/ppermute | solution.py:25
  43.0 7.7 %collective-permute-start.17 = (bf16[376,256]{1,0:T(8,128)(2,1)S(1)}, bf16[376,256]{1,0:T(8,128)(2,1)S(1)}, u32[]{:S(2)}, u32[]{:S(2)}) collective-permute-start(bf16[376,256]{1,0:T(8,128)(2,1)S(1)} %get-tuple-element.71), channel_id=1, source_target_pairs={{0,224},{4,228},{8,232},{12,236},{16,240},{20,244},{24,248},{28,25... | collective-permute-start | bytes 577544 | tf_op jit(solution)/shard_map/ppermute | solution.py:25
  44.1 7.3 %collective-permute-start.18 = (bf16[376,256]{1,0:T(8,128)(2,1)S(1)}, bf16[376,256]{1,0:T(8,128)(2,1)S(1)}, u32[]{:S(2)}, u32[]{:S(2)}) collective-permute-start(bf16[376,256]{1,0:T(8,128)(2,1)S(1)} %get-tuple-element.72), channel_id=1, source_target_pairs={{0,32},{4,36},{8,40},{12,44},{16,48},{20,52},{24,56},{28,60},{32,6... | collective-permute-start | bytes 577544 | tf_op jit(solution)/shard_map/ppermute | solution.py:25
  52.2 3.9 %collective-permute-start.19 = (bf16[376,256]{1,0:T(8,128)(2,1)S(1)}, bf16[376,256]{1,0:T(8,128)(2,1)S(1)}, u32[]{:S(2)}, u32[]{:S(2)}) collective-permute-start(bf16[376,256]{1,0:T(8,128)(2,1)S(1)} %get-tuple-element.74), channel_id=1, source_target_pairs={{0,252},{4,0},{8,4},{12,8},{16,12},{20,16},{24,20},{28,24},{32,28}... | collective-permute-start | bytes 577544 | tf_op jit(solution)/shard_map/ppermute | solution.py:25
  53.0 8.4 %collective-permute-start.20 = (bf16[376,256]{1,0:T(8,128)(2,1)S(1)}, bf16[376,256]{1,0:T(8,128)(2,1)S(1)}, u32[]{:S(2)}, u32[]{:S(2)}) collective-permute-start(bf16[376,256]{1,0:T(8,128)(2,1)S(1)} %get-tuple-element.75), channel_id=1, source_target_pairs={{0,4},{4,8},{8,12},{12,16},{16,20},{20,24},{24,28},{28,32},{32,36}... | collective-permute-start | bytes 577544 | tf_op jit(solution)/shard_map/ppermute | solution.py:25
  61.4 1.2 %copy-start.3 = (bf16[256,2048]{1,0:T(8,128)(2,1)S(1)}, bf16[256,2048]{1,0:T(8,128)(2,1)}, u32[]{:S(2)}) copy-start(bf16[256,2048]{1,0:T(8,128)(2,1)} %w_out.1) | copy-start | bytes 3145732
  62.1 8.4 %copy-start.13 = (s32[8]{0:T(128)S(1)}, s32[8]{0:T(128)}, u32[]{:S(2)}) copy-start(s32[8]{0:T(128)} %occupied.1) | copy-start | bytes 100
  65.2 8.5 %collective-permute-start.21 = (bf16[32,2048]{1,0:T(8,128)(2,1)S(1)}, bf16[32,2048]{1,0:T(8,128)(2,1)S(1)}, u32[]{:S(2)}, u32[]{:S(2)}) collective-permute-start(bf16[32,2048]{1,0:T(8,128)(2,1)S(1)} %get-tuple-element.84.p_own), channel_id=1, source_target_pairs={{0,1},{1,2},{2,3},{3,0},{4,5},{5,6},{6,7},{7,4},{8,9},{9,10},{10,1... | collective-permute-start | bytes 393224 | tf_op jit(solution)/shard_map/ppermute | solution.py:25
  65.2 8.5 %collective-permute-start.22 = (bf16[32,2048]{1,0:T(8,128)(2,1)S(1)}, bf16[32,2048]{1,0:T(8,128)(2,1)S(1)}, u32[]{:S(2)}, u32[]{:S(2)}) collective-permute-start(bf16[32,2048]{1,0:T(8,128)(2,1)S(1)} %get-tuple-element.84.p_own), channel_id=1, source_target_pairs={{0,2},{1,3},{2,0},{3,1},{4,6},{5,7},{6,4},{7,5},{8,10},{9,11},{10,... | collective-permute-start | bytes 393224 | tf_op jit(solution)/shard_map/ppermute | solution.py:25
  70.4 5.0 %collective-permute-start.23 = (bf16[32,2048]{1,0:T(8,128)(2,1)S(1)}, bf16[32,2048]{1,0:T(8,128)(2,1)S(1)}, u32[]{:S(2)}, u32[]{:S(2)}) collective-permute-start(bf16[32,2048]{1,0:T(8,128)(2,1)S(1)} %get-tuple-element.84.p_own), channel_id=1, source_target_pairs={{0,3},{1,0},{2,1},{3,2},{4,7},{5,4},{6,5},{7,6},{8,11},{9,8},{10,9... | collective-permute-start | bytes 393224 | tf_op jit(solution)/shard_map/ppermute | solution.py:25
  78.0 5.9 %collective-permute-start.24 = (bf16[32,512]{1,0:T(8,128)(2,1)S(1)}, bf16[32,512]{1,0:T(8,128)(2,1)S(1)}, u32[]{:S(2)}, u32[]{:S(2)}) collective-permute-start(bf16[32,512]{1,0:T(8,128)(2,1)S(1)} %get-tuple-element.91), channel_id=1, source_target_pairs={{0,1},{1,2},{2,3},{3,0},{4,5},{5,6},{6,7},{7,4},{8,9},{9,10},{10,1... | collective-permute-start | bytes 98312 | tf_op jit(solution)/shard_map/ppermute | solution.py:25
  78.4 5.5 %collective-permute-start.25 = (bf16[32,512]{1,0:T(8,128)(2,1)S(1)}, bf16[32,512]{1,0:T(8,128)(2,1)S(1)}, u32[]{:S(2)}, u32[]{:S(2)}) collective-permute-start(bf16[32,512]{1,0:T(8,128)(2,1)S(1)} %get-tuple-element.92), channel_id=1, source_target_pairs={{0,2},{1,3},{2,0},{3,1},{4,6},{5,7},{6,4},{7,5},{8,10},{9,11},{10,... | collective-permute-start | bytes 98312 | tf_op jit(solution)/shard_map/ppermute | solution.py:25
  81.5 3.9 %collective-permute-start.26 = (bf16[32,512]{1,0:T(8,128)(2,1)S(1)}, bf16[32,512]{1,0:T(8,128)(2,1)S(1)}, u32[]{:S(2)}, u32[]{:S(2)}) collective-permute-start(bf16[32,512]{1,0:T(8,128)(2,1)S(1)} %get-tuple-element.93), channel_id=1, source_target_pairs={{0,3},{1,0},{2,1},{3,2},{4,7},{5,4},{6,5},{7,6},{8,11},{9,8},{10,9... | collective-permute-start | bytes 98312 | tf_op jit(solution)/shard_map/ppermute | solution.py:25

commit v5 on v4

--- a/solution.py
+++ b/solution.py
@@ -166,11 +166,9 @@
 def load_row(plan, stage, index, count, target, plus, minus, stay):
     digit = plan[DIGIT + stage * count + index]
     seat = seat_rows(plan, stage, index, count)
-    for sign, source, rows in ((1, plus, seat), (-1, minus, seat), (0, stay, home_rows(index))):
-
-        @pl.when(digit == sign)
-        def _(source=source, rows=rows):
-            target[home_rows(index), :] = source[rows, :]
+    rows = home_rows(index)
+    came = jnp.where(digit == 1, plus[seat, :], minus[seat, :])
+    target[rows, :] = jnp.where(digit == 0, stay[rows, :], came)
 
 
 def pack_kernel(

time: 86.6 us -> 86.3 us (level)
  no operation moved by 1% of the time
where the time goes in v5:
time: 86.3 us; the launch traced here: 85.9 us
  starting transfers between devices  34.9 us (40%)
  waiting for transfers between devices  28.2 us (33%)
  Pallas kernels  18.8 us (22%)
  local copies, waits for them, and re-layouts  1.82 us (2%)
  between operations  1.42 us (2%)
    ppermute x19, starting transfers between devices, rotate(): return lax.ppermute(value, axis, pairs)  34.9 us
    ppermute x19, waiting for transfers between devices, rotate(): return lax.ppermute(value, axis, pairs)  28.2 us
    pallas_call x9, Pallas kernels, call(): pl.pallas_call(kernel, name=name, out_shape=out_shape, in_specs=[SPECS[pl...  18.8 us
  transfers between devices with their start and end apart: 19, of which 10 were waited for; matrix products, arithmetic and copies ran while one was open for 2% of the time, Pallas kernels for 8%

profile of v5, /device:TPU:2, one launch (start us, length us, event | category | flops | bytes accessed | tf_op | source)
XLA Modules:
  0.0 85.9 jit_solution(17574095353868963678)
XLA Ops:
  0.6 3.9 %pack.1 = (bf16[112,512]{1,0:T(8,128)(2,1)S(1)}, bf16[320,256]{1,0:T(8,128)(2,1)S(1)}, bf16[320,256]{1,0:T(8,128)(2,1)S(1)}, bf16[512,256]{1,0:T(8,128)(2,1)S(1)...) custom-call(s32[8]{0:T(128)} %former.1, s32[8]{0:T(128)} %marks.1, ...), custom_call_target="tpu_custom_call" | custom-call | tf_op jit(solution)/shard_map/pack/pallas_call | solution.py:41
  4.6 2.3 %collective-permute-start.10 = (bf16[112,512]{1,0:T(8,128)(2,1)S(1)}, bf16[112,512]{1,0:T(8,128)(2,1)S(1)}, u32[]{:S(2)}, u32[]{:S(2)}) collective-permute-start(bf16[112,512]{1,0:T(8,128)(2,1)S(1)} %get-tuple-element.59.own), channel_id=1, source_target_pairs={{0,3},{1,0},{2,1},{3,2},{4,7},{5,4},{6,5},{7,6},{8,11},{9,8},{10,9... | collective-permute-start | bytes 344072 | tf_op jit(solution)/shard_map/ppermute | solution.py:25
  6.9 0.0 collective-permute-start.8
  6.9 3.1 %collective-permute-start.9 = (bf16[112,512]{1,0:T(8,128)(2,1)S(1)}, bf16[112,512]{1,0:T(8,128)(2,1)S(1)}, u32[]{:S(2)}, u32[]{:S(2)}) collective-permute-start(bf16[112,512]{1,0:T(8,128)(2,1)S(1)} %get-tuple-element.59.own), channel_id=1, source_target_pairs={{0,2},{1,3},{2,0},{3,1},{4,6},{5,7},{6,4},{7,5},{8,10},{9,11},{10,... | collective-permute-start | bytes 344072 | tf_op jit(solution)/shard_map/ppermute | solution.py:25
  10.0 6.7 %collective-permute-start.11 = (bf16[320,256]{1,0:T(8,128)(2,1)S(1)}, bf16[320,256]{1,0:T(8,128)(2,1)S(1)}, u32[]{:S(2)}, u32[]{:S(2)}) collective-permute-start(bf16[320,256]{1,0:T(8,128)(2,1)S(1)} %get-tuple-element.60), channel_id=1, source_target_pairs={{0,160},{4,164},{8,168},{12,172},{16,176},{20,180},{24,184},{28,18... | collective-permute-start | bytes 491528 | tf_op jit(solution)/shard_map/ppermute | solution.py:25
  16.7 0.0 collective-permute-start.12
  16.7 0.0 collective-permute-done.10.by_three
  16.7 0.0 collective-permute-done.8.by_one
  16.7 0.0 collective-permute-done.9.by_two
  16.8 3.6 %project.1 = (f32[32,256]{1,0:T(8,128)S(1)}, f32[32,256]{1,0:T(8,128)S(1)}, f32[32,256]{1,0:T(8,128)S(1)}, f32[32,64]{1,0:T(8,128)S(1)}, f32[2,64,256]{2,1,0:T(8...) custom-call(s32[88]{0:T(128)S(1)} %get-tuple-element.58.plan, ...), custom_call_target="tpu_custom_call" | custom-call | flops 20000000000 | bytes 8000000 | tf_op jit(solution)/shard_map/project/pallas_call | solution.py:41
  20.4 5.1 %collective-permute-start.13 = (bf16[56,256]{1,0:T(8,128)(2,1)S(1)}, bf16[56,256]{1,0:T(8,128)(2,1)S(1)}, u32[]{:S(2)}, u32[]{:S(2)}) collective-permute-start(bf16[56,256]{1,0:T(8,128)(2,1)S(1)} %get-tuple-element.67.refs_5_), channel_id=1, source_target_pairs={{0,160},{4,164},{8,168},{12,172},{16,176},{20,180},{24,184},{28,18... | collective-permute-start | bytes 86024 | tf_op jit(solution)/shard_map/ppermute | solution.py:25
  25.5 0.0 collective-permute-start.14
  25.5 2.7 %collective-permute-done.13.refs_3_ = bf16[56,256]{1,0:T(8,128)(2,1)S(1)} collective-permute-done((bf16[56,256]{1,0:T(8,128)(2,1)S(1)}, bf16[56,256]{1,0:T(8,128)(2,1)S(1)}, u32[]{:S(2)}, u32[]{:S(2)}) %collective-permute-start.13) | collective-permute-done | bytes 28704 | tf_op jit(solution)/shard_map/ppermute | solution.py:25
  28.3 4.1 %collective-permute-done.14.refs_4_ = bf16[56,256]{1,0:T(8,128)(2,1)S(1)} collective-permute-done((bf16[56,256]{1,0:T(8,128)(2,1)S(1)}, bf16[56,256]{1,0:T(8,128)(2,1)S(1)}, u32[]{:S(2)}, u32[]{:S(2)}) %collective-permute-start.14) | collective-permute-done | bytes 28704 | tf_op jit(solution)/shard_map/ppermute | solution.py:25
  32.4 0.0 collective-permute-done.11.refs_0_
  32.4 0.0 collective-permute-done.12.refs_1_
  32.4 0.7 merge.4
  33.1 0.1 collective-permute-start.15
  33.2 1.7 %collective-permute-start.16 = (bf16[376,256]{1,0:T(8,128)(2,1)S(1)}, bf16[376,256]{1,0:T(8,128)(2,1)S(1)}, u32[]{:S(2)}, u32[]{:S(2)}) collective-permute-start(bf16[376,256]{1,0:T(8,128)(2,1)S(1)} %get-tuple-element.69), channel_id=1, source_target_pairs={{0,12},{4,16},{8,20},{12,24},{16,28},{20,32},{24,36},{28,40},{32,4... | collective-permute-start | bytes 577544 | tf_op jit(solution)/shard_map/ppermute | solution.py:25
  35.0 3.3 %collective-permute-done.15.refs_0_ = bf16[376,256]{1,0:T(8,128)(2,1)S(1)} collective-permute-done((bf16[376,256]{1,0:T(8,128)(2,1)S(1)}, bf16[376,256]{1,0:T(8,128)(2,1)S(1)}, u32[]{:S(2)}, u32[]{:S(2)}) %collective-permute-start.15) | collective-permute-done | bytes 192544 | tf_op jit(solution)/shard_map/ppermute | solution.py:25
  38.3 3.8 %collective-permute-done.16.refs_1_ = bf16[376,256]{1,0:T(8,128)(2,1)S(1)} collective-permute-done((bf16[376,256]{1,0:T(8,128)(2,1)S(1)}, bf16[376,256]{1,0:T(8,128)(2,1)S(1)}, u32[]{:S(2)}, u32[]{:S(2)}) %collective-permute-start.16) | collective-permute-done | bytes 192544 | tf_op jit(solution)/shard_map/ppermute | solution.py:25
  42.1 0.7 merge.5
  42.8 1.1 %collective-permute-start.17 = (bf16[376,256]{1,0:T(8,128)(2,1)S(1)}, bf16[376,256]{1,0:T(8,128)(2,1)S(1)}, u32[]{:S(2)}, u32[]{:S(2)}) collective-permute-start(bf16[376,256]{1,0:T(8,128)(2,1)S(1)} %get-tuple-element.71), channel_id=1, source_target_pairs={{0,224},{4,228},{8,232},{12,236},{16,240},{20,244},{24,248},{28,25... | collective-permute-start | bytes 577544 | tf_op jit(solution)/shard_map/ppermute | solution.py:25
  43.9 2.3 %collective-permute-start.18 = (bf16[376,256]{1,0:T(8,128)(2,1)S(1)}, bf16[376,256]{1,0:T(8,128)(2,1)S(1)}, u32[]{:S(2)}, u32[]{:S(2)}) collective-permute-start(bf16[376,256]{1,0:T(8,128)(2,1)S(1)} %get-tuple-element.72), channel_id=1, source_target_pairs={{0,32},{4,36},{8,40},{12,44},{16,48},{20,52},{24,56},{28,60},{32,6... | collective-permute-start | bytes 577544 | tf_op jit(solution)/shard_map/ppermute | solution.py:25
  46.2 4.3 %collective-permute-done.17.refs_0_ = bf16[376,256]{1,0:T(8,128)(2,1)S(1)} collective-permute-done((bf16[376,256]{1,0:T(8,128)(2,1)S(1)}, bf16[376,256]{1,0:T(8,128)(2,1)S(1)}, u32[]{:S(2)}, u32[]{:S(2)}) %collective-permute-start.17) | collective-permute-done | bytes 192544 | tf_op jit(solution)/shard_map/ppermute | solution.py:25
  50.5 0.7 collective-permute-done.18.refs_1_
  51.2 0.7 merge.6
  51.9 0.6 collective-permute-start.19
  52.5 1.2 %collective-permute-start.20 = (bf16[376,256]{1,0:T(8,128)(2,1)S(1)}, bf16[376,256]{1,0:T(8,128)(2,1)S(1)}, u32[]{:S(2)}, u32[]{:S(2)}) collective-permute-start(bf16[376,256]{1,0:T(8,128)(2,1)S(1)} %get-tuple-element.75), channel_id=1, source_target_pairs={{0,4},{4,8},{8,12},{12,16},{16,20},{20,24},{24,28},{28,32},{32,36}... | collective-permute-start | bytes 577544 | tf_op jit(solution)/shard_map/ppermute | solution.py:25
  53.7 0.6 slice.3
  54.9 0.7 collective-permute-done.19.refs_0_
  55.7 5.2 %collective-permute-done.20.refs_1_ = bf16[376,256]{1,0:T(8,128)(2,1)S(1)} collective-permute-done((bf16[376,256]{1,0:T(8,128)(2,1)S(1)}, bf16[376,256]{1,0:T(8,128)(2,1)S(1)}, u32[]{:S(2)}, u32[]{:S(2)}) %collective-permute-start.20) | collective-permute-done | bytes 192544 | tf_op jit(solution)/shard_map/ppermute | solution.py:25
  60.9 0.0 copy-start.3
  60.9 0.6 merge.7
  61.5 0.0 copy-start.13
  61.5 0.6 copy-done.3
  62.1 2.7 %recur.1 = (f32[8,4,64,64]{3,2,1,0:T(8,128)}, bf16[32,2048]{1,0:T(8,128)(2,1)S(1)}, f32[8,896]{1,0:T(8,128)S(1)}) custom-call(s32[88]{0:T(128)S(1)} %get-tuple-element.58.plan, bf16[568,256]{1,0:T(8,128)(2,1)S(1)} %get-tuple-element.100.moved, f32[3,8,256]{2,1,0:T(8,128)S(1)} %get-tuple-element.77.hist_first, f32[8,64]{1,0:T(8,128)S(1)} %get-tuple-element.78.hist_low, ...), custom_call_target="tpu_custom_call" | custom-call | tf_op jit(solution)/shard_map/recur/pallas_call | solution.py:41
  64.8 0.0 collective-permute-start.21
  64.8 5.4 %collective-permute-start.22 = (bf16[32,2048]{1,0:T(8,128)(2,1)S(1)}, bf16[32,2048]{1,0:T(8,128)(2,1)S(1)}, u32[]{:S(2)}, u32[]{:S(2)}) collective-permute-start(bf16[32,2048]{1,0:T(8,128)(2,1)S(1)} %get-tuple-element.84.p_own), channel_id=1, source_target_pairs={{0,2},{1,3},{2,0},{3,1},{4,6},{5,7},{6,4},{7,5},{8,10},{9,11},{10,... | collective-permute-start | bytes 393224 | tf_op jit(solution)/shard_map/ppermute | solution.py:25
  70.1 0.0 collective-permute-start.23
  70.1 0.0 copy-done.13
  70.1 0.1 iota_compare_fusion
  70.2 3.2 %fetch.1 = (bf16[2048,896]{1,0:T(8,128)(2,1)S(1)}, bf16[896,2048]{1,0:T(8,128)(2,1)S(1)}) custom-call(bf16[2048,896]{1,0:T(8,128)(2,1)} %refs_0_, bf16[896,2048]{1,0:T(8,128)(2,1)} %refs_1_), custom_call_target="tpu_custom_call" | custom-call | tf_op jit(solution)/shard_map/fetch/pallas_call | solution.py:41
  73.4 0.0 collective-permute-done.21.p_one
  73.4 0.0 collective-permute-done.22.p_two
  73.4 1.7 %collective-permute-done.23.p_three = bf16[32,2048]{1,0:T(8,128)(2,1)S(1)} collective-permute-done((bf16[32,2048]{1,0:T(8,128)(2,1)S(1)}, bf16[32,2048]{1,0:T(8,128)(2,1)S(1)}, u32[]{:S(2)}, u32[]{:S(2)}) %collective-permute-start.23) | collective-permute-done | bytes 131104 | tf_op jit(solution)/shard_map/ppermute | solution.py:25
  75.1 2.6 %ffn.1 = (f32[32,512]{1,0:T(8,128)S(1)}, bf16[32,512]{1,0:T(8,128)(2,1)S(1)}, bf16[32,512]{1,0:T(8,128)(2,1)S(1)}, bf16[32,512]{1,0:T(8,128)(2,1)S(1)}, f32[8,512]{1,0:T(8,128)S(1)}) custom-call(s32[88]{0:T(128)S(1)} %get-tuple-element.58.plan, bf16[112,512]{1,0:T(8,128)(2,1)S(1)} %get-tuple-element.59.own, ...), custom_call_target="tpu_custom_call" | custom-call | tf_op jit(solution)/shard_map/ffn/pallas_call | solution.py:41
  77.7 0.4 collective-permute-start.24
  78.1 3.2 %collective-permute-start.25 = (bf16[32,512]{1,0:T(8,128)(2,1)S(1)}, bf16[32,512]{1,0:T(8,128)(2,1)S(1)}, u32[]{:S(2)}, u32[]{:S(2)}) collective-permute-start(bf16[32,512]{1,0:T(8,128)(2,1)S(1)} %get-tuple-element.92), channel_id=1, source_target_pairs={{0,2},{1,3},{2,0},{3,1},{4,6},{5,7},{6,4},{7,5},{8,10},{9,11},{10,... | collective-permute-start | bytes 98312 | tf_op jit(solution)/shard_map/ppermute | solution.py:25
  81.2 1.7 %collective-permute-start.26 = (bf16[32,512]{1,0:T(8,128)(2,1)S(1)}, bf16[32,512]{1,0:T(8,128)(2,1)S(1)}, u32[]{:S(2)}, u32[]{:S(2)}) collective-permute-start(bf16[32,512]{1,0:T(8,128)(2,1)S(1)} %get-tuple-element.93), channel_id=1, source_target_pairs={{0,3},{1,0},{2,1},{3,2},{4,7},{5,4},{6,5},{7,6},{8,11},{9,8},{10,9... | collective-permute-start | bytes 98312 | tf_op jit(solution)/shard_map/ppermute | solution.py:25
  83.0 0.6 copy.25
  83.6 0.0 collective-permute-done.24
  83.6 0.0 collective-permute-done.25
  83.6 1.5 %collective-permute-done.26 = bf16[32,512]{1,0:T(8,128)(2,1)S(1)} collective-permute-done((bf16[32,512]{1,0:T(8,128)(2,1)S(1)}, bf16[32,512]{1,0:T(8,128)(2,1)S(1)}, u32[]{:S(2)}, u32[]{:S(2)}) %collective-permute-start.26) | collective-permute-done | bytes 32800 | tf_op jit(solution)/shard_map/ppermute | solution.py:25
  85.2 0.7 bitcast_select_fusion
  (3 shorter events, 0.0 us)
Async XLA Ops:
  4.6 12.2 %collective-permute-start.10 = (bf16[112,512]{1,0:T(8,128)(2,1)S(1)}, bf16[112,512]{1,0:T(8,128)(2,1)S(1)}, u32[]{:S(2)}, u32[]{:S(2)}) collective-permute-start(bf16[112,512]{1,0:T(8,128)(2,1)S(1)} %get-tuple-element.59.own), channel_id=1, source_target_pairs={{0,3},{1,0},{2,1},{3,2},{4,7},{5,4},{6,5},{7,6},{8,11},{9,8},{10,9... | collective-permute-start | bytes 344072 | tf_op jit(solution)/shard_map/ppermute | solution.py:25
  6.9 9.8 %collective-permute-start.8 = (bf16[112,512]{1,0:T(8,128)(2,1)S(1)}, bf16[112,512]{1,0:T(8,128)(2,1)S(1)}, u32[]{:S(2)}, u32[]{:S(2)}) collective-permute-start(bf16[112,512]{1,0:T(8,128)(2,1)S(1)} %get-tuple-element.59.own), channel_id=1, source_target_pairs={{0,1},{1,2},{2,3},{3,0},{4,5},{5,6},{6,7},{7,4},{8,9},{9,10},{10,1... | collective-permute-start | bytes 344072 | tf_op jit(solution)/shard_map/ppermute | solution.py:25
  6.9 9.8 %collective-permute-start.9 = (bf16[112,512]{1,0:T(8,128)(2,1)S(1)}, bf16[112,512]{1,0:T(8,128)(2,1)S(1)}, u32[]{:S(2)}, u32[]{:S(2)}) collective-permute-start(bf16[112,512]{1,0:T(8,128)(2,1)S(1)} %get-tuple-element.59.own), channel_id=1, source_target_pairs={{0,2},{1,3},{2,0},{3,1},{4,6},{5,7},{6,4},{7,5},{8,10},{9,11},{10,... | collective-permute-start | bytes 344072 | tf_op jit(solution)/shard_map/ppermute | solution.py:25
  10.0 22.4 %collective-permute-start.11 = (bf16[320,256]{1,0:T(8,128)(2,1)S(1)}, bf16[320,256]{1,0:T(8,128)(2,1)S(1)}, u32[]{:S(2)}, u32[]{:S(2)}) collective-permute-start(bf16[320,256]{1,0:T(8,128)(2,1)S(1)} %get-tuple-element.60), channel_id=1, source_target_pairs={{0,160},{4,164},{8,168},{12,172},{16,176},{20,180},{24,184},{28,18... | collective-permute-start | bytes 491528 | tf_op jit(solution)/shard_map/ppermute | solution.py:25
  16.7 15.7 %collective-permute-start.12 = (bf16[320,256]{1,0:T(8,128)(2,1)S(1)}, bf16[320,256]{1,0:T(8,128)(2,1)S(1)}, u32[]{:S(2)}, u32[]{:S(2)}) collective-permute-start(bf16[320,256]{1,0:T(8,128)(2,1)S(1)} %get-tuple-element.61), channel_id=1, source_target_pairs={{0,96},{4,100},{8,104},{12,108},{16,112},{20,116},{24,120},{28,124... | collective-permute-start | bytes 491528 | tf_op jit(solution)/shard_map/ppermute | solution.py:25
  20.4 7.8 %collective-permute-start.13 = (bf16[56,256]{1,0:T(8,128)(2,1)S(1)}, bf16[56,256]{1,0:T(8,128)(2,1)S(1)}, u32[]{:S(2)}, u32[]{:S(2)}) collective-permute-start(bf16[56,256]{1,0:T(8,128)(2,1)S(1)} %get-tuple-element.67.refs_5_), channel_id=1, source_target_pairs={{0,160},{4,164},{8,168},{12,172},{16,176},{20,180},{24,184},{28,18... | collective-permute-start | bytes 86024 | tf_op jit(solution)/shard_map/ppermute | solution.py:25
  25.5 6.9 %collective-permute-start.14 = (bf16[56,256]{1,0:T(8,128)(2,1)S(1)}, bf16[56,256]{1,0:T(8,128)(2,1)S(1)}, u32[]{:S(2)}, u32[]{:S(2)}) collective-permute-start(bf16[56,256]{1,0:T(8,128)(2,1)S(1)} %get-tuple-element.67.refs_5_), channel_id=1, source_target_pairs={{0,96},{4,100},{8,104},{12,108},{16,112},{20,116},{24,120},{28,124... | collective-permute-start | bytes 86024 | tf_op jit(solution)/shard_map/ppermute | solution.py:25
  33.1 5.1 %collective-permute-start.15 = (bf16[376,256]{1,0:T(8,128)(2,1)S(1)}, bf16[376,256]{1,0:T(8,128)(2,1)S(1)}, u32[]{:S(2)}, u32[]{:S(2)}) collective-permute-start(bf16[376,256]{1,0:T(8,128)(2,1)S(1)} %get-tuple-element.68), channel_id=1, source_target_pairs={{0,244},{4,248},{8,252},{12,0},{16,4},{20,8},{24,12},{28,16},{32,2... | collective-permute-start | bytes 577544 | tf_op jit(solution)/shard_map/ppermute | solution.py:25
  33.2 8.8 %collective-permute-start.16 = (bf16[376,256]{1,0:T(8,128)(2,1)S(1)}, bf16[376,256]{1,0:T(8,128)(2,1)S(1)}, u32[]{:S(2)}, u32[]{:S(2)}) collective-permute-start(bf16[376,256]{1,0:T(8,128)(2,1)S(1)} %get-tuple-element.69), channel_id=1, source_target_pairs={{0,12},{4,16},{8,20},{12,24},{16,28},{20,32},{24,36},{28,40},{32,4... | collective-permute-start | bytes 577544 | tf_op jit(solution)/shard_map/ppermute | solution.py:25
  42.8 7.7 %collective-permute-start.17 = (bf16[376,256]{1,0:T(8,128)(2,1)S(1)}, bf16[376,256]{1,0:T(8,128)(2,1)S(1)}, u32[]{:S(2)}, u32[]{:S(2)}) collective-permute-start(bf16[376,256]{1,0:T(8,128)(2,1)S(1)} %get-tuple-element.71), channel_id=1, source_target_pairs={{0,224},{4,228},{8,232},{12,236},{16,240},{20,244},{24,248},{28,25... | collective-permute-start | bytes 577544 | tf_op jit(solution)/shard_map/ppermute | solution.py:25
  43.9 7.3 %collective-permute-start.18 = (bf16[376,256]{1,0:T(8,128)(2,1)S(1)}, bf16[376,256]{1,0:T(8,128)(2,1)S(1)}, u32[]{:S(2)}, u32[]{:S(2)}) collective-permute-start(bf16[376,256]{1,0:T(8,128)(2,1)S(1)} %get-tuple-element.72), channel_id=1, source_target_pairs={{0,32},{4,36},{8,40},{12,44},{16,48},{20,52},{24,56},{28,60},{32,6... | collective-permute-start | bytes 577544 | tf_op jit(solution)/shard_map/ppermute | solution.py:25
  51.9 3.7 %collective-permute-start.19 = (bf16[376,256]{1,0:T(8,128)(2,1)S(1)}, bf16[376,256]{1,0:T(8,128)(2,1)S(1)}, u32[]{:S(2)}, u32[]{:S(2)}) collective-permute-start(bf16[376,256]{1,0:T(8,128)(2,1)S(1)} %get-tuple-element.74), channel_id=1, source_target_pairs={{0,252},{4,0},{8,4},{12,8},{16,12},{20,16},{24,20},{28,24},{32,28}... | collective-permute-start | bytes 577544 | tf_op jit(solution)/shard_map/ppermute | solution.py:25
  52.5 8.4 %collective-permute-start.20 = (bf16[376,256]{1,0:T(8,128)(2,1)S(1)}, bf16[376,256]{1,0:T(8,128)(2,1)S(1)}, u32[]{:S(2)}, u32[]{:S(2)}) collective-permute-start(bf16[376,256]{1,0:T(8,128)(2,1)S(1)} %get-tuple-element.75), channel_id=1, source_target_pairs={{0,4},{4,8},{8,12},{12,16},{16,20},{20,24},{24,28},{28,32},{32,36}... | collective-permute-start | bytes 577544 | tf_op jit(solution)/shard_map/ppermute | solution.py:25
  60.9 1.2 %copy-start.3 = (bf16[256,2048]{1,0:T(8,128)(2,1)S(1)}, bf16[256,2048]{1,0:T(8,128)(2,1)}, u32[]{:S(2)}) copy-start(bf16[256,2048]{1,0:T(8,128)(2,1)} %w_out.1) | copy-start | bytes 3145732
  61.5 8.6 %copy-start.13 = (s32[8]{0:T(128)S(1)}, s32[8]{0:T(128)}, u32[]{:S(2)}) copy-start(s32[8]{0:T(128)} %occupied.1) | copy-start | bytes 100
  64.8 8.6 %collective-permute-start.21 = (bf16[32,2048]{1,0:T(8,128)(2,1)S(1)}, bf16[32,2048]{1,0:T(8,128)(2,1)S(1)}, u32[]{:S(2)}, u32[]{:S(2)}) collective-permute-start(bf16[32,2048]{1,0:T(8,128)(2,1)S(1)} %get-tuple-element.84.p_own), channel_id=1, source_target_pairs={{0,1},{1,2},{2,3},{3,0},{4,5},{5,6},{6,7},{7,4},{8,9},{9,10},{10,1... | collective-permute-start | bytes 393224 | tf_op jit(solution)/shard_map/ppermute | solution.py:25
  64.8 8.6 %collective-permute-start.22 = (bf16[32,2048]{1,0:T(8,128)(2,1)S(1)}, bf16[32,2048]{1,0:T(8,128)(2,1)S(1)}, u32[]{:S(2)}, u32[]{:S(2)}) collective-permute-start(bf16[32,2048]{1,0:T(8,128)(2,1)S(1)} %get-tuple-element.84.p_own), channel_id=1, source_target_pairs={{0,2},{1,3},{2,0},{3,1},{4,6},{5,7},{6,4},{7,5},{8,10},{9,11},{10,... | collective-permute-start | bytes 393224 | tf_op jit(solution)/shard_map/ppermute | solution.py:25
  70.1 5.0 %collective-permute-start.23 = (bf16[32,2048]{1,0:T(8,128)(2,1)S(1)}, bf16[32,2048]{1,0:T(8,128)(2,1)S(1)}, u32[]{:S(2)}, u32[]{:S(2)}) collective-permute-start(bf16[32,2048]{1,0:T(8,128)(2,1)S(1)} %get-tuple-element.84.p_own), channel_id=1, source_target_pairs={{0,3},{1,0},{2,1},{3,2},{4,7},{5,4},{6,5},{7,6},{8,11},{9,8},{10,9... | collective-permute-start | bytes 393224 | tf_op jit(solution)/shard_map/ppermute | solution.py:25
  77.7 5.9 %collective-permute-start.24 = (bf16[32,512]{1,0:T(8,128)(2,1)S(1)}, bf16[32,512]{1,0:T(8,128)(2,1)S(1)}, u32[]{:S(2)}, u32[]{:S(2)}) collective-permute-start(bf16[32,512]{1,0:T(8,128)(2,1)S(1)} %get-tuple-element.91), channel_id=1, source_target_pairs={{0,1},{1,2},{2,3},{3,0},{4,5},{5,6},{6,7},{7,4},{8,9},{9,10},{10,1... | collective-permute-start | bytes 98312 | tf_op jit(solution)/shard_map/ppermute | solution.py:25
  78.1 5.5 %collective-permute-start.25 = (bf16[32,512]{1,0:T(8,128)(2,1)S(1)}, bf16[32,512]{1,0:T(8,128)(2,1)S(1)}, u32[]{:S(2)}, u32[]{:S(2)}) collective-permute-start(bf16[32,512]{1,0:T(8,128)(2,1)S(1)} %get-tuple-element.92), channel_id=1, source_target_pairs={{0,2},{1,3},{2,0},{3,1},{4,6},{5,7},{6,4},{7,5},{8,10},{9,11},{10,... | collective-permute-start | bytes 98312 | tf_op jit(solution)/shard_map/ppermute | solution.py:25
  81.2 3.9 %collective-permute-start.26 = (bf16[32,512]{1,0:T(8,128)(2,1)S(1)}, bf16[32,512]{1,0:T(8,128)(2,1)S(1)}, u32[]{:S(2)}, u32[]{:S(2)}) collective-permute-start(bf16[32,512]{1,0:T(8,128)(2,1)S(1)} %get-tuple-element.93), channel_id=1, source_target_pairs={{0,3},{1,0},{2,1},{3,2},{4,7},{5,4},{6,5},{7,6},{8,11},{9,8},{10,9... | collective-permute-start | bytes 98312 | tf_op jit(solution)/shard_map/ppermute | solution.py:25

commit v6 on v5

--- a/solution.py
+++ b/solution.py
@@ -163,12 +163,11 @@
             target[rows, :] = value()
 
 
-def load_row(plan, stage, index, count, target, plus, minus, stay):
+def arrived_row(plan, stage, index, count, plus, minus, stay):
     digit = plan[DIGIT + stage * count + index]
     seat = seat_rows(plan, stage, index, count)
-    rows = home_rows(index)
     came = jnp.where(digit == 1, plus[seat, :], minus[seat, :])
-    target[rows, :] = jnp.where(digit == 0, stay[rows, :], came)
+    return jnp.where(digit == 0, stay[home_rows(index), :], came)
 
 
 def pack_kernel(
@@ -268,15 +267,13 @@
     if stage + 1 == STAGES:
         (moved,) = refs
         for index in range(count):
-            load_row(plan, stage, index, count, moved, plus, minus, stay)
+            moved[home_rows(index), :] = arrived_row(plan, stage, index, count, plus, minus, stay)
         moved[pl.ds(home, aux), :] = picked
         return
-    next_plus, next_minus, next_stay, hold = refs
+    next_plus, next_minus, next_stay = refs
     for index in range(count):
-        load_row(plan, stage, index, count, hold, plus, minus, stay)
-    for index in range(count):
-        rows = home_rows(index)
-        store_row(plan, stage + 1, index, count, lambda: hold[rows, :], next_plus, next_minus, next_stay)
+        value = arrived_row(plan, stage, index, count, plus, minus, stay)
+        store_row(plan, stage + 1, index, count, lambda: value, next_plus, next_minus, next_stay)
     next_plus[pl.ds(seated, aux), :] = picked
     next_minus[pl.ds(seated, aux), :] = picked
     next_stay[pl.ds(home, aux), :] = picked
@@ -638,7 +635,6 @@
             "merge",
             shape(home) if last else (shape(seated), shape(seated), shape(home)),
             [(plan, "smem")] + [(value, "vmem") for value in arrived],
-            [] if last else [pltpu.VMEM((home, channels), BF16)],
         )
         if not last:
             arrived = (*send(stage + 1, *merged[:2]), merged[2])

time: 86.3 us -> 86.2 us (level)
  no operation moved by 1% of the time
where the time goes in v6:
time: 86.2 us; the launch traced here: 85.8 us
  starting transfers between devices  34.9 us (40%)
  waiting for transfers between devices  28.2 us (33%)
  Pallas kernels  18.7 us (22%)
  local copies, waits for them, and re-layouts  1.82 us (2%)
  between operations  1.42 us (2%)
    ppermute x19, starting transfers between devices, rotate(): return lax.ppermute(value, axis, pairs)  34.9 us
    ppermute x19, waiting for transfers between devices, rotate(): return lax.ppermute(value, axis, pairs)  28.2 us
    pallas_call x9, Pallas kernels, call(): pl.pallas_call(kernel, name=name, out_shape=out_shape, in_specs=[SPECS[pl...  18.7 us
  transfers between devices with their start and end apart: 19, of which 10 were waited for; matrix products, arithmetic and copies ran while one was open for 2% of the time, Pallas kernels for 8%

profile of v6, /device:TPU:2, one launch (start us, length us, event | category | flops | bytes accessed | tf_op | source)
XLA Modules:
  0.0 85.8 jit_solution(7016536937462420690)
XLA Ops:
  0.6 3.9 %pack.1 = (bf16[112,512]{1,0:T(8,128)(2,1)S(1)}, bf16[320,256]{1,0:T(8,128)(2,1)S(1)}, bf16[320,256]{1,0:T(8,128)(2,1)S(1)}, bf16[512,256]{1,0:T(8,128)(2,1)S(1)...) custom-call(s32[8]{0:T(128)} %former.1, s32[8]{0:T(128)} %marks.1, ...), custom_call_target="tpu_custom_call" | custom-call | tf_op jit(solution)/shard_map/pack/pallas_call | solution.py:41
  4.6 2.3 %collective-permute-start.10 = (bf16[112,512]{1,0:T(8,128)(2,1)S(1)}, bf16[112,512]{1,0:T(8,128)(2,1)S(1)}, u32[]{:S(2)}, u32[]{:S(2)}) collective-permute-start(bf16[112,512]{1,0:T(8,128)(2,1)S(1)} %get-tuple-element.59.own), channel_id=1, source_target_pairs={{0,3},{1,0},{2,1},{3,2},{4,7},{5,4},{6,5},{7,6},{8,11},{9,8},{10,9... | collective-permute-start | bytes 344072 | tf_op jit(solution)/shard_map/ppermute | solution.py:25
  6.9 0.0 collective-permute-start.8
  6.9 3.1 %collective-permute-start.9 = (bf16[112,512]{1,0:T(8,128)(2,1)S(1)}, bf16[112,512]{1,0:T(8,128)(2,1)S(1)}, u32[]{:S(2)}, u32[]{:S(2)}) collective-permute-start(bf16[112,512]{1,0:T(8,128)(2,1)S(1)} %get-tuple-element.59.own), channel_id=1, source_target_pairs={{0,2},{1,3},{2,0},{3,1},{4,6},{5,7},{6,4},{7,5},{8,10},{9,11},{10,... | collective-permute-start | bytes 344072 | tf_op jit(solution)/shard_map/ppermute | solution.py:25
  10.0 6.7 %collective-permute-start.11 = (bf16[320,256]{1,0:T(8,128)(2,1)S(1)}, bf16[320,256]{1,0:T(8,128)(2,1)S(1)}, u32[]{:S(2)}, u32[]{:S(2)}) collective-permute-start(bf16[320,256]{1,0:T(8,128)(2,1)S(1)} %get-tuple-element.60), channel_id=1, source_target_pairs={{0,160},{4,164},{8,168},{12,172},{16,176},{20,180},{24,184},{28,18... | collective-permute-start | bytes 491528 | tf_op jit(solution)/shard_map/ppermute | solution.py:25
  16.7 0.0 collective-permute-start.12
  16.7 0.0 collective-permute-done.10.by_three
  16.7 0.0 collective-permute-done.8.by_one
  16.8 0.0 collective-permute-done.9.by_two
  16.8 3.6 %project.1 = (f32[32,256]{1,0:T(8,128)S(1)}, f32[32,256]{1,0:T(8,128)S(1)}, f32[32,256]{1,0:T(8,128)S(1)}, f32[32,64]{1,0:T(8,128)S(1)}, f32[2,64,256]{2,1,0:T(8...) custom-call(s32[88]{0:T(128)S(1)} %get-tuple-element.58.plan, ...), custom_call_target="tpu_custom_call" | custom-call | flops 20000000000 | bytes 8000000 | tf_op jit(solution)/shard_map/project/pallas_call | solution.py:41
  20.4 5.1 %collective-permute-start.13 = (bf16[56,256]{1,0:T(8,128)(2,1)S(1)}, bf16[56,256]{1,0:T(8,128)(2,1)S(1)}, u32[]{:S(2)}, u32[]{:S(2)}) collective-permute-start(bf16[56,256]{1,0:T(8,128)(2,1)S(1)} %get-tuple-element.67.refs_5_), channel_id=1, source_target_pairs={{0,160},{4,164},{8,168},{12,172},{16,176},{20,180},{24,184},{28,18... | collective-permute-start | bytes 86024 | tf_op jit(solution)/shard_map/ppermute | solution.py:25
  25.5 0.0 collective-permute-start.14
  25.5 2.7 %collective-permute-done.13.refs_3_ = bf16[56,256]{1,0:T(8,128)(2,1)S(1)} collective-permute-done((bf16[56,256]{1,0:T(8,128)(2,1)S(1)}, bf16[56,256]{1,0:T(8,128)(2,1)S(1)}, u32[]{:S(2)}, u32[]{:S(2)}) %collective-permute-start.13) | collective-permute-done | bytes 28704 | tf_op jit(solution)/shard_map/ppermute | solution.py:25
  28.3 4.1 %collective-permute-done.14.refs_4_ = bf16[56,256]{1,0:T(8,128)(2,1)S(1)} collective-permute-done((bf16[56,256]{1,0:T(8,128)(2,1)S(1)}, bf16[56,256]{1,0:T(8,128)(2,1)S(1)}, u32[]{:S(2)}, u32[]{:S(2)}) %collective-permute-start.14) | collective-permute-done | bytes 28704 | tf_op jit(solution)/shard_map/ppermute | solution.py:25
  32.4 0.0 collective-permute-done.11.refs_0_
  32.4 0.0 collective-permute-done.12.refs_1_
  32.4 0.7 merge.4
  33.1 0.1 collective-permute-start.15
  33.2 1.7 %collective-permute-start.16 = (bf16[376,256]{1,0:T(8,128)(2,1)S(1)}, bf16[376,256]{1,0:T(8,128)(2,1)S(1)}, u32[]{:S(2)}, u32[]{:S(2)}) collective-permute-start(bf16[376,256]{1,0:T(8,128)(2,1)S(1)} %get-tuple-element.69), channel_id=1, source_target_pairs={{0,12},{4,16},{8,20},{12,24},{16,28},{20,32},{24,36},{28,40},{32,4... | collective-permute-start | bytes 577544 | tf_op jit(solution)/shard_map/ppermute | solution.py:25
  34.9 3.3 %collective-permute-done.15.refs_0_ = bf16[376,256]{1,0:T(8,128)(2,1)S(1)} collective-permute-done((bf16[376,256]{1,0:T(8,128)(2,1)S(1)}, bf16[376,256]{1,0:T(8,128)(2,1)S(1)}, u32[]{:S(2)}, u32[]{:S(2)}) %collective-permute-start.15) | collective-permute-done | bytes 192544 | tf_op jit(solution)/shard_map/ppermute | solution.py:25
  38.3 3.8 %collective-permute-done.16.refs_1_ = bf16[376,256]{1,0:T(8,128)(2,1)S(1)} collective-permute-done((bf16[376,256]{1,0:T(8,128)(2,1)S(1)}, bf16[376,256]{1,0:T(8,128)(2,1)S(1)}, u32[]{:S(2)}, u32[]{:S(2)}) %collective-permute-start.16) | collective-permute-done | bytes 192544 | tf_op jit(solution)/shard_map/ppermute | solution.py:25
  42.1 0.7 merge.5
  42.8 1.1 %collective-permute-start.17 = (bf16[376,256]{1,0:T(8,128)(2,1)S(1)}, bf16[376,256]{1,0:T(8,128)(2,1)S(1)}, u32[]{:S(2)}, u32[]{:S(2)}) collective-permute-start(bf16[376,256]{1,0:T(8,128)(2,1)S(1)} %get-tuple-element.71), channel_id=1, source_target_pairs={{0,224},{4,228},{8,232},{12,236},{16,240},{20,244},{24,248},{28,25... | collective-permute-start | bytes 577544 | tf_op jit(solution)/shard_map/ppermute | solution.py:25
  43.9 2.3 %collective-permute-start.18 = (bf16[376,256]{1,0:T(8,128)(2,1)S(1)}, bf16[376,256]{1,0:T(8,128)(2,1)S(1)}, u32[]{:S(2)}, u32[]{:S(2)}) collective-permute-start(bf16[376,256]{1,0:T(8,128)(2,1)S(1)} %get-tuple-element.72), channel_id=1, source_target_pairs={{0,32},{4,36},{8,40},{12,44},{16,48},{20,52},{24,56},{28,60},{32,6... | collective-permute-start | bytes 577544 | tf_op jit(solution)/shard_map/ppermute | solution.py:25
  46.2 4.3 %collective-permute-done.17.refs_0_ = bf16[376,256]{1,0:T(8,128)(2,1)S(1)} collective-permute-done((bf16[376,256]{1,0:T(8,128)(2,1)S(1)}, bf16[376,256]{1,0:T(8,128)(2,1)S(1)}, u32[]{:S(2)}, u32[]{:S(2)}) %collective-permute-start.17) | collective-permute-done | bytes 192544 | tf_op jit(solution)/shard_map/ppermute | solution.py:25
  50.4 0.7 collective-permute-done.18.refs_1_
  51.1 0.7 merge.6
  51.9 0.6 collective-permute-start.19
  52.5 1.2 %collective-permute-start.20 = (bf16[376,256]{1,0:T(8,128)(2,1)S(1)}, bf16[376,256]{1,0:T(8,128)(2,1)S(1)}, u32[]{:S(2)}, u32[]{:S(2)}) collective-permute-start(bf16[376,256]{1,0:T(8,128)(2,1)S(1)} %get-tuple-element.75), channel_id=1, source_target_pairs={{0,4},{4,8},{8,12},{12,16},{16,20},{20,24},{24,28},{28,32},{32,36}... | collective-permute-start | bytes 577544 | tf_op jit(solution)/shard_map/ppermute | solution.py:25
  53.6 0.6 slice.3
  54.9 0.7 collective-permute-done.19.refs_0_
  55.6 5.2 %collective-permute-done.20.refs_1_ = bf16[376,256]{1,0:T(8,128)(2,1)S(1)} collective-permute-done((bf16[376,256]{1,0:T(8,128)(2,1)S(1)}, bf16[376,256]{1,0:T(8,128)(2,1)S(1)}, u32[]{:S(2)}, u32[]{:S(2)}) %collective-permute-start.20) | collective-permute-done | bytes 192544 | tf_op jit(solution)/shard_map/ppermute | solution.py:25
  60.8 0.0 copy-start.3
  60.8 0.6 merge.7
  61.4 0.0 copy-start.13
  61.5 0.6 copy-done.3
  62.1 2.7 %recur.1 = (f32[8,4,64,64]{3,2,1,0:T(8,128)}, bf16[32,2048]{1,0:T(8,128)(2,1)S(1)}, f32[8,896]{1,0:T(8,128)S(1)}) custom-call(s32[88]{0:T(128)S(1)} %get-tuple-element.58.plan, bf16[568,256]{1,0:T(8,128)(2,1)S(1)} %get-tuple-element.100.moved, f32[3,8,256]{2,1,0:T(8,128)S(1)} %get-tuple-element.77.hist_first, f32[8,64]{1,0:T(8,128)S(1)} %get-tuple-element.78.hist_low, ...), custom_call_target="tpu_custom_call" | custom-call | tf_op jit(solution)/shard_map/recur/pallas_call | solution.py:41
  64.7 0.0 collective-permute-start.21
  64.7 5.4 %collective-permute-start.22 = (bf16[32,2048]{1,0:T(8,128)(2,1)S(1)}, bf16[32,2048]{1,0:T(8,128)(2,1)S(1)}, u32[]{:S(2)}, u32[]{:S(2)}) collective-permute-start(bf16[32,2048]{1,0:T(8,128)(2,1)S(1)} %get-tuple-element.84.p_own), channel_id=1, source_target_pairs={{0,2},{1,3},{2,0},{3,1},{4,6},{5,7},{6,4},{7,5},{8,10},{9,11},{10,... | collective-permute-start | bytes 393224 | tf_op jit(solution)/shard_map/ppermute | solution.py:25
  70.1 0.0 collective-permute-start.23
  70.1 0.0 copy-done.13
  70.1 0.1 iota_compare_fusion
  70.2 3.2 %fetch.1 = (bf16[2048,896]{1,0:T(8,128)(2,1)S(1)}, bf16[896,2048]{1,0:T(8,128)(2,1)S(1)}) custom-call(bf16[2048,896]{1,0:T(8,128)(2,1)} %refs_0_, bf16[896,2048]{1,0:T(8,128)(2,1)} %refs_1_), custom_call_target="tpu_custom_call" | custom-call | tf_op jit(solution)/shard_map/fetch/pallas_call | solution.py:41
  73.3 0.0 collective-permute-done.21.p_one
  73.4 0.0 collective-permute-done.22.p_two
  73.4 1.7 %collective-permute-done.23.p_three = bf16[32,2048]{1,0:T(8,128)(2,1)S(1)} collective-permute-done((bf16[32,2048]{1,0:T(8,128)(2,1)S(1)}, bf16[32,2048]{1,0:T(8,128)(2,1)S(1)}, u32[]{:S(2)}, u32[]{:S(2)}) %collective-permute-start.23) | collective-permute-done | bytes 131104 | tf_op jit(solution)/shard_map/ppermute | solution.py:25
  75.1 2.6 %ffn.1 = (f32[32,512]{1,0:T(8,128)S(1)}, bf16[32,512]{1,0:T(8,128)(2,1)S(1)}, bf16[32,512]{1,0:T(8,128)(2,1)S(1)}, bf16[32,512]{1,0:T(8,128)(2,1)S(1)}, f32[8,512]{1,0:T(8,128)S(1)}) custom-call(s32[88]{0:T(128)S(1)} %get-tuple-element.58.plan, bf16[112,512]{1,0:T(8,128)(2,1)S(1)} %get-tuple-element.59.own, ...), custom_call_target="tpu_custom_call" | custom-call | tf_op jit(solution)/shard_map/ffn/pallas_call | solution.py:41
  77.7 0.4 collective-permute-start.24
  78.0 3.2 %collective-permute-start.25 = (bf16[32,512]{1,0:T(8,128)(2,1)S(1)}, bf16[32,512]{1,0:T(8,128)(2,1)S(1)}, u32[]{:S(2)}, u32[]{:S(2)}) collective-permute-start(bf16[32,512]{1,0:T(8,128)(2,1)S(1)} %get-tuple-element.92), channel_id=1, source_target_pairs={{0,2},{1,3},{2,0},{3,1},{4,6},{5,7},{6,4},{7,5},{8,10},{9,11},{10,... | collective-permute-start | bytes 98312 | tf_op jit(solution)/shard_map/ppermute | solution.py:25
  81.2 1.7 %collective-permute-start.26 = (bf16[32,512]{1,0:T(8,128)(2,1)S(1)}, bf16[32,512]{1,0:T(8,128)(2,1)S(1)}, u32[]{:S(2)}, u32[]{:S(2)}) collective-permute-start(bf16[32,512]{1,0:T(8,128)(2,1)S(1)} %get-tuple-element.93), channel_id=1, source_target_pairs={{0,3},{1,0},{2,1},{3,2},{4,7},{5,4},{6,5},{7,6},{8,11},{9,8},{10,9... | collective-permute-start | bytes 98312 | tf_op jit(solution)/shard_map/ppermute | solution.py:25
  82.9 0.6 copy.25
  83.6 0.0 collective-permute-done.24
  83.6 0.0 collective-permute-done.25
  83.6 1.5 %collective-permute-done.26 = bf16[32,512]{1,0:T(8,128)(2,1)S(1)} collective-permute-done((bf16[32,512]{1,0:T(8,128)(2,1)S(1)}, bf16[32,512]{1,0:T(8,128)(2,1)S(1)}, u32[]{:S(2)}, u32[]{:S(2)}) %collective-permute-start.26) | collective-permute-done | bytes 32800 | tf_op jit(solution)/shard_map/ppermute | solution.py:25
  85.1 0.7 bitcast_select_fusion
  (3 shorter events, 0.0 us)
Async XLA Ops:
  4.6 12.2 %collective-permute-start.10 = (bf16[112,512]{1,0:T(8,128)(2,1)S(1)}, bf16[112,512]{1,0:T(8,128)(2,1)S(1)}, u32[]{:S(2)}, u32[]{:S(2)}) collective-permute-start(bf16[112,512]{1,0:T(8,128)(2,1)S(1)} %get-tuple-element.59.own), channel_id=1, source_target_pairs={{0,3},{1,0},{2,1},{3,2},{4,7},{5,4},{6,5},{7,6},{8,11},{9,8},{10,9... | collective-permute-start | bytes 344072 | tf_op jit(solution)/shard_map/ppermute | solution.py:25
  6.9 9.8 %collective-permute-start.8 = (bf16[112,512]{1,0:T(8,128)(2,1)S(1)}, bf16[112,512]{1,0:T(8,128)(2,1)S(1)}, u32[]{:S(2)}, u32[]{:S(2)}) collective-permute-start(bf16[112,512]{1,0:T(8,128)(2,1)S(1)} %get-tuple-element.59.own), channel_id=1, source_target_pairs={{0,1},{1,2},{2,3},{3,0},{4,5},{5,6},{6,7},{7,4},{8,9},{9,10},{10,1... | collective-permute-start | bytes 344072 | tf_op jit(solution)/shard_map/ppermute | solution.py:25
  6.9 9.8 %collective-permute-start.9 = (bf16[112,512]{1,0:T(8,128)(2,1)S(1)}, bf16[112,512]{1,0:T(8,128)(2,1)S(1)}, u32[]{:S(2)}, u32[]{:S(2)}) collective-permute-start(bf16[112,512]{1,0:T(8,128)(2,1)S(1)} %get-tuple-element.59.own), channel_id=1, source_target_pairs={{0,2},{1,3},{2,0},{3,1},{4,6},{5,7},{6,4},{7,5},{8,10},{9,11},{10,... | collective-permute-start | bytes 344072 | tf_op jit(solution)/shard_map/ppermute | solution.py:25
  10.0 22.4 %collective-permute-start.11 = (bf16[320,256]{1,0:T(8,128)(2,1)S(1)}, bf16[320,256]{1,0:T(8,128)(2,1)S(1)}, u32[]{:S(2)}, u32[]{:S(2)}) collective-permute-start(bf16[320,256]{1,0:T(8,128)(2,1)S(1)} %get-tuple-element.60), channel_id=1, source_target_pairs={{0,160},{4,164},{8,168},{12,172},{16,176},{20,180},{24,184},{28,18... | collective-permute-start | bytes 491528 | tf_op jit(solution)/shard_map/ppermute | solution.py:25
  16.7 15.7 %collective-permute-start.12 = (bf16[320,256]{1,0:T(8,128)(2,1)S(1)}, bf16[320,256]{1,0:T(8,128)(2,1)S(1)}, u32[]{:S(2)}, u32[]{:S(2)}) collective-permute-start(bf16[320,256]{1,0:T(8,128)(2,1)S(1)} %get-tuple-element.61), channel_id=1, source_target_pairs={{0,96},{4,100},{8,104},{12,108},{16,112},{20,116},{24,120},{28,124... | collective-permute-start | bytes 491528 | tf_op jit(solution)/shard_map/ppermute | solution.py:25
  20.4 7.8 %collective-permute-start.13 = (bf16[56,256]{1,0:T(8,128)(2,1)S(1)}, bf16[56,256]{1,0:T(8,128)(2,1)S(1)}, u32[]{:S(2)}, u32[]{:S(2)}) collective-permute-start(bf16[56,256]{1,0:T(8,128)(2,1)S(1)} %get-tuple-element.67.refs_5_), channel_id=1, source_target_pairs={{0,160},{4,164},{8,168},{12,172},{16,176},{20,180},{24,184},{28,18... | collective-permute-start | bytes 86024 | tf_op jit(solution)/shard_map/ppermute | solution.py:25
  25.5 6.9 %collective-permute-start.14 = (bf16[56,256]{1,0:T(8,128)(2,1)S(1)}, bf16[56,256]{1,0:T(8,128)(2,1)S(1)}, u32[]{:S(2)}, u32[]{:S(2)}) collective-permute-start(bf16[56,256]{1,0:T(8,128)(2,1)S(1)} %get-tuple-element.67.refs_5_), channel_id=1, source_target_pairs={{0,96},{4,100},{8,104},{12,108},{16,112},{20,116},{24,120},{28,124... | collective-permute-start | bytes 86024 | tf_op jit(solution)/shard_map/ppermute | solution.py:25
  33.1 5.1 %collective-permute-start.15 = (bf16[376,256]{1,0:T(8,128)(2,1)S(1)}, bf16[376,256]{1,0:T(8,128)(2,1)S(1)}, u32[]{:S(2)}, u32[]{:S(2)}) collective-permute-start(bf16[376,256]{1,0:T(8,128)(2,1)S(1)} %get-tuple-element.68), channel_id=1, source_target_pairs={{0,244},{4,248},{8,252},{12,0},{16,4},{20,8},{24,12},{28,16},{32,2... | collective-permute-start | bytes 577544 | tf_op jit(solution)/shard_map/ppermute | solution.py:25
  33.2 8.8 %collective-permute-start.16 = (bf16[376,256]{1,0:T(8,128)(2,1)S(1)}, bf16[376,256]{1,0:T(8,128)(2,1)S(1)}, u32[]{:S(2)}, u32[]{:S(2)}) collective-permute-start(bf16[376,256]{1,0:T(8,128)(2,1)S(1)} %get-tuple-element.69), channel_id=1, source_target_pairs={{0,12},{4,16},{8,20},{12,24},{16,28},{20,32},{24,36},{28,40},{32,4... | collective-permute-start | bytes 577544 | tf_op jit(solution)/shard_map/ppermute | solution.py:25
  42.8 7.7 %collective-permute-start.17 = (bf16[376,256]{1,0:T(8,128)(2,1)S(1)}, bf16[376,256]{1,0:T(8,128)(2,1)S(1)}, u32[]{:S(2)}, u32[]{:S(2)}) collective-permute-start(bf16[376,256]{1,0:T(8,128)(2,1)S(1)} %get-tuple-element.71), channel_id=1, source_target_pairs={{0,224},{4,228},{8,232},{12,236},{16,240},{20,244},{24,248},{28,25... | collective-permute-start | bytes 577544 | tf_op jit(solution)/shard_map/ppermute | solution.py:25
  43.9 7.3 %collective-permute-start.18 = (bf16[376,256]{1,0:T(8,128)(2,1)S(1)}, bf16[376,256]{1,0:T(8,128)(2,1)S(1)}, u32[]{:S(2)}, u32[]{:S(2)}) collective-permute-start(bf16[376,256]{1,0:T(8,128)(2,1)S(1)} %get-tuple-element.72), channel_id=1, source_target_pairs={{0,32},{4,36},{8,40},{12,44},{16,48},{20,52},{24,56},{28,60},{32,6... | collective-permute-start | bytes 577544 | tf_op jit(solution)/shard_map/ppermute | solution.py:25
  51.9 3.7 %collective-permute-start.19 = (bf16[376,256]{1,0:T(8,128)(2,1)S(1)}, bf16[376,256]{1,0:T(8,128)(2,1)S(1)}, u32[]{:S(2)}, u32[]{:S(2)}) collective-permute-start(bf16[376,256]{1,0:T(8,128)(2,1)S(1)} %get-tuple-element.74), channel_id=1, source_target_pairs={{0,252},{4,0},{8,4},{12,8},{16,12},{20,16},{24,20},{28,24},{32,28}... | collective-permute-start | bytes 577544 | tf_op jit(solution)/shard_map/ppermute | solution.py:25
  52.5 8.4 %collective-permute-start.20 = (bf16[376,256]{1,0:T(8,128)(2,1)S(1)}, bf16[376,256]{1,0:T(8,128)(2,1)S(1)}, u32[]{:S(2)}, u32[]{:S(2)}) collective-permute-start(bf16[376,256]{1,0:T(8,128)(2,1)S(1)} %get-tuple-element.75), channel_id=1, source_target_pairs={{0,4},{4,8},{8,12},{12,16},{16,20},{20,24},{24,28},{28,32},{32,36}... | collective-permute-start | bytes 577544 | tf_op jit(solution)/shard_map/ppermute | solution.py:25
  60.8 1.2 %copy-start.3 = (bf16[256,2048]{1,0:T(8,128)(2,1)S(1)}, bf16[256,2048]{1,0:T(8,128)(2,1)}, u32[]{:S(2)}) copy-start(bf16[256,2048]{1,0:T(8,128)(2,1)} %w_out.1) | copy-start | bytes 3145732
  61.4 8.7 %copy-start.13 = (s32[8]{0:T(128)S(1)}, s32[8]{0:T(128)}, u32[]{:S(2)}) copy-start(s32[8]{0:T(128)} %occupied.1) | copy-start | bytes 100
  64.7 8.6 %collective-permute-start.21 = (bf16[32,2048]{1,0:T(8,128)(2,1)S(1)}, bf16[32,2048]{1,0:T(8,128)(2,1)S(1)}, u32[]{:S(2)}, u32[]{:S(2)}) collective-permute-start(bf16[32,2048]{1,0:T(8,128)(2,1)S(1)} %get-tuple-element.84.p_own), channel_id=1, source_target_pairs={{0,1},{1,2},{2,3},{3,0},{4,5},{5,6},{6,7},{7,4},{8,9},{9,10},{10,1... | collective-permute-start | bytes 393224 | tf_op jit(solution)/shard_map/ppermute | solution.py:25
  64.7 8.6 %collective-permute-start.22 = (bf16[32,2048]{1,0:T(8,128)(2,1)S(1)}, bf16[32,2048]{1,0:T(8,128)(2,1)S(1)}, u32[]{:S(2)}, u32[]{:S(2)}) collective-permute-start(bf16[32,2048]{1,0:T(8,128)(2,1)S(1)} %get-tuple-element.84.p_own), channel_id=1, source_target_pairs={{0,2},{1,3},{2,0},{3,1},{4,6},{5,7},{6,4},{7,5},{8,10},{9,11},{10,... | collective-permute-start | bytes 393224 | tf_op jit(solution)/shard_map/ppermute | solution.py:25
  70.1 5.0 %collective-permute-start.23 = (bf16[32,2048]{1,0:T(8,128)(2,1)S(1)}, bf16[32,2048]{1,0:T(8,128)(2,1)S(1)}, u32[]{:S(2)}, u32[]{:S(2)}) collective-permute-start(bf16[32,2048]{1,0:T(8,128)(2,1)S(1)} %get-tuple-element.84.p_own), channel_id=1, source_target_pairs={{0,3},{1,0},{2,1},{3,2},{4,7},{5,4},{6,5},{7,6},{8,11},{9,8},{10,9... | collective-permute-start | bytes 393224 | tf_op jit(solution)/shard_map/ppermute | solution.py:25
  77.7 5.9 %collective-permute-start.24 = (bf16[32,512]{1,0:T(8,128)(2,1)S(1)}, bf16[32,512]{1,0:T(8,128)(2,1)S(1)}, u32[]{:S(2)}, u32[]{:S(2)}) collective-permute-start(bf16[32,512]{1,0:T(8,128)(2,1)S(1)} %get-tuple-element.91), channel_id=1, source_target_pairs={{0,1},{1,2},{2,3},{3,0},{4,5},{5,6},{6,7},{7,4},{8,9},{9,10},{10,1... | collective-permute-start | bytes 98312 | tf_op jit(solution)/shard_map/ppermute | solution.py:25
  78.0 5.5 %collective-permute-start.25 = (bf16[32,512]{1,0:T(8,128)(2,1)S(1)}, bf16[32,512]{1,0:T(8,128)(2,1)S(1)}, u32[]{:S(2)}, u32[]{:S(2)}) collective-permute-start(bf16[32,512]{1,0:T(8,128)(2,1)S(1)} %get-tuple-element.92), channel_id=1, source_target_pairs={{0,2},{1,3},{2,0},{3,1},{4,6},{5,7},{6,4},{7,5},{8,10},{9,11},{10,... | collective-permute-start | bytes 98312 | tf_op jit(solution)/shard_map/ppermute | solution.py:25
  81.2 3.9 %collective-permute-start.26 = (bf16[32,512]{1,0:T(8,128)(2,1)S(1)}, bf16[32,512]{1,0:T(8,128)(2,1)S(1)}, u32[]{:S(2)}, u32[]{:S(2)}) collective-permute-start(bf16[32,512]{1,0:T(8,128)(2,1)S(1)} %get-tuple-element.93), channel_id=1, source_target_pairs={{0,3},{1,0},{2,1},{3,2},{4,7},{5,4},{6,5},{7,6},{8,11},{9,8},{10,9... | collective-permute-start | bytes 98312 | tf_op jit(solution)/shard_map/ppermute | solution.py:25
